TPU v7x, 512 devices: a whole 4x4x16 slice. The times are simulated.
512 devices in a mesh: tm: 8 (over x, core), tile: 64 (over y, z).
Axes of the slice: x: 4, y: 4, z: 16, core: 2. Of those that a mesh axis runs over, the one named last changes fastest.
Arguments:
- starts: float32 [8, 98304, 128], P('tm', 'tile'), may hold values from -6 to 6
- sources: float32 [98304, 128], P('tile'), may hold values from -6 to 6
- fine_ops: float32 [8, 768, 4, 128, 128], P('tm', 'tile'), may hold values from -0.1875 to 0.1875
- col_index: int32 [8, 768, 4], P('tm', 'tile'), may hold values from 0 to 15, as said below
- live_count: int32 [8, 768], P('tm', 'tile'), may hold values from 1 to 4, as said below
- coarse_op: float32 [24576, 768], P('tile'), may hold values from -0.15625 to 0.15625
- cell_map: int32 [98304], P('tile'), may hold values from 0 to 383, as said below
Outputs:
- corrected: float32 [8, 98304, 128], P('tm', 'tile')
Inputs may be any that keep to these rules, and one draw needn't show every extreme that they name: `col_index`: each entry names one of the 16 blocks of a tile's fine window. Slots from live_count on are padding and carry no transport. `cell_map`: each entry is a local coarse index within its own tile; every coarse cell of every tile has at least one fine cell.
All inputs are finite; a program needn't handle non-finite values.
Results may differ from a plain program's by a relative error of at most 0.0003.
Values sent between devices are 32-bit elements; how exact they have to be, the bound alone decides.
No kernel may reach another device: no remote copies, remote signals or barrier semaphores. Data moves between devices by JAX's collectives and lax.ppermute only.
A program may use at most 64 MiB of HBM per device.

v0:
```python
import jax
import jax.numpy as jnp
from jax import lax
from jax.experimental import pallas as pl
from jax.experimental.pallas import tpu as pltpu
from jax.sharding import PartitionSpec as P


HALO = 256
BS = 128
F32 = jnp.float32
BF16 = jnp.bfloat16
VMEM = pl.BlockSpec(memory_space=pltpu.VMEM)
SMEM = pl.BlockSpec(memory_space=pltpu.SMEM)
HBM = pl.BlockSpec(memory_space=pltpu.HBM)


def call(kernel, outs, in_specs, flops, nbytes, scratch=(), out_spec=VMEM, aliases=None):
    return pl.pallas_call(
        kernel,
        out_shape=[jax.ShapeDtypeStruct(shape, dtype) for shape, dtype in outs],
        in_specs=in_specs,
        out_specs=[out_spec] * len(outs),
        input_output_aliases=aliases or {},
        scratch_shapes=list(scratch),
        cost_estimate=pl.CostEstimate(flops=flops, bytes_accessed=nbytes, transcendentals=0),
        compiler_params=pltpu.CompilerParams(vmem_limit_bytes=16 << 20),
    )


def kept(value):
    return pltpu.with_memory_space_constraint(value, pltpu.HBM)


def halves(value):
    high = value.astype(BF16)
    return high, (value - high.astype(F32)).astype(BF16)


def pair(value):
    return jnp.concatenate(halves(value), axis=1)


def dot(a, b):
    return jnp.dot(a, b, preferred_element_type=F32)


def folded(product):
    width = product.shape[1] // 2
    return product[:, :width] + product[:, width:]


def odd_tile():
    return lax.rem(lax.axis_index("tile"), 2)


def ends(starts_ref, far_ref, near_ref, sems):
    last = starts_ref.shape[0] - HALO
    odd = odd_tile()
    copies = [
        pltpu.make_async_copy(
            starts_ref.at[pl.ds(pl.multiple_of(side * last, BS), HALO), :], out_ref, sems.at[index]
        )
        for index, (side, out_ref) in enumerate(((odd, far_ref), (1 - odd, near_ref)))
    ]
    for copy in copies:
        copy.start()
    for copy in copies:
        copy.wait()


def run_copies(copies):
    for copy in copies:
        copy.start()
    return copies


def fetch(ops_ref, starts_ref, sources_ref, ops_out, own_ref, sources_out, held, sems):
    copies = run_copies([
        pltpu.make_async_copy(starts_ref, held, sems.at[0]),
        pltpu.make_async_copy(ops_ref, ops_out, sems.at[1]),
        pltpu.make_async_copy(sources_ref, sources_out, sems.at[2]),
    ])
    copies[0].wait()
    for b in range(held.shape[0] // BS):
        own_ref[b * BS:(b + 1) * BS, :] = pair(held[b * BS:(b + 1) * BS, :])
    for copy in copies[1:]:
        copy.wait()


def prepare(map_hbm, own_ref, token_ref, gather_ref, inverse_ref, rstart_ref, map_ref, sems):
    copy = pltpu.make_async_copy(map_hbm, map_ref, sems.at[0])
    copy.start()
    copy.wait()
    coarse = gather_ref.shape[0]
    cells = lax.broadcasted_iota(jnp.int32, (coarse, BS), 0)
    children = jnp.zeros((coarse, 1), F32)
    for b in range(map_ref.shape[0]):
        chosen = jnp.where(map_ref[b:b + 1, :] == cells, 1.0, 0.0)
        children = children + jnp.sum(chosen, axis=1, keepdims=True)
        gather_ref[:, b * BS:(b + 1) * BS] = chosen.astype(BF16)
    inverse = jnp.broadcast_to(1.0 / children, inverse_ref.shape)
    inverse_ref[...] = inverse
    rstart_ref[...] = folded(dot(gather_ref[...], own_ref[...])) * inverse


def prepare_late(coarse_hbm, gather_ref, token_ref, spread_ref, coarse2_ref, coarse_ref, sems):
    copy = pltpu.make_async_copy(coarse_hbm, coarse_ref, sems.at[0])
    copy.start()
    for b in range(gather_ref.shape[1] // BS):
        spread_ref[b * BS:(b + 1) * BS, :] = gather_ref[:, b * BS:(b + 1) * BS].astype(F32).T.astype(BF16)
    copy.wait()
    width = coarse_ref.shape[1]
    high, low = halves(coarse_ref[...])
    coarse2_ref[:, :width] = high
    coarse2_ref[:, width:] = low


def transport(cols_hbm, live_hbm, ops_ref, own_ref, far_ref, near_ref, sources_ref,
              cols_ref, live_ref, window, sems, emit):
    copies = run_copies([
        pltpu.make_async_copy(cols_hbm, cols_ref, sems.at[0]),
        pltpu.make_async_copy(live_hbm, live_ref, sems.at[1]),
    ])
    rows = own_ref.shape[0]
    blocks, slots = ops_ref.shape[:2]
    odd = odd_tile()
    window[pl.ds(pl.multiple_of(odd * (HALO + rows), BS), HALO), :] = pair(far_ref[...])
    window[pl.ds(pl.multiple_of((1 - odd) * (HALO + rows), BS), HALO), :] = pair(near_ref[...])
    window[HALO:HALO + rows, :] = own_ref[...]
    for copy in copies:
        copy.wait()
    for b in range(blocks):
        pieces, highs, lows = [], [], []
        for k in range(slots):
            at = pl.multiple_of(cols_ref[k, b] * BS, BS)
            pieces.append(window[pl.ds(at, BS), :])
            high, low = halves(jnp.where(k < live_ref[0, b], ops_ref[b, k], 0.0))
            highs.append(high)
            lows.append(low)
        pieces = jnp.concatenate(pieces, axis=0)
        tracers = pieces.shape[1] // 2
        value = folded(dot(jnp.concatenate(highs, axis=1), pieces))
        value = value + dot(jnp.concatenate(lows, axis=1), pieces[:, :tracers])
        emit(b, value + sources_ref[b * BS:(b + 1) * BS, :])


def sides(block, far_ref, near_ref, width):
    odd = odd_tile()
    last = block.shape[0] - width
    far_ref[...] = block[pl.ds(pl.multiple_of(odd * last, 64), width), :]
    near_ref[...] = block[pl.ds(pl.multiple_of((1 - odd) * last, 64), width), :]


def first_step(cols_hbm, live_hbm, ops_ref, own_ref, far_ref, near_ref, sources_ref,
               next_ref, nfar_ref, nnear_ref, token_ref, cols_ref, live_ref, window, sems, rims):
    blocks = ops_ref.shape[0]
    side = HALO // BS

    def emit(b, value):
        next_ref[b * BS:(b + 1) * BS, :] = pair(value)
        if b < side:
            rims[b * BS:(b + 1) * BS, :] = value
        if b >= blocks - side:
            at = b - blocks + 2 * side
            rims[at * BS:(at + 1) * BS, :] = value

    transport(cols_hbm, live_hbm, ops_ref, own_ref, far_ref, near_ref, sources_ref,
              cols_ref, live_ref, window, sems, emit)
    sides(rims, nfar_ref, nnear_ref, HALO)
    token_ref[...] = jnp.zeros_like(token_ref)


def restricted_step(refs, gather_ref, inverse_ref, end_ref, jump_ref, cols_ref, live_ref, window, sems, split):
    def emit(b, value):
        end_ref[b * BS:(b + 1) * BS, :] = value
        split[b * BS:(b + 1) * BS, :] = pair(value)

    transport(*refs, cols_ref, live_ref, window, sems, emit)
    jump_ref[...] = folded(dot(gather_ref[...], split[...])) * inverse_ref[...]


def second_step_first(*refs):
    operands, (gather_ref, inverse_ref, following_ref) = refs[:7], refs[7:10]
    end_ref, jump_ref, nfar_ref, nnear_ref = refs[10:14]

    @pl.when(lax.axis_index("tm") == 0)
    def _():
        restricted_step(operands, gather_ref, inverse_ref, end_ref, jump_ref, *refs[14:])
        jump_ref[...] = jump_ref[...] - following_ref[...]
        sides(jump_ref, nfar_ref, nnear_ref, nfar_ref.shape[0])


def second_step_rest(*refs):
    operands, (gather_ref, inverse_ref) = refs[:7], refs[7:9]
    end_ref, jump_ref = refs[10:12]
    first = lax.axis_index("tm") == 0

    @pl.when(first)
    def _():
        jump_ref[...] = jnp.zeros_like(jump_ref)

    @pl.when(jnp.logical_not(first))
    def _():
        restricted_step(operands, gather_ref, inverse_ref, end_ref, jump_ref, *refs[12:])


def coarse_product(coarse2_ref, far_ref, own_ref, near_ref, window):
    width = coarse2_ref.shape[1] // 2
    rim, rows = far_ref.shape[0], own_ref.shape[0]
    odd = odd_tile()
    window[pl.ds(pl.multiple_of(odd * (rim + rows), 64), rim), :] = pair(far_ref[...])
    window[pl.ds(pl.multiple_of((1 - odd) * (rim + rows), 64), rim), :] = pair(near_ref[...])
    window[rim:rim + rows, :] = pair(own_ref[...])
    tracers = own_ref.shape[1]
    product = folded(dot(coarse2_ref[:, :width], window[...]))
    return product + dot(coarse2_ref[:, width:], window[:, :tracers])


def advance(coarse2_ref, far_ref, own_ref, near_ref, jump_ref, later_ref, *refs):
    state_ref, nfar_ref, nnear_ref, total_ref, window = refs[-5:]
    image = coarse_product(coarse2_ref, far_ref, own_ref, near_ref, window)
    state_ref[...] = image + (jump_ref[...] - later_ref[...])
    sides(state_ref, nfar_ref, nnear_ref, nfar_ref.shape[0])
    total_ref[...] = image if len(refs) == 5 else refs[0][...] + image


def finish(coarse2_ref, far_ref, own_ref, near_ref, image_ref, spread_ref, end_ref, out_hbm, window, held, sems):
    image = image_ref[...] + coarse_product(coarse2_ref, far_ref, own_ref, near_ref, window)
    split = pair(image)
    copies = []
    for b in range(sems.shape[0]):
        part = end_ref.shape[0] // sems.shape[0]
        rows = slice(b * part, (b + 1) * part)
        held[rows, :] = end_ref[rows, :] + folded(dot(spread_ref[rows, :], split))
        copies.append(pltpu.make_async_copy(held.at[rows, :], out_hbm.at[rows, :], sems.at[b]))
        copies[-1].start()
    for copy in copies:
        copy.wait()


def swapped(far, near):
    count = lax.axis_size("tile")
    far = lax.ppermute(far, "tile", [(i, (i + 1 if i % 2 else i - 1) % count) for i in range(count)])
    near = lax.ppermute(near, "tile", [(i, i ^ 1) for i in range(count)])
    return far, near


def on_device(starts, sources, fine_ops, col_index, live_count, coarse_op, cell_map):
    first_state = starts[0]
    ops = fine_ops[0]
    rows, tracers = first_state.shape
    blocks, slots = ops.shape[:2]
    columns = col_index[0].T
    live = live_count
    coarse, reach = coarse_op.shape
    rim = (reach - coarse) // 2
    slices = lax.axis_size("tm")
    tiles = lax.axis_size("tile")
    window = pltpu.VMEM((rows + 2 * HALO, 2 * tracers), BF16)
    step_flops = 6 * rows * slots * BS * tracers
    coarse_flops = 6 * coarse * reach * tracers
    side = ((HALO, tracers), F32)
    coarse_rim = ((rim, tracers), F32)
    coarse_all = ((coarse, tracers), F32)

    far, near = call(ends, [side, side], [HBM], 0, 500_000, [pltpu.SemaphoreType.DMA((2,))])(kept(first_state))
    far, near = swapped(far, near)
    ops, own, sources = call(
        fetch, [(ops.shape, F32), ((rows, 2 * tracers), BF16), (sources.shape, F32)],
        [HBM] * 3, 0, 9_000_000, [pltpu.VMEM((rows, tracers), F32), pltpu.SemaphoreType.DMA((3,))],
    )(kept(ops), kept(first_state), kept(sources))

    step_in = [HBM] * 2 + [VMEM] * 5
    step_scratch = [pltpu.SMEM(columns.shape, jnp.int32), pltpu.SMEM(live.shape, jnp.int32), window,
                    pltpu.SemaphoreType.DMA((2,))]
    state, far, near, token = call(
        first_step, [((rows, 2 * tracers), BF16), side, side, ((8, tracers), F32)],
        step_in, step_flops, 6_000_000, step_scratch + [pltpu.VMEM((2 * HALO, tracers), F32)],
    )(kept(columns), kept(live), ops, own, far, near, sources)
    far, near = swapped(far, near)
    gather, inverse, rstart = call(
        prepare, [((coarse, rows), BF16), coarse_all, coarse_all],
        [HBM, VMEM, VMEM], 4 * coarse * rows * tracers, 3_000_000,
        [pltpu.VMEM((blocks, BS), jnp.int32), pltpu.SemaphoreType.DMA((1,))],
    )(kept(cell_map.reshape(-1, BS)), own, token)
    following = lax.ppermute(rstart, "tm", [(1, 0)])
    later = lax.ppermute(rstart, "tm", [(i + 1, i) for i in range(1, slices - 1)])
    step_scratch = step_scratch + [pltpu.VMEM((rows, 2 * tracers), BF16)]
    step_args = (kept(columns), kept(live), ops, state, far, near, sources, gather, inverse)
    step_flops = step_flops + 4 * coarse * rows * tracers
    fine_end, jump, far, near = call(
        second_step_first, [((rows, tracers), F32), coarse_all, coarse_rim, coarse_rim],
        step_in + [VMEM] * 3, step_flops, 8_000_000, step_scratch,
    )(*step_args, following)

    def to_slice(block, n, target):
        route = [((n - 1) * tiles + i, n * tiles + target(i) % tiles) for i in range(tiles)]
        return lax.ppermute(block, ("tm", "tile"), route)

    image = ()
    state = jump
    coarse_window = [pltpu.VMEM((reach, 2 * tracers), BF16)]
    for n in range(1, slices):
        far = to_slice(far, n, lambda i: i + 1 if i % 2 else i - 1)
        near = to_slice(near, n, lambda i: i ^ 1)
        own = to_slice(state, n, lambda i: i)
        if n == 1:
            fine_end, jump = call(
                second_step_rest, [((rows, tracers), F32), coarse_all],
                step_in + [VMEM] * 3, step_flops, 8_000_000, step_scratch, aliases={9: 0},
            )(*step_args, fine_end)
            spread, coarse2 = call(
                prepare_late, [((rows, coarse), BF16), ((coarse, 2 * reach), BF16)],
                [HBM] + [VMEM] * 2, 0, 4_000_000,
                [pltpu.VMEM((coarse, reach), F32), pltpu.SemaphoreType.DMA((1,))],
            )(kept(coarse_op), gather, token)
        if n < slices - 1:
            state, far, near, *image = call(
                advance, [coarse_all, coarse_rim, coarse_rim, coarse_all],
                [VMEM] * (6 + len(image)), coarse_flops, 2_000_000, coarse_window,
            )(coarse2, far, own, near, jump, later, *image)
        else:
            (result,) = call(
                finish, [((rows, tracers), F32)], [VMEM] * 7,
                coarse_flops + 4 * coarse * rows * tracers, 4_000_000,
                coarse_window + [pltpu.VMEM((rows, tracers), F32), pltpu.SemaphoreType.DMA((6,))], HBM,
            )(coarse2, far, own, near, *image, spread, fine_end)
    return result[None]


def solution(mesh):
    placed = (
        P("tm", "tile", None),
        P("tile", None),
        P("tm", "tile", None, None, None),
        P("tm", "tile", None),
        P("tm", "tile"),
        P("tile", None),
        P("tile"),
    )

    return jax.shard_map(on_device, mesh=mesh, in_specs=placed, out_specs=P("tm", "tile", None), check_vma=False)
```

profile of v0, /device:TPU:6, one launch (start us, length us, event | category | flops | bytes accessed | tf_op | source)
XLA Modules:
  0.0 98.0 jit_solution(8028931088371019020)
XLA Ops:
  0.0 1.0 %shard_map.74 = (f32[256,128]{1,0:T(8,128)S(1)}, f32[256,128]{1,0:T(8,128)S(1)}) custom-call(f32[1536,128]{1,0:T(8,128)} %bitcast.7), custom_call_target="tpu_custom_call" | custom-call | bytes 500000 | tf_op jit(solution)/shard_map/pallas_call | solution.py:267
  1.0 13.9 %collective-permute-start = (f32[256,128]{1,0:T(8,128)S(1)}, f32[256,128]{1,0:T(8,128)S(1)}, u32[]{:S(2)}, u32[]{:S(2)}) collective-permute-start(f32[256,128]{1,0:T(8,128)S(1)} %get-tuple-element.51), channel_id=1, source_target_pairs={{0,63},{1,2},{2,1},{3,4},{4,3},{5,6},{6,5},{7,8},{8,7},{9,10},{10,... | collective-permute-start | bytes 393224 | tf_op jit(solution)/shard_map/ppermute | solution.py:244
  14.9 1.9 %collective-permute-start.1 = (f32[256,128]{1,0:T(8,128)S(1)}, f32[256,128]{1,0:T(8,128)S(1)}, u32[]{:S(2)}, u32[]{:S(2)}) collective-permute-start(f32[256,128]{1,0:T(8,128)S(1)} %get-tuple-element.52), channel_id=1, source_target_pairs={{0,1},{1,0},{2,3},{3,2},{4,5},{5,4},{6,7},{7,6},{8,9},{9,8},{10,11... | collective-permute-start | bytes 393224 | tf_op jit(solution)/shard_map/ppermute | solution.py:245
  16.8 2.3 %shard_map.73 = (f32[12,4,128,128]{3,2,1,0:T(8,128)S(1)}, bf16[1536,256]{1,0:T(8,128)(2,1)S(1)}, f32[1536,128]{1,0:T(8,128)S(1)}) custom-call(f32[12,4,128,128]{3,2,1,0:T(8,128)} %bitcast.9, f32[1536,128]{1,0:T(8,128)} %bitcast.8, f32[1536,128]{1,0:T(8,128)} %sources_ref.1), custom_call_target="tpu_custom_call" | custom-call | bytes 9000000 | tf_op jit(solution)/shard_map/pallas_call | solution.py:269
  19.1 0.0 collective-permute-done.far_ref
  19.1 2.6 %collective-permute-done.1.near_ref = f32[256,128]{1,0:T(8,128)S(1)} collective-permute-done((f32[256,128]{1,0:T(8,128)S(1)}, f32[256,128]{1,0:T(8,128)S(1)}, u32[]{:S(2)}, u32[]{:S(2)}) %collective-permute-start.1) | collective-permute-done | bytes 131104 | tf_op jit(solution)/shard_map/ppermute | solution.py:245
  21.7 1.7 %shard_map.75 = (bf16[1536,256]{1,0:T(8,128)(2,1)S(1)}, f32[256,128]{1,0:T(8,128)S(1)}, f32[256,128]{1,0:T(8,128)S(1)}, f32[8,128]{1,0:T(8,128)S(1)}) custom-call(s32[4,12]{1,0:T(4,128)} %bitcast.10, s32[1,12]{1,0:T(1,128)} %refs_1_.3, f32[12,4,128,128]{3,2,1,0:T(8,128)S(1)} %get-tuple-element.50.ops_ref.refs_2_, ...), custom_call_target="tpu_custom_call" | custom-call | flops 603979776 | bytes 6000000 | tf_op jit(solution)/shard_map/pallas_call | solution.py:277
  23.5 1.5 %shard_map.76 = (bf16[384,1536]{1,0:T(8,128)(2,1)S(1)}, f32[384,128]{1,0:T(8,128)S(1)}, f32[384,128]{1,0:T(8,128)S(1)}) custom-call(s32[12,128]{1,0:T(8,128)} %bitcast.13, bf16[1536,256]{1,0:T(8,128)(2,1)S(1)} %get-tuple-element.49.own_ref, f32[8,128]{1,0:T(8,128)S(1)} %get-tuple-element.54.token_ref), custom_call_target="tpu_custom_call" | custom-call | flops 301989888 | bytes 3000000 | tf_op jit(solution)/shard_map/pallas_call | solution.py:282
  25.0 0.7 collective-permute-start.4
  25.7 3.6 %collective-permute-start.2 = (f32[256,128]{1,0:T(8,128)S(1)}, f32[256,128]{1,0:T(8,128)S(1)}, u32[]{:S(2)}, u32[]{:S(2)}) collective-permute-start(f32[256,128]{1,0:T(8,128)S(1)} %get-tuple-element.58), channel_id=1, source_target_pairs={{0,63},{1,2},{2,1},{3,4},{4,3},{5,6},{6,5},{7,8},{8,7},{9,10},{10,... | collective-permute-start | bytes 393224 | tf_op jit(solution)/shard_map/ppermute | solution.py:244
  29.3 1.9 %collective-permute-start.3 = (f32[256,128]{1,0:T(8,128)S(1)}, f32[256,128]{1,0:T(8,128)S(1)}, u32[]{:S(2)}, u32[]{:S(2)}) collective-permute-start(f32[256,128]{1,0:T(8,128)S(1)} %get-tuple-element.59), channel_id=1, source_target_pairs={{0,1},{1,0},{2,3},{3,2},{4,5},{5,4},{6,7},{7,6},{8,9},{9,8},{10,11... | collective-permute-start | bytes 393224 | tf_op jit(solution)/shard_map/ppermute | solution.py:245
  31.2 1.9 %collective-permute-start.8 = (f32[384,128]{1,0:T(8,128)S(1)}, f32[384,128]{1,0:T(8,128)S(1)}, u32[]{:S(2)}, u32[]{:S(2)}) collective-permute-start(f32[384,128]{1,0:T(8,128)S(1)} %get-tuple-element.61), channel_id=1, source_target_pairs={{128,64},{192,128},{256,192},{320,256},{384,320},{448,384},{129,65... | collective-permute-start | bytes 589832 | tf_op jit(solution)/shard_map/ppermute | solution.py:288
  33.1 2.7 %collective-permute-done.2.refs_4_ = f32[256,128]{1,0:T(8,128)S(1)} collective-permute-done((f32[256,128]{1,0:T(8,128)S(1)}, f32[256,128]{1,0:T(8,128)S(1)}, u32[]{:S(2)}, u32[]{:S(2)}) %collective-permute-start.2) | collective-permute-done | bytes 131104 | tf_op jit(solution)/shard_map/ppermute | solution.py:244
  35.8 0.3 collective-permute-done.3.refs_5_
  36.1 0.0 collective-permute-done.4.refs_9_
  36.1 0.7 collective-permute-start.6
  36.8 0.7 collective-permute-start.5
  37.5 0.7 collective-permute-start.7
  38.2 1.4 %shard_map.77 = (bf16[1536,384]{1,0:T(8,128)(2,1)S(1)}, bf16[384,1536]{1,0:T(8,128)(2,1)S(1)}) custom-call(f32[384,768]{1,0:T(8,128)} %coarse_hbm.1, bf16[384,1536]{1,0:T(8,128)(2,1)S(1)} %get-tuple-element.55.gather_ref.refs_7_, f32[8,128]{1,0:T(8,128)S(1)} %get-tuple-element.54.token_ref), custom_call_target="tpu_custom_call" | custom-call | bytes 4000000 | tf_op jit(solution)/shard_map/pallas_call | solution.py:313
  39.6 2.0 %shard_map.79 = (f32[1536,128]{1,0:T(8,128)S(1)}, f32[384,128]{1,0:T(8,128)S(1)}) custom-call(s32[4,12]{1,0:T(4,128)} %bitcast.12, s32[1,12]{1,0:T(1,128)} %refs_1_.3, f32[12,4,128,128]{3,2,1,0:T(8,128)S(1)} %get-tuple-element.50.ops_ref.refs_2_, bf16[1536,256]{1,0:T(8,128)(2,1)S(1)} %get-tuple-element.57.refs_3_, ...), custom_call_target="tpu_custom_call", output_to_operand_aliasing={{0}: (9, {})} | custom-call | flops 905969664 | bytes 8000000 | tf_op jit(solution)/shard_map/pallas_call | solution.py:309
  41.7 0.6 shard_map.80
  42.3 0.7 collective-permute-start.10
  42.9 0.7 collective-permute-start.9
  43.6 0.7 collective-permute-start.11
  44.3 0.6 shard_map.81
  44.9 0.7 collective-permute-start.13
  45.6 0.7 collective-permute-start.12
  46.3 0.7 collective-permute-start.14
  47.0 0.6 shard_map.82
  47.5 0.7 collective-permute-start.16
  48.2 0.7 collective-permute-start.15
  48.9 0.7 collective-permute-start.17
  49.6 0.6 shard_map.83
  50.2 0.7 collective-permute-start.19
  50.8 0.7 collective-permute-start.18
  51.5 0.7 collective-permute-start.20
  52.2 0.6 shard_map.84
  52.8 1.3 %collective-permute-start.22 = (f32[384,128]{1,0:T(8,128)S(1)}, f32[384,128]{1,0:T(8,128)S(1)}, u32[]{:S(2)}, u32[]{:S(2)}) collective-permute-start(f32[384,128]{1,0:T(8,128)S(1)} %get-tuple-element.84), channel_id=1, source_target_pairs={{320,384},{321,385},{322,386},{323,387},{324,388},{325,389},{326,3... | collective-permute-start | bytes 589832 | tf_op jit(solution)/shard_map/ppermute | solution.py:299
  54.1 1.3 %collective-permute-start.21 = (f32[192,128]{1,0:T(8,128)S(1)}, f32[192,128]{1,0:T(8,128)S(1)}, u32[]{:S(2)}, u32[]{:S(2)}) collective-permute-start(f32[192,128]{1,0:T(8,128)S(1)} %get-tuple-element.83), channel_id=1, source_target_pairs={{320,447},{321,386},{322,385},{323,388},{324,387},{325,390},{326,3... | collective-permute-start | bytes 294920 | tf_op jit(solution)/shard_map/ppermute | solution.py:299
  55.4 1.3 %collective-permute-start.23 = (f32[192,128]{1,0:T(8,128)S(1)}, f32[192,128]{1,0:T(8,128)S(1)}, u32[]{:S(2)}, u32[]{:S(2)}) collective-permute-start(f32[192,128]{1,0:T(8,128)S(1)} %get-tuple-element.85), channel_id=1, source_target_pairs={{320,385},{321,384},{322,387},{323,386},{324,389},{325,388},{326,3... | collective-permute-start | bytes 294920 | tf_op jit(solution)/shard_map/ppermute | solution.py:299
  56.7 32.8 %collective-permute-done.21.far_ref = f32[192,128]{1,0:T(8,128)S(1)} collective-permute-done((f32[192,128]{1,0:T(8,128)S(1)}, f32[192,128]{1,0:T(8,128)S(1)}, u32[]{:S(2)}, u32[]{:S(2)}) %collective-permute-start.21) | collective-permute-done | bytes 98336 | tf_op jit(solution)/shard_map/ppermute | solution.py:299
  89.5 0.6 shard_map.85
  90.1 1.3 %collective-permute-start.25 = (f32[384,128]{1,0:T(8,128)S(1)}, f32[384,128]{1,0:T(8,128)S(1)}, u32[]{:S(2)}, u32[]{:S(2)}) collective-permute-start(f32[384,128]{1,0:T(8,128)S(1)} %get-tuple-element.88), channel_id=1, source_target_pairs={{384,448},{385,449},{386,450},{387,451},{388,452},{389,453},{390,4... | collective-permute-start | bytes 589832 | tf_op jit(solution)/shard_map/ppermute | solution.py:299
  91.4 1.3 %collective-permute-start.24 = (f32[192,128]{1,0:T(8,128)S(1)}, f32[192,128]{1,0:T(8,128)S(1)}, u32[]{:S(2)}, u32[]{:S(2)}) collective-permute-start(f32[192,128]{1,0:T(8,128)S(1)} %get-tuple-element.87), channel_id=1, source_target_pairs={{384,511},{385,450},{386,449},{387,452},{388,451},{389,454},{390,4... | collective-permute-start | bytes 294920 | tf_op jit(solution)/shard_map/ppermute | solution.py:299
  92.7 1.3 %collective-permute-start.26 = (f32[192,128]{1,0:T(8,128)S(1)}, f32[192,128]{1,0:T(8,128)S(1)}, u32[]{:S(2)}, u32[]{:S(2)}) collective-permute-start(f32[192,128]{1,0:T(8,128)S(1)} %get-tuple-element.89), channel_id=1, source_target_pairs={{384,449},{385,448},{386,451},{387,450},{388,453},{389,452},{390,4... | collective-permute-start | bytes 294920 | tf_op jit(solution)/shard_map/ppermute | solution.py:299
  94.0 0.9 collective-permute-done.24.far_ref
  94.9 1.3 %collective-permute-done.26.near_ref = f32[192,128]{1,0:T(8,128)S(1)} collective-permute-done((f32[192,128]{1,0:T(8,128)S(1)}, f32[192,128]{1,0:T(8,128)S(1)}, u32[]{:S(2)}, u32[]{:S(2)}) %collective-permute-start.26) | collective-permute-done | bytes 98336 | tf_op jit(solution)/shard_map/ppermute | solution.py:299
  96.2 1.8 %shard_map.86 = f32[1536,128]{1,0:T(8,128)} custom-call(bf16[384,1536]{1,0:T(8,128)(2,1)S(1)} %get-tuple-element.56.coarse2_ref, f32[192,128]{1,0:T(8,128)S(1)} %collective-permute-done.24.far_ref, f32[384,128]{1,0:T(8,128)S(1)} %collective-permute-done.25.own_ref, f32[192,128]{1,0:T(8,128)S(1)} %collective-permute-done.26.near_ref, ...), custom_call_target="tpu_custom_call" | custom-call | flops 528482304 | bytes 4000000 | tf_op jit(solution)/shard_map/pallas_call | solution.py:324
  (20 shorter events, 0.1 us)
Async XLA Ops:
  1.0 18.1 %collective-permute-start = (f32[256,128]{1,0:T(8,128)S(1)}, f32[256,128]{1,0:T(8,128)S(1)}, u32[]{:S(2)}, u32[]{:S(2)}) collective-permute-start(f32[256,128]{1,0:T(8,128)S(1)} %get-tuple-element.51), channel_id=1, source_target_pairs={{0,63},{1,2},{2,1},{3,4},{4,3},{5,6},{6,5},{7,8},{8,7},{9,10},{10,... | collective-permute-start | bytes 393224 | tf_op jit(solution)/shard_map/ppermute | solution.py:244
  14.9 6.9 %collective-permute-start.1 = (f32[256,128]{1,0:T(8,128)S(1)}, f32[256,128]{1,0:T(8,128)S(1)}, u32[]{:S(2)}, u32[]{:S(2)}) collective-permute-start(f32[256,128]{1,0:T(8,128)S(1)} %get-tuple-element.52), channel_id=1, source_target_pairs={{0,1},{1,0},{2,3},{3,2},{4,5},{5,4},{6,7},{7,6},{8,9},{9,8},{10,11... | collective-permute-start | bytes 393224 | tf_op jit(solution)/shard_map/ppermute | solution.py:245
  25.0 11.1 %collective-permute-start.4 = (f32[384,128]{1,0:T(8,128)S(1)}, f32[384,128]{1,0:T(8,128)S(1)}, u32[]{:S(2)}, u32[]{:S(2)}) collective-permute-start(f32[384,128]{1,0:T(8,128)S(1)} %get-tuple-element.61), channel_id=1, source_target_pairs={{64,0},{65,1},{66,2},{67,3},{68,4},{69,5},{70,6},{71,7},{72,8},{73... | collective-permute-start | bytes 589832 | tf_op jit(solution)/shard_map/ppermute | solution.py:287
  25.7 10.2 %collective-permute-start.2 = (f32[256,128]{1,0:T(8,128)S(1)}, f32[256,128]{1,0:T(8,128)S(1)}, u32[]{:S(2)}, u32[]{:S(2)}) collective-permute-start(f32[256,128]{1,0:T(8,128)S(1)} %get-tuple-element.58), channel_id=1, source_target_pairs={{0,63},{1,2},{2,1},{3,4},{4,3},{5,6},{6,5},{7,8},{8,7},{9,10},{10,... | collective-permute-start | bytes 393224 | tf_op jit(solution)/shard_map/ppermute | solution.py:244
  29.3 6.9 %collective-permute-start.3 = (f32[256,128]{1,0:T(8,128)S(1)}, f32[256,128]{1,0:T(8,128)S(1)}, u32[]{:S(2)}, u32[]{:S(2)}) collective-permute-start(f32[256,128]{1,0:T(8,128)S(1)} %get-tuple-element.59), channel_id=1, source_target_pairs={{0,1},{1,0},{2,3},{3,2},{4,5},{5,4},{6,7},{7,6},{8,9},{9,8},{10,11... | collective-permute-start | bytes 393224 | tf_op jit(solution)/shard_map/ppermute | solution.py:245
  31.2 10.5 %collective-permute-start.8 = (f32[384,128]{1,0:T(8,128)S(1)}, f32[384,128]{1,0:T(8,128)S(1)}, u32[]{:S(2)}, u32[]{:S(2)}) collective-permute-start(f32[384,128]{1,0:T(8,128)S(1)} %get-tuple-element.61), channel_id=1, source_target_pairs={{128,64},{192,128},{256,192},{320,256},{384,320},{448,384},{129,65... | collective-permute-start | bytes 589832 | tf_op jit(solution)/shard_map/ppermute | solution.py:288
  36.1 5.6 %collective-permute-start.6 = (f32[384,128]{1,0:T(8,128)S(1)}, f32[384,128]{1,0:T(8,128)S(1)}, u32[]{:S(2)}, u32[]{:S(2)}) collective-permute-start(f32[384,128]{1,0:T(8,128)S(1)} %get-tuple-element.63), channel_id=1, source_target_pairs={{0,64},{1,65},{2,66},{3,67},{4,68},{5,69},{6,70},{7,71},{8,72},{9,... | collective-permute-start | bytes 589832 | tf_op jit(solution)/shard_map/ppermute | solution.py:299
  36.8 4.8 %collective-permute-start.5 = (f32[192,128]{1,0:T(8,128)S(1)}, f32[192,128]{1,0:T(8,128)S(1)}, u32[]{:S(2)}, u32[]{:S(2)}) collective-permute-start(f32[192,128]{1,0:T(8,128)S(1)} %get-tuple-element.62), channel_id=1, source_target_pairs={{0,127},{1,66},{2,65},{3,68},{4,67},{5,70},{6,69},{7,72},{8,71},{9... | collective-permute-start | bytes 294920 | tf_op jit(solution)/shard_map/ppermute | solution.py:299
  37.5 4.2 %collective-permute-start.7 = (f32[192,128]{1,0:T(8,128)S(1)}, f32[192,128]{1,0:T(8,128)S(1)}, u32[]{:S(2)}, u32[]{:S(2)}) collective-permute-start(f32[192,128]{1,0:T(8,128)S(1)} %get-tuple-element.64), channel_id=1, source_target_pairs={{0,65},{1,64},{2,67},{3,66},{4,69},{5,68},{6,71},{7,70},{8,73},{9,... | collective-permute-start | bytes 294920 | tf_op jit(solution)/shard_map/ppermute | solution.py:299
  42.3 2.1 %collective-permute-start.10 = (f32[384,128]{1,0:T(8,128)S(1)}, f32[384,128]{1,0:T(8,128)S(1)}, u32[]{:S(2)}, u32[]{:S(2)}) collective-permute-start(f32[384,128]{1,0:T(8,128)S(1)} %get-tuple-element.68), channel_id=1, source_target_pairs={{64,128},{65,129},{66,130},{67,131},{68,132},{69,133},{70,134},{71... | collective-permute-start | bytes 589832 | tf_op jit(solution)/shard_map/ppermute | solution.py:299
  42.9 1.4 %collective-permute-start.9 = (f32[192,128]{1,0:T(8,128)S(1)}, f32[192,128]{1,0:T(8,128)S(1)}, u32[]{:S(2)}, u32[]{:S(2)}) collective-permute-start(f32[192,128]{1,0:T(8,128)S(1)} %get-tuple-element.67), channel_id=1, source_target_pairs={{64,191},{65,130},{66,129},{67,132},{68,131},{69,134},{70,133},{71... | collective-permute-start | bytes 294920 | tf_op jit(solution)/shard_map/ppermute | solution.py:299
  43.6 0.7 collective-permute-start.11
  44.9 2.1 %collective-permute-start.13 = (f32[384,128]{1,0:T(8,128)S(1)}, f32[384,128]{1,0:T(8,128)S(1)}, u32[]{:S(2)}, u32[]{:S(2)}) collective-permute-start(f32[384,128]{1,0:T(8,128)S(1)} %get-tuple-element.72), channel_id=1, source_target_pairs={{128,192},{129,193},{130,194},{131,195},{132,196},{133,197},{134,1... | collective-permute-start | bytes 589832 | tf_op jit(solution)/shard_map/ppermute | solution.py:299
  45.6 1.4 %collective-permute-start.12 = (f32[192,128]{1,0:T(8,128)S(1)}, f32[192,128]{1,0:T(8,128)S(1)}, u32[]{:S(2)}, u32[]{:S(2)}) collective-permute-start(f32[192,128]{1,0:T(8,128)S(1)} %get-tuple-element.71), channel_id=1, source_target_pairs={{128,255},{129,194},{130,193},{131,196},{132,195},{133,198},{134,1... | collective-permute-start | bytes 294920 | tf_op jit(solution)/shard_map/ppermute | solution.py:299
  46.3 0.7 collective-permute-start.14
  47.5 2.1 %collective-permute-start.16 = (f32[384,128]{1,0:T(8,128)S(1)}, f32[384,128]{1,0:T(8,128)S(1)}, u32[]{:S(2)}, u32[]{:S(2)}) collective-permute-start(f32[384,128]{1,0:T(8,128)S(1)} %get-tuple-element.76), channel_id=1, source_target_pairs={{192,256},{193,257},{194,258},{195,259},{196,260},{197,261},{198,2... | collective-permute-start | bytes 589832 | tf_op jit(solution)/shard_map/ppermute | solution.py:299
  48.2 1.4 %collective-permute-start.15 = (f32[192,128]{1,0:T(8,128)S(1)}, f32[192,128]{1,0:T(8,128)S(1)}, u32[]{:S(2)}, u32[]{:S(2)}) collective-permute-start(f32[192,128]{1,0:T(8,128)S(1)} %get-tuple-element.75), channel_id=1, source_target_pairs={{192,319},{193,258},{194,257},{195,260},{196,259},{197,262},{198,2... | collective-permute-start | bytes 294920 | tf_op jit(solution)/shard_map/ppermute | solution.py:299
  48.9 0.7 collective-permute-start.17
  50.2 2.1 %collective-permute-start.19 = (f32[384,128]{1,0:T(8,128)S(1)}, f32[384,128]{1,0:T(8,128)S(1)}, u32[]{:S(2)}, u32[]{:S(2)}) collective-permute-start(f32[384,128]{1,0:T(8,128)S(1)} %get-tuple-element.80), channel_id=1, source_target_pairs={{256,320},{257,321},{258,322},{259,323},{260,324},{261,325},{262,3... | collective-permute-start | bytes 589832 | tf_op jit(solution)/shard_map/ppermute | solution.py:299
  50.8 1.4 %collective-permute-start.18 = (f32[192,128]{1,0:T(8,128)S(1)}, f32[192,128]{1,0:T(8,128)S(1)}, u32[]{:S(2)}, u32[]{:S(2)}) collective-permute-start(f32[192,128]{1,0:T(8,128)S(1)} %get-tuple-element.79), channel_id=1, source_target_pairs={{256,383},{257,322},{258,321},{259,324},{260,323},{261,326},{262,3... | collective-permute-start | bytes 294920 | tf_op jit(solution)/shard_map/ppermute | solution.py:299
  51.5 0.7 collective-permute-start.20
  52.8 36.7 %collective-permute-start.22 = (f32[384,128]{1,0:T(8,128)S(1)}, f32[384,128]{1,0:T(8,128)S(1)}, u32[]{:S(2)}, u32[]{:S(2)}) collective-permute-start(f32[384,128]{1,0:T(8,128)S(1)} %get-tuple-element.84), channel_id=1, source_target_pairs={{320,384},{321,385},{322,386},{323,387},{324,388},{325,389},{326,3... | collective-permute-start | bytes 589832 | tf_op jit(solution)/shard_map/ppermute | solution.py:299
  54.1 35.4 %collective-permute-start.21 = (f32[192,128]{1,0:T(8,128)S(1)}, f32[192,128]{1,0:T(8,128)S(1)}, u32[]{:S(2)}, u32[]{:S(2)}) collective-permute-start(f32[192,128]{1,0:T(8,128)S(1)} %get-tuple-element.83), channel_id=1, source_target_pairs={{320,447},{321,386},{322,385},{323,388},{324,387},{325,390},{326,3... | collective-permute-start | bytes 294920 | tf_op jit(solution)/shard_map/ppermute | solution.py:299
  55.4 34.1 %collective-permute-start.23 = (f32[192,128]{1,0:T(8,128)S(1)}, f32[192,128]{1,0:T(8,128)S(1)}, u32[]{:S(2)}, u32[]{:S(2)}) collective-permute-start(f32[192,128]{1,0:T(8,128)S(1)} %get-tuple-element.85), channel_id=1, source_target_pairs={{320,385},{321,384},{322,387},{323,386},{324,389},{325,388},{326,3... | collective-permute-start | bytes 294920 | tf_op jit(solution)/shard_map/ppermute | solution.py:299
  90.1 6.1 %collective-permute-start.25 = (f32[384,128]{1,0:T(8,128)S(1)}, f32[384,128]{1,0:T(8,128)S(1)}, u32[]{:S(2)}, u32[]{:S(2)}) collective-permute-start(f32[384,128]{1,0:T(8,128)S(1)} %get-tuple-element.88), channel_id=1, source_target_pairs={{384,448},{385,449},{386,450},{387,451},{388,452},{389,453},{390,4... | collective-permute-start | bytes 589832 | tf_op jit(solution)/shard_map/ppermute | solution.py:299
  91.4 3.5 %collective-permute-start.24 = (f32[192,128]{1,0:T(8,128)S(1)}, f32[192,128]{1,0:T(8,128)S(1)}, u32[]{:S(2)}, u32[]{:S(2)}) collective-permute-start(f32[192,128]{1,0:T(8,128)S(1)} %get-tuple-element.87), channel_id=1, source_target_pairs={{384,511},{385,450},{386,449},{387,452},{388,451},{389,454},{390,4... | collective-permute-start | bytes 294920 | tf_op jit(solution)/shard_map/ppermute | solution.py:299
  92.7 3.5 %collective-permute-start.26 = (f32[192,128]{1,0:T(8,128)S(1)}, f32[192,128]{1,0:T(8,128)S(1)}, u32[]{:S(2)}, u32[]{:S(2)}) collective-permute-start(f32[192,128]{1,0:T(8,128)S(1)} %get-tuple-element.89), channel_id=1, source_target_pairs={{384,449},{385,448},{386,451},{387,450},{388,453},{389,452},{390,4... | collective-permute-start | bytes 294920 | tf_op jit(solution)/shard_map/ppermute | solution.py:299
where the time goes:
time: 99.5 us; the launch traced here: 98 us
  starting transfers between devices  41.7 us (42%)
  waiting for transfers between devices  40.6 us (41%)
  Pallas kernels  15.3 us (15%)
    ppermute x21, waiting for transfers between devices, to_slice(): return lax.ppermute(block, ('tm', 'tile'), route)  35.1 us
    ppermute x21, starting transfers between devices, to_slice(): return lax.ppermute(block, ('tm', 'tile'), route)  17.8 us
    ppermute x2, starting transfers between devices, swapped(): lax.ppermute(far, 'tile', [(i, (i + 1 if i % 2 else i - 1) % count) for i...  17.4 us
    ppermute x2, starting transfers between devices, swapped(): near = lax.ppermute(near, 'tile', [(i, i ^ 1) for i in range(count)])  3.84 us
    pallas_call x6, Pallas kernels, on_device(): call(advance, [coarse_all, coarse_rim, coarse_rim, coarse_all], [VMEM] *...  3.4 us
    ppermute x2, waiting for transfers between devices, swapped(): near = lax.ppermute(near, 'tile', [(i, i ^ 1) for i in range(count)])  2.85 us
    ppermute x2, waiting for transfers between devices, swapped(): lax.ppermute(far, 'tile', [(i, (i + 1 if i % 2 else i - 1) % count) for i...  2.73 us
    pallas_call x1, Pallas kernels, on_device(): call(fetch, [(ops.shape, F32), ((rows, 2 * tracers), BF16), (sources.shap...  2.35 us
  transfers between devices with their start and end apart: 27, of which 6 were waited for; matrix products, arithmetic and copies ran while one was open for 0% of the time, Pallas kernels for 6%

commit v1 on v0

--- a/solution.py
+++ b/solution.py
@@ -48,6 +48,12 @@
 def folded(product):
     width = product.shape[1] // 2
     return product[:, :width] + product[:, width:]
+
+
+def folded_twice(product):
+    half = folded(product)
+    rows = half.shape[0] // 2
+    return half[:rows] + half[rows:]
 
 
 def odd_tile():
@@ -104,16 +110,14 @@
     rstart_ref[...] = folded(dot(gather_ref[...], own_ref[...])) * inverse
 
 
-def prepare_late(coarse_hbm, gather_ref, token_ref, spread_ref, coarse2_ref, coarse_ref, sems):
+def split_coarse(coarse_hbm, token_ref, coarse2_ref, coarse_ref, sems):
     copy = pltpu.make_async_copy(coarse_hbm, coarse_ref, sems.at[0])
     copy.start()
-    for b in range(gather_ref.shape[1] // BS):
-        spread_ref[b * BS:(b + 1) * BS, :] = gather_ref[:, b * BS:(b + 1) * BS].astype(F32).T.astype(BF16)
     copy.wait()
-    width = coarse_ref.shape[1]
+    rows = coarse_ref.shape[0]
     high, low = halves(coarse_ref[...])
-    coarse2_ref[:, :width] = high
-    coarse2_ref[:, width:] = low
+    coarse2_ref[:rows, :] = high
+    coarse2_ref[rows:, :] = low
 
 
 def transport(cols_hbm, live_hbm, ops_ref, own_ref, far_ref, near_ref, sources_ref,
@@ -139,9 +143,8 @@
             highs.append(high)
             lows.append(low)
         pieces = jnp.concatenate(pieces, axis=0)
-        tracers = pieces.shape[1] // 2
-        value = folded(dot(jnp.concatenate(highs, axis=1), pieces))
-        value = value + dot(jnp.concatenate(lows, axis=1), pieces[:, :tracers])
+        operator = jnp.concatenate([jnp.concatenate(highs, axis=1), jnp.concatenate(lows, axis=1)], axis=0)
+        value = folded_twice(dot(operator, pieces))
         emit(b, value + sources_ref[b * BS:(b + 1) * BS, :])
 
 
@@ -191,30 +194,34 @@
         sides(jump_ref, nfar_ref, nnear_ref, nfar_ref.shape[0])
 
 
-def second_step_rest(*refs):
-    operands, (gather_ref, inverse_ref) = refs[:7], refs[7:9]
-    end_ref, jump_ref = refs[10:12]
-    first = lax.axis_index("tm") == 0
-
-    @pl.when(first)
+def second_step_rest(chosen, gather_ref, inverse_ref, operands, end_ref, jump_ref, scratch):
+    @pl.when(jnp.logical_not(chosen))
     def _():
         jump_ref[...] = jnp.zeros_like(jump_ref)
 
-    @pl.when(jnp.logical_not(first))
+    @pl.when(chosen)
     def _():
-        restricted_step(operands, gather_ref, inverse_ref, end_ref, jump_ref, *refs[12:])
+        restricted_step(operands, gather_ref, inverse_ref, end_ref, jump_ref, *scratch)
+
+
+def second_step_one(*refs):
+    second_step_rest(lax.axis_index("tm") == 1, refs[7], refs[8], refs[:7], refs[10], refs[11], refs[12:])
+
+
+def second_step_others(*refs):
+    second_step_rest(lax.axis_index("tm") > 1, refs[7], refs[8], refs[:7], refs[10], refs[11], refs[13:])
+    gather_ref, spread_ref = refs[7], refs[12]
+    for b in range(gather_ref.shape[1] // BS):
+        spread_ref[b * BS:(b + 1) * BS, :] = gather_ref[:, b * BS:(b + 1) * BS].astype(F32).T.astype(BF16)
 
 
 def coarse_product(coarse2_ref, far_ref, own_ref, near_ref, window):
-    width = coarse2_ref.shape[1] // 2
     rim, rows = far_ref.shape[0], own_ref.shape[0]
     odd = odd_tile()
     window[pl.ds(pl.multiple_of(odd * (rim + rows), 64), rim), :] = pair(far_ref[...])
     window[pl.ds(pl.multiple_of((1 - odd) * (rim + rows), 64), rim), :] = pair(near_ref[...])
     window[rim:rim + rows, :] = pair(own_ref[...])
-    tracers = own_ref.shape[1]
-    product = folded(dot(coarse2_ref[:, :width], window[...]))
-    return product + dot(coarse2_ref[:, width:], window[:, :tracers])
+    return folded_twice(dot(coarse2_ref[...], window[...]))
 
 
 def advance(coarse2_ref, far_ref, own_ref, near_ref, jump_ref, later_ref, *refs):
@@ -284,8 +291,8 @@
         [HBM, VMEM, VMEM], 4 * coarse * rows * tracers, 3_000_000,
         [pltpu.VMEM((blocks, BS), jnp.int32), pltpu.SemaphoreType.DMA((1,))],
     )(kept(cell_map.reshape(-1, BS)), own, token)
+    later = lax.ppermute(rstart, "tm", [(i + 1, i) for i in range(1, slices - 1)])
     following = lax.ppermute(rstart, "tm", [(1, 0)])
-    later = lax.ppermute(rstart, "tm", [(i + 1, i) for i in range(1, slices - 1)])
     step_scratch = step_scratch + [pltpu.VMEM((rows, 2 * tracers), BF16)]
     step_args = (kept(columns), kept(live), ops, state, far, near, sources, gather, inverse)
     step_flops = step_flops + 4 * coarse * rows * tracers
@@ -307,14 +314,18 @@
         own = to_slice(state, n, lambda i: i)
         if n == 1:
             fine_end, jump = call(
-                second_step_rest, [((rows, tracers), F32), coarse_all],
+                second_step_one, [((rows, tracers), F32), coarse_all],
                 step_in + [VMEM] * 3, step_flops, 8_000_000, step_scratch, aliases={9: 0},
             )(*step_args, fine_end)
-            spread, coarse2 = call(
-                prepare_late, [((rows, coarse), BF16), ((coarse, 2 * reach), BF16)],
-                [HBM] + [VMEM] * 2, 0, 4_000_000,
+            (coarse2,) = call(
+                split_coarse, [((2 * coarse, reach), BF16)], [HBM, VMEM], 0, 4_000_000,
                 [pltpu.VMEM((coarse, reach), F32), pltpu.SemaphoreType.DMA((1,))],
-            )(kept(coarse_op), gather, token)
+            )(kept(coarse_op), token)
+        if n == 2:
+            fine_end, jump, spread = call(
+                second_step_others, [((rows, tracers), F32), coarse_all, ((rows, coarse), BF16)],
+                step_in + [VMEM] * 3, step_flops, 8_000_000, step_scratch, aliases={9: 0},
+            )(*step_args, fine_end)
         if n < slices - 1:
             state, far, near, *image = call(
                 advance, [coarse_all, coarse_rim, coarse_rim, coarse_all],

time: 99.5 us -> 100 us (level)
    pallas_call x2 -> x3, Pallas kernels: 3.47 us -> 3.95 us  [the longest x1 2.46 us: on_device(): call(second_step_others, [((rows, tracers), F32), coarse_all, ((rows, coa...]
where the time goes in v1:
time: 100 us; the launch traced here: 98.5 us
  starting transfers between devices  41.7 us (42%)
  waiting for transfers between devices  40.2 us (40%)
  Pallas kernels  16.2 us (16%)
    ppermute x21, waiting for transfers between devices, to_slice(): return lax.ppermute(block, ('tm', 'tile'), route)  34.6 us
    ppermute x21, starting transfers between devices, to_slice(): return lax.ppermute(block, ('tm', 'tile'), route)  17.8 us
    ppermute x2, starting transfers between devices, swapped(): lax.ppermute(far, 'tile', [(i, (i + 1 if i % 2 else i - 1) % count) for i...  17.4 us
    ppermute x2, starting transfers between devices, swapped(): near = lax.ppermute(near, 'tile', [(i, i ^ 1) for i in range(count)])  3.84 us
    pallas_call x6, Pallas kernels, on_device(): call(advance, [coarse_all, coarse_rim, coarse_rim, coarse_all], [VMEM] *...  3.31 us
    ppermute x2, waiting for transfers between devices, swapped(): near = lax.ppermute(near, 'tile', [(i, i ^ 1) for i in range(count)])  2.85 us
    ppermute x2, waiting for transfers between devices, swapped(): lax.ppermute(far, 'tile', [(i, (i + 1 if i % 2 else i - 1) % count) for i...  2.73 us
    pallas_call x1, Pallas kernels, on_device(): call(second_step_others, [((rows, tracers), F32), coarse_all, ((rows, coa...  2.46 us
  transfers between devices with their start and end apart: 27, of which 6 were waited for; matrix products, arithmetic and copies ran while one was open for 0% of the time, Pallas kernels for 6%

profile of v1, /device:TPU:6, one launch (start us, length us, event | category | flops | bytes accessed | tf_op | source)
XLA Modules:
  0.0 98.5 jit_solution(5491157985542572024)
XLA Ops:
  0.0 1.0 shard_map.74
  1.0 13.9 %collective-permute-start = (f32[256,128]{1,0:T(8,128)S(1)}, f32[256,128]{1,0:T(8,128)S(1)}, u32[]{:S(2)}, u32[]{:S(2)}) collective-permute-start(f32[256,128]{1,0:T(8,128)S(1)} %get-tuple-element.52), channel_id=1, source_target_pairs={{0,63},{1,2},{2,1},{3,4},{4,3},{5,6},{6,5},{7,8},{8,7},{9,10},{10,... | collective-permute-start | bytes 393224 | tf_op jit(solution)/shard_map/ppermute | solution.py:251
  14.9 1.9 %collective-permute-start.1 = (f32[256,128]{1,0:T(8,128)S(1)}, f32[256,128]{1,0:T(8,128)S(1)}, u32[]{:S(2)}, u32[]{:S(2)}) collective-permute-start(f32[256,128]{1,0:T(8,128)S(1)} %get-tuple-element.53), channel_id=1, source_target_pairs={{0,1},{1,0},{2,3},{3,2},{4,5},{5,4},{6,7},{7,6},{8,9},{9,8},{10,11... | collective-permute-start | bytes 393224 | tf_op jit(solution)/shard_map/ppermute | solution.py:252
  16.8 2.3 %shard_map.73 = (f32[12,4,128,128]{3,2,1,0:T(8,128)S(1)}, bf16[1536,256]{1,0:T(8,128)(2,1)S(1)}, f32[1536,128]{1,0:T(8,128)S(1)}) custom-call(f32[12,4,128,128]{3,2,1,0:T(8,128)} %bitcast.9, f32[1536,128]{1,0:T(8,128)} %bitcast.8, f32[1536,128]{1,0:T(8,128)} %sources_ref.1), custom_call_target="tpu_custom_call" | custom-call | bytes 9000000 | tf_op jit(solution)/shard_map/pallas_call | solution.py:276
  19.1 0.0 collective-permute-done.far_ref
  19.1 2.6 %collective-permute-done.1.near_ref = f32[256,128]{1,0:T(8,128)S(1)} collective-permute-done((f32[256,128]{1,0:T(8,128)S(1)}, f32[256,128]{1,0:T(8,128)S(1)}, u32[]{:S(2)}, u32[]{:S(2)}) %collective-permute-start.1) | collective-permute-done | bytes 131104 | tf_op jit(solution)/shard_map/ppermute | solution.py:252
  21.7 1.8 %shard_map.75 = (bf16[1536,256]{1,0:T(8,128)(2,1)S(1)}, f32[256,128]{1,0:T(8,128)S(1)}, f32[256,128]{1,0:T(8,128)S(1)}, f32[8,128]{1,0:T(8,128)S(1)}) custom-call(s32[4,12]{1,0:T(4,128)} %bitcast.10, s32[1,12]{1,0:T(1,128)} %refs_1_.5, f32[12,4,128,128]{3,2,1,0:T(8,128)S(1)} %get-tuple-element.50.ops_ref.refs_2_, ...), custom_call_target="tpu_custom_call" | custom-call | flops 603979776 | bytes 6000000 | tf_op jit(solution)/shard_map/pallas_call | solution.py:284
  23.5 1.5 %shard_map.77 = (bf16[384,1536]{1,0:T(8,128)(2,1)S(1)}, f32[384,128]{1,0:T(8,128)S(1)}, f32[384,128]{1,0:T(8,128)S(1)}) custom-call(s32[12,128]{1,0:T(8,128)} %bitcast.14, bf16[1536,256]{1,0:T(8,128)(2,1)S(1)} %get-tuple-element.51.own_ref, f32[8,128]{1,0:T(8,128)S(1)} %get-tuple-element.55.token_ref), custom_call_target="tpu_custom_call" | custom-call | flops 301989888 | bytes 3000000 | tf_op jit(solution)/shard_map/pallas_call | solution.py:289
  25.1 0.7 collective-permute-start.4
  25.7 3.6 %collective-permute-start.2 = (f32[256,128]{1,0:T(8,128)S(1)}, f32[256,128]{1,0:T(8,128)S(1)}, u32[]{:S(2)}, u32[]{:S(2)}) collective-permute-start(f32[256,128]{1,0:T(8,128)S(1)} %get-tuple-element.57), channel_id=1, source_target_pairs={{0,63},{1,2},{2,1},{3,4},{4,3},{5,6},{6,5},{7,8},{8,7},{9,10},{10,... | collective-permute-start | bytes 393224 | tf_op jit(solution)/shard_map/ppermute | solution.py:251
  29.3 1.9 %collective-permute-start.3 = (f32[256,128]{1,0:T(8,128)S(1)}, f32[256,128]{1,0:T(8,128)S(1)}, u32[]{:S(2)}, u32[]{:S(2)}) collective-permute-start(f32[256,128]{1,0:T(8,128)S(1)} %get-tuple-element.58), channel_id=1, source_target_pairs={{0,1},{1,0},{2,3},{3,2},{4,5},{5,4},{6,7},{7,6},{8,9},{9,8},{10,11... | collective-permute-start | bytes 393224 | tf_op jit(solution)/shard_map/ppermute | solution.py:252
  31.3 1.9 %collective-permute-start.8 = (f32[384,128]{1,0:T(8,128)S(1)}, f32[384,128]{1,0:T(8,128)S(1)}, u32[]{:S(2)}, u32[]{:S(2)}) collective-permute-start(f32[384,128]{1,0:T(8,128)S(1)} %get-tuple-element.61), channel_id=1, source_target_pairs={{128,64},{192,128},{256,192},{320,256},{384,320},{448,384},{129,65... | collective-permute-start | bytes 589832 | tf_op jit(solution)/shard_map/ppermute | solution.py:294
  33.2 2.7 %collective-permute-done.2.refs_4_ = f32[256,128]{1,0:T(8,128)S(1)} collective-permute-done((f32[256,128]{1,0:T(8,128)S(1)}, f32[256,128]{1,0:T(8,128)S(1)}, u32[]{:S(2)}, u32[]{:S(2)}) %collective-permute-start.2) | collective-permute-done | bytes 131104 | tf_op jit(solution)/shard_map/ppermute | solution.py:251
  35.9 0.3 collective-permute-done.3.refs_5_
  36.2 0.7 collective-permute-start.6
  36.9 0.7 collective-permute-start.5
  37.6 0.7 collective-permute-start.7
  38.3 1.4 %shard_map.76.coarse2_ref = bf16[768,768]{1,0:T(8,128)(2,1)S(1)} custom-call(f32[384,768]{1,0:T(8,128)} %coarse_hbm.1, f32[8,128]{1,0:T(8,128)S(1)} %get-tuple-element.55.token_ref), custom_call_target="tpu_custom_call" | custom-call | bytes 4000000 | tf_op jit(solution)/shard_map/pallas_call | solution.py:320
  39.7 0.1 shard_map.79
  39.8 0.6 shard_map.80
  40.4 0.7 collective-permute-start.10
  41.0 0.7 collective-permute-start.9
  41.7 0.7 collective-permute-start.11
  42.4 2.5 %shard_map.81 = (f32[1536,128]{1,0:T(8,128)S(1)}, f32[384,128]{1,0:T(8,128)S(1)}, bf16[1536,384]{1,0:T(8,128)(2,1)S(1)}) custom-call(s32[4,12]{1,0:T(4,128)} %bitcast.13, s32[1,12]{1,0:T(1,128)} %refs_1_.5, f32[12,4,128,128]{3,2,1,0:T(8,128)S(1)} %get-tuple-element.50.ops_ref.refs_2_, ...), custom_call_target="tpu_custom_call", output_to_operand_aliasing={{0}: (9, {})} | custom-call | flops 905969664 | bytes 8000000 | tf_op jit(solution)/shard_map/pallas_call | solution.py:325
  44.9 0.6 shard_map.82
  45.4 0.7 collective-permute-start.13
  46.1 0.7 collective-permute-start.12
  46.8 0.7 collective-permute-start.14
  47.5 0.6 shard_map.83
  48.0 0.7 collective-permute-start.16
  48.7 0.7 collective-permute-start.15
  49.4 0.7 collective-permute-start.17
  50.1 0.6 shard_map.84
  50.7 0.7 collective-permute-start.19
  51.3 0.7 collective-permute-start.18
  52.0 0.7 collective-permute-start.20
  52.7 0.6 shard_map.85
  53.3 1.3 %collective-permute-start.22 = (f32[384,128]{1,0:T(8,128)S(1)}, f32[384,128]{1,0:T(8,128)S(1)}, u32[]{:S(2)}, u32[]{:S(2)}) collective-permute-start(f32[384,128]{1,0:T(8,128)S(1)} %get-tuple-element.86), channel_id=1, source_target_pairs={{320,384},{321,385},{322,386},{323,387},{324,388},{325,389},{326,3... | collective-permute-start | bytes 589832 | tf_op jit(solution)/shard_map/ppermute | solution.py:306
  54.6 1.3 %collective-permute-start.21 = (f32[192,128]{1,0:T(8,128)S(1)}, f32[192,128]{1,0:T(8,128)S(1)}, u32[]{:S(2)}, u32[]{:S(2)}) collective-permute-start(f32[192,128]{1,0:T(8,128)S(1)} %get-tuple-element.85), channel_id=1, source_target_pairs={{320,447},{321,386},{322,385},{323,388},{324,387},{325,390},{326,3... | collective-permute-start | bytes 294920 | tf_op jit(solution)/shard_map/ppermute | solution.py:306
  55.9 1.3 %collective-permute-start.23 = (f32[192,128]{1,0:T(8,128)S(1)}, f32[192,128]{1,0:T(8,128)S(1)}, u32[]{:S(2)}, u32[]{:S(2)}) collective-permute-start(f32[192,128]{1,0:T(8,128)S(1)} %get-tuple-element.87), channel_id=1, source_target_pairs={{320,385},{321,384},{322,387},{323,386},{324,389},{325,388},{326,3... | collective-permute-start | bytes 294920 | tf_op jit(solution)/shard_map/ppermute | solution.py:306
  57.2 32.3 %collective-permute-done.21.far_ref = f32[192,128]{1,0:T(8,128)S(1)} collective-permute-done((f32[192,128]{1,0:T(8,128)S(1)}, f32[192,128]{1,0:T(8,128)S(1)}, u32[]{:S(2)}, u32[]{:S(2)}) %collective-permute-start.21) | collective-permute-done | bytes 98336 | tf_op jit(solution)/shard_map/ppermute | solution.py:306
  89.5 0.5 shard_map.86
  90.1 1.3 %collective-permute-start.25 = (f32[384,128]{1,0:T(8,128)S(1)}, f32[384,128]{1,0:T(8,128)S(1)}, u32[]{:S(2)}, u32[]{:S(2)}) collective-permute-start(f32[384,128]{1,0:T(8,128)S(1)} %get-tuple-element.90), channel_id=1, source_target_pairs={{384,448},{385,449},{386,450},{387,451},{388,452},{389,453},{390,4... | collective-permute-start | bytes 589832 | tf_op jit(solution)/shard_map/ppermute | solution.py:306
  91.4 1.3 %collective-permute-start.24 = (f32[192,128]{1,0:T(8,128)S(1)}, f32[192,128]{1,0:T(8,128)S(1)}, u32[]{:S(2)}, u32[]{:S(2)}) collective-permute-start(f32[192,128]{1,0:T(8,128)S(1)} %get-tuple-element.89), channel_id=1, source_target_pairs={{384,511},{385,450},{386,449},{387,452},{388,451},{389,454},{390,4... | collective-permute-start | bytes 294920 | tf_op jit(solution)/shard_map/ppermute | solution.py:306
  92.7 1.3 %collective-permute-start.26 = (f32[192,128]{1,0:T(8,128)S(1)}, f32[192,128]{1,0:T(8,128)S(1)}, u32[]{:S(2)}, u32[]{:S(2)}) collective-permute-start(f32[192,128]{1,0:T(8,128)S(1)} %get-tuple-element.91), channel_id=1, source_target_pairs={{384,449},{385,448},{386,451},{387,450},{388,453},{389,452},{390,4... | collective-permute-start | bytes 294920 | tf_op jit(solution)/shard_map/ppermute | solution.py:306
  94.0 0.9 collective-permute-done.24.far_ref
  94.9 1.3 %collective-permute-done.26.near_ref = f32[192,128]{1,0:T(8,128)S(1)} collective-permute-done((f32[192,128]{1,0:T(8,128)S(1)}, f32[192,128]{1,0:T(8,128)S(1)}, u32[]{:S(2)}, u32[]{:S(2)}) %collective-permute-start.26) | collective-permute-done | bytes 98336 | tf_op jit(solution)/shard_map/ppermute | solution.py:306
  96.2 2.3 %shard_map.87 = f32[1536,128]{1,0:T(8,128)} custom-call(bf16[768,768]{1,0:T(8,128)(2,1)S(1)} %shard_map.76.coarse2_ref, f32[192,128]{1,0:T(8,128)S(1)} %collective-permute-done.24.far_ref, f32[384,128]{1,0:T(8,128)S(1)} %collective-permute-done.25.own_ref, f32[192,128]{1,0:T(8,128)S(1)} %collective-permute-done.26.near_ref, ...), custom_call_target="tpu_custom_call" | custom-call | flops 528482304 | bytes 4000000 | tf_op jit(solution)/shard_map/pallas_call | solution.py:335
  (21 shorter events, 0.1 us)
Async XLA Ops:
  1.0 18.1 %collective-permute-start = (f32[256,128]{1,0:T(8,128)S(1)}, f32[256,128]{1,0:T(8,128)S(1)}, u32[]{:S(2)}, u32[]{:S(2)}) collective-permute-start(f32[256,128]{1,0:T(8,128)S(1)} %get-tuple-element.52), channel_id=1, source_target_pairs={{0,63},{1,2},{2,1},{3,4},{4,3},{5,6},{6,5},{7,8},{8,7},{9,10},{10,... | collective-permute-start | bytes 393224 | tf_op jit(solution)/shard_map/ppermute | solution.py:251
  14.9 6.9 %collective-permute-start.1 = (f32[256,128]{1,0:T(8,128)S(1)}, f32[256,128]{1,0:T(8,128)S(1)}, u32[]{:S(2)}, u32[]{:S(2)}) collective-permute-start(f32[256,128]{1,0:T(8,128)S(1)} %get-tuple-element.53), channel_id=1, source_target_pairs={{0,1},{1,0},{2,3},{3,2},{4,5},{5,4},{6,7},{7,6},{8,9},{9,8},{10,11... | collective-permute-start | bytes 393224 | tf_op jit(solution)/shard_map/ppermute | solution.py:252
  25.1 11.1 %collective-permute-start.4 = (f32[384,128]{1,0:T(8,128)S(1)}, f32[384,128]{1,0:T(8,128)S(1)}, u32[]{:S(2)}, u32[]{:S(2)}) collective-permute-start(f32[384,128]{1,0:T(8,128)S(1)} %get-tuple-element.61), channel_id=1, source_target_pairs={{64,0},{65,1},{66,2},{67,3},{68,4},{69,5},{70,6},{71,7},{72,8},{73... | collective-permute-start | bytes 589832 | tf_op jit(solution)/shard_map/ppermute | solution.py:295
  25.7 10.2 %collective-permute-start.2 = (f32[256,128]{1,0:T(8,128)S(1)}, f32[256,128]{1,0:T(8,128)S(1)}, u32[]{:S(2)}, u32[]{:S(2)}) collective-permute-start(f32[256,128]{1,0:T(8,128)S(1)} %get-tuple-element.57), channel_id=1, source_target_pairs={{0,63},{1,2},{2,1},{3,4},{4,3},{5,6},{6,5},{7,8},{8,7},{9,10},{10,... | collective-permute-start | bytes 393224 | tf_op jit(solution)/shard_map/ppermute | solution.py:251
  29.3 6.9 %collective-permute-start.3 = (f32[256,128]{1,0:T(8,128)S(1)}, f32[256,128]{1,0:T(8,128)S(1)}, u32[]{:S(2)}, u32[]{:S(2)}) collective-permute-start(f32[256,128]{1,0:T(8,128)S(1)} %get-tuple-element.58), channel_id=1, source_target_pairs={{0,1},{1,0},{2,3},{3,2},{4,5},{5,4},{6,7},{7,6},{8,9},{9,8},{10,11... | collective-permute-start | bytes 393224 | tf_op jit(solution)/shard_map/ppermute | solution.py:252
  31.3 8.5 %collective-permute-start.8 = (f32[384,128]{1,0:T(8,128)S(1)}, f32[384,128]{1,0:T(8,128)S(1)}, u32[]{:S(2)}, u32[]{:S(2)}) collective-permute-start(f32[384,128]{1,0:T(8,128)S(1)} %get-tuple-element.61), channel_id=1, source_target_pairs={{128,64},{192,128},{256,192},{320,256},{384,320},{448,384},{129,65... | collective-permute-start | bytes 589832 | tf_op jit(solution)/shard_map/ppermute | solution.py:294
  36.2 3.6 %collective-permute-start.6 = (f32[384,128]{1,0:T(8,128)S(1)}, f32[384,128]{1,0:T(8,128)S(1)}, u32[]{:S(2)}, u32[]{:S(2)}) collective-permute-start(f32[384,128]{1,0:T(8,128)S(1)} %get-tuple-element.63), channel_id=1, source_target_pairs={{0,64},{1,65},{2,66},{3,67},{4,68},{5,69},{6,70},{7,71},{8,72},{9,... | collective-permute-start | bytes 589832 | tf_op jit(solution)/shard_map/ppermute | solution.py:306
  36.9 2.9 %collective-permute-start.5 = (f32[192,128]{1,0:T(8,128)S(1)}, f32[192,128]{1,0:T(8,128)S(1)}, u32[]{:S(2)}, u32[]{:S(2)}) collective-permute-start(f32[192,128]{1,0:T(8,128)S(1)} %get-tuple-element.62), channel_id=1, source_target_pairs={{0,127},{1,66},{2,65},{3,68},{4,67},{5,70},{6,69},{7,72},{8,71},{9... | collective-permute-start | bytes 294920 | tf_op jit(solution)/shard_map/ppermute | solution.py:306
  37.6 2.2 %collective-permute-start.7 = (f32[192,128]{1,0:T(8,128)S(1)}, f32[192,128]{1,0:T(8,128)S(1)}, u32[]{:S(2)}, u32[]{:S(2)}) collective-permute-start(f32[192,128]{1,0:T(8,128)S(1)} %get-tuple-element.64), channel_id=1, source_target_pairs={{0,65},{1,64},{2,67},{3,66},{4,69},{5,68},{6,71},{7,70},{8,73},{9,... | collective-permute-start | bytes 294920 | tf_op jit(solution)/shard_map/ppermute | solution.py:306
  40.4 4.5 %collective-permute-start.10 = (f32[384,128]{1,0:T(8,128)S(1)}, f32[384,128]{1,0:T(8,128)S(1)}, u32[]{:S(2)}, u32[]{:S(2)}) collective-permute-start(f32[384,128]{1,0:T(8,128)S(1)} %get-tuple-element.68), channel_id=1, source_target_pairs={{64,128},{65,129},{66,130},{67,131},{68,132},{69,133},{70,134},{71... | collective-permute-start | bytes 589832 | tf_op jit(solution)/shard_map/ppermute | solution.py:306
  41.0 3.8 %collective-permute-start.9 = (f32[192,128]{1,0:T(8,128)S(1)}, f32[192,128]{1,0:T(8,128)S(1)}, u32[]{:S(2)}, u32[]{:S(2)}) collective-permute-start(f32[192,128]{1,0:T(8,128)S(1)} %get-tuple-element.67), channel_id=1, source_target_pairs={{64,191},{65,130},{66,129},{67,132},{68,131},{69,134},{70,133},{71... | collective-permute-start | bytes 294920 | tf_op jit(solution)/shard_map/ppermute | solution.py:306
  41.7 3.2 %collective-permute-start.11 = (f32[192,128]{1,0:T(8,128)S(1)}, f32[192,128]{1,0:T(8,128)S(1)}, u32[]{:S(2)}, u32[]{:S(2)}) collective-permute-start(f32[192,128]{1,0:T(8,128)S(1)} %get-tuple-element.69), channel_id=1, source_target_pairs={{64,129},{65,128},{66,131},{67,130},{68,133},{69,132},{70,135},{71... | collective-permute-start | bytes 294920 | tf_op jit(solution)/shard_map/ppermute | solution.py:306
  45.4 2.1 %collective-permute-start.13 = (f32[384,128]{1,0:T(8,128)S(1)}, f32[384,128]{1,0:T(8,128)S(1)}, u32[]{:S(2)}, u32[]{:S(2)}) collective-permute-start(f32[384,128]{1,0:T(8,128)S(1)} %get-tuple-element.74), channel_id=1, source_target_pairs={{128,192},{129,193},{130,194},{131,195},{132,196},{133,197},{134,1... | collective-permute-start | bytes 589832 | tf_op jit(solution)/shard_map/ppermute | solution.py:306
  46.1 1.4 %collective-permute-start.12 = (f32[192,128]{1,0:T(8,128)S(1)}, f32[192,128]{1,0:T(8,128)S(1)}, u32[]{:S(2)}, u32[]{:S(2)}) collective-permute-start(f32[192,128]{1,0:T(8,128)S(1)} %get-tuple-element.73), channel_id=1, source_target_pairs={{128,255},{129,194},{130,193},{131,196},{132,195},{133,198},{134,1... | collective-permute-start | bytes 294920 | tf_op jit(solution)/shard_map/ppermute | solution.py:306
  46.8 0.7 collective-permute-start.14
  48.0 2.1 %collective-permute-start.16 = (f32[384,128]{1,0:T(8,128)S(1)}, f32[384,128]{1,0:T(8,128)S(1)}, u32[]{:S(2)}, u32[]{:S(2)}) collective-permute-start(f32[384,128]{1,0:T(8,128)S(1)} %get-tuple-element.78), channel_id=1, source_target_pairs={{192,256},{193,257},{194,258},{195,259},{196,260},{197,261},{198,2... | collective-permute-start | bytes 589832 | tf_op jit(solution)/shard_map/ppermute | solution.py:306
  48.7 1.4 %collective-permute-start.15 = (f32[192,128]{1,0:T(8,128)S(1)}, f32[192,128]{1,0:T(8,128)S(1)}, u32[]{:S(2)}, u32[]{:S(2)}) collective-permute-start(f32[192,128]{1,0:T(8,128)S(1)} %get-tuple-element.77), channel_id=1, source_target_pairs={{192,319},{193,258},{194,257},{195,260},{196,259},{197,262},{198,2... | collective-permute-start | bytes 294920 | tf_op jit(solution)/shard_map/ppermute | solution.py:306
  49.4 0.7 collective-permute-start.17
  50.7 2.1 %collective-permute-start.19 = (f32[384,128]{1,0:T(8,128)S(1)}, f32[384,128]{1,0:T(8,128)S(1)}, u32[]{:S(2)}, u32[]{:S(2)}) collective-permute-start(f32[384,128]{1,0:T(8,128)S(1)} %get-tuple-element.82), channel_id=1, source_target_pairs={{256,320},{257,321},{258,322},{259,323},{260,324},{261,325},{262,3... | collective-permute-start | bytes 589832 | tf_op jit(solution)/shard_map/ppermute | solution.py:306
  51.3 1.4 %collective-permute-start.18 = (f32[192,128]{1,0:T(8,128)S(1)}, f32[192,128]{1,0:T(8,128)S(1)}, u32[]{:S(2)}, u32[]{:S(2)}) collective-permute-start(f32[192,128]{1,0:T(8,128)S(1)} %get-tuple-element.81), channel_id=1, source_target_pairs={{256,383},{257,322},{258,321},{259,324},{260,323},{261,326},{262,3... | collective-permute-start | bytes 294920 | tf_op jit(solution)/shard_map/ppermute | solution.py:306
  52.0 0.7 collective-permute-start.20
  53.3 36.2 %collective-permute-start.22 = (f32[384,128]{1,0:T(8,128)S(1)}, f32[384,128]{1,0:T(8,128)S(1)}, u32[]{:S(2)}, u32[]{:S(2)}) collective-permute-start(f32[384,128]{1,0:T(8,128)S(1)} %get-tuple-element.86), channel_id=1, source_target_pairs={{320,384},{321,385},{322,386},{323,387},{324,388},{325,389},{326,3... | collective-permute-start | bytes 589832 | tf_op jit(solution)/shard_map/ppermute | solution.py:306
  54.6 34.9 %collective-permute-start.21 = (f32[192,128]{1,0:T(8,128)S(1)}, f32[192,128]{1,0:T(8,128)S(1)}, u32[]{:S(2)}, u32[]{:S(2)}) collective-permute-start(f32[192,128]{1,0:T(8,128)S(1)} %get-tuple-element.85), channel_id=1, source_target_pairs={{320,447},{321,386},{322,385},{323,388},{324,387},{325,390},{326,3... | collective-permute-start | bytes 294920 | tf_op jit(solution)/shard_map/ppermute | solution.py:306
  55.9 33.6 %collective-permute-start.23 = (f32[192,128]{1,0:T(8,128)S(1)}, f32[192,128]{1,0:T(8,128)S(1)}, u32[]{:S(2)}, u32[]{:S(2)}) collective-permute-start(f32[192,128]{1,0:T(8,128)S(1)} %get-tuple-element.87), channel_id=1, source_target_pairs={{320,385},{321,384},{322,387},{323,386},{324,389},{325,388},{326,3... | collective-permute-start | bytes 294920 | tf_op jit(solution)/shard_map/ppermute | solution.py:306
  90.1 6.1 %collective-permute-start.25 = (f32[384,128]{1,0:T(8,128)S(1)}, f32[384,128]{1,0:T(8,128)S(1)}, u32[]{:S(2)}, u32[]{:S(2)}) collective-permute-start(f32[384,128]{1,0:T(8,128)S(1)} %get-tuple-element.90), channel_id=1, source_target_pairs={{384,448},{385,449},{386,450},{387,451},{388,452},{389,453},{390,4... | collective-permute-start | bytes 589832 | tf_op jit(solution)/shard_map/ppermute | solution.py:306
  91.4 3.5 %collective-permute-start.24 = (f32[192,128]{1,0:T(8,128)S(1)}, f32[192,128]{1,0:T(8,128)S(1)}, u32[]{:S(2)}, u32[]{:S(2)}) collective-permute-start(f32[192,128]{1,0:T(8,128)S(1)} %get-tuple-element.89), channel_id=1, source_target_pairs={{384,511},{385,450},{386,449},{387,452},{388,451},{389,454},{390,4... | collective-permute-start | bytes 294920 | tf_op jit(solution)/shard_map/ppermute | solution.py:306
  92.7 3.5 %collective-permute-start.26 = (f32[192,128]{1,0:T(8,128)S(1)}, f32[192,128]{1,0:T(8,128)S(1)}, u32[]{:S(2)}, u32[]{:S(2)}) collective-permute-start(f32[192,128]{1,0:T(8,128)S(1)} %get-tuple-element.91), channel_id=1, source_target_pairs={{384,449},{385,448},{386,451},{387,450},{388,453},{389,452},{390,4... | collective-permute-start | bytes 294920 | tf_op jit(solution)/shard_map/ppermute | solution.py:306

commit v2 on v1

--- a/solution.py
+++ b/solution.py
@@ -79,6 +79,25 @@
     for copy in copies:
         copy.start()
     return copies
+
+
+def in_turn(kernel, operand_count, outs, in_specs, flops, nbytes, scratch, operands, order):
+    def predicated(core, skipped):
+        def body(*refs):
+            @pl.when(lax.rem(lax.axis_index("tm"), 2) == core)
+            def _():
+                kernel(*refs[:operand_count], *refs[operand_count + skipped:])
+
+        return body
+
+    count = len(outs)
+    held = call(predicated(1, 0), outs, in_specs, flops, nbytes, scratch)(*operands)
+    between = order()
+    held = call(
+        predicated(0, count), outs, in_specs + [VMEM] * count, flops, nbytes, scratch,
+        aliases={operand_count + index: index for index in range(count)},
+    )(*operands, *held)
+    return held, between
 
 
 def fetch(ops_ref, starts_ref, sources_ref, ops_out, own_ref, sources_out, held, sems):
@@ -215,12 +234,16 @@
         spread_ref[b * BS:(b + 1) * BS, :] = gather_ref[:, b * BS:(b + 1) * BS].astype(F32).T.astype(BF16)
 
 
-def coarse_product(coarse2_ref, far_ref, own_ref, near_ref, window):
+def fill(far_ref, own_ref, near_ref, window):
     rim, rows = far_ref.shape[0], own_ref.shape[0]
     odd = odd_tile()
     window[pl.ds(pl.multiple_of(odd * (rim + rows), 64), rim), :] = pair(far_ref[...])
     window[pl.ds(pl.multiple_of((1 - odd) * (rim + rows), 64), rim), :] = pair(near_ref[...])
     window[rim:rim + rows, :] = pair(own_ref[...])
+
+
+def coarse_product(coarse2_ref, far_ref, own_ref, near_ref, window):
+    fill(far_ref, own_ref, near_ref, window)
     return folded_twice(dot(coarse2_ref[...], window[...]))
 
 
@@ -233,7 +256,10 @@
 
 
 def finish(coarse2_ref, far_ref, own_ref, near_ref, image_ref, spread_ref, end_ref, out_hbm, window, held, sems):
-    image = image_ref[...] + coarse_product(coarse2_ref, far_ref, own_ref, near_ref, window)
+    fill(far_ref, own_ref, near_ref, window)
+    rows, tracers = own_ref.shape
+    image = folded(dot(coarse2_ref[:rows, :], window[...]))
+    image = image_ref[...] + image + dot(coarse2_ref[rows:, :], window[:, :tracers])
     split = pair(image)
     copies = []
     for b in range(sems.shape[0]):
@@ -272,11 +298,11 @@
     coarse_all = ((coarse, tracers), F32)
 
     far, near = call(ends, [side, side], [HBM], 0, 500_000, [pltpu.SemaphoreType.DMA((2,))])(kept(first_state))
-    far, near = swapped(far, near)
-    ops, own, sources = call(
-        fetch, [(ops.shape, F32), ((rows, 2 * tracers), BF16), (sources.shape, F32)],
+    (ops, own, sources), (far, near) = in_turn(
+        fetch, 3, [(ops.shape, F32), ((rows, 2 * tracers), BF16), (sources.shape, F32)],
         [HBM] * 3, 0, 9_000_000, [pltpu.VMEM((rows, tracers), F32), pltpu.SemaphoreType.DMA((3,))],
-    )(kept(ops), kept(first_state), kept(sources))
+        (kept(ops), kept(first_state), kept(sources)), lambda: swapped(far, near),
+    )
 
     step_in = [HBM] * 2 + [VMEM] * 5
     step_scratch = [pltpu.SMEM(columns.shape, jnp.int32), pltpu.SMEM(live.shape, jnp.int32), window,
@@ -285,12 +311,12 @@
         first_step, [((rows, 2 * tracers), BF16), side, side, ((8, tracers), F32)],
         step_in, step_flops, 6_000_000, step_scratch + [pltpu.VMEM((2 * HALO, tracers), F32)],
     )(kept(columns), kept(live), ops, own, far, near, sources)
-    far, near = swapped(far, near)
-    gather, inverse, rstart = call(
-        prepare, [((coarse, rows), BF16), coarse_all, coarse_all],
+    (gather, inverse, rstart), (far, near) = in_turn(
+        prepare, 3, [((coarse, rows), BF16), coarse_all, coarse_all],
         [HBM, VMEM, VMEM], 4 * coarse * rows * tracers, 3_000_000,
         [pltpu.VMEM((blocks, BS), jnp.int32), pltpu.SemaphoreType.DMA((1,))],
-    )(kept(cell_map.reshape(-1, BS)), own, token)
+        (kept(cell_map.reshape(-1, BS)), own, token), lambda: swapped(far, near),
+    )
     later = lax.ppermute(rstart, "tm", [(i + 1, i) for i in range(1, slices - 1)])
     following = lax.ppermute(rstart, "tm", [(1, 0)])
     step_scratch = step_scratch + [pltpu.VMEM((rows, 2 * tracers), BF16)]

time: 100 us -> 101 us (1.010)
  waiting for transfers between devices: 40.2 us -> 41.4 us
    ppermute x21, waiting for transfers between devices: 34.6 us -> 35.9 us  [to_slice(): return lax.ppermute(block, ('tm', 'tile'), route)]
    pallas_call x2 -> x4, Pallas kernels: 3.85 us -> 3.95 us  [the longest x2 3.87 us: in_turn(): call(predicated(0, count), outs, in_specs + [VMEM] * count, flops, nbytes...]
where the time goes in v2:
time: 101 us; the launch traced here: 99.3 us
  starting transfers between devices  41.7 us (41%)
  waiting for transfers between devices  41.4 us (41%)
  Pallas kernels  15.8 us (16%)
    ppermute x21, waiting for transfers between devices, to_slice(): return lax.ppermute(block, ('tm', 'tile'), route)  35.9 us
    ppermute x21, starting transfers between devices, to_slice(): return lax.ppermute(block, ('tm', 'tile'), route)  17.8 us
    ppermute x2, starting transfers between devices, swapped(): lax.ppermute(far, 'tile', [(i, (i + 1 if i % 2 else i - 1) % count) for i...  17.4 us
    pallas_call x2, Pallas kernels, in_turn(): call(predicated(0, count), outs, in_specs + [VMEM] * count, flops, nbytes...  3.87 us
    ppermute x2, starting transfers between devices, swapped(): near = lax.ppermute(near, 'tile', [(i, i ^ 1) for i in range(count)])  3.84 us
    pallas_call x6, Pallas kernels, on_device(): call(advance, [coarse_all, coarse_rim, coarse_rim, coarse_all], [VMEM] *...  3.31 us
    ppermute x2, waiting for transfers between devices, swapped(): near = lax.ppermute(near, 'tile', [(i, i ^ 1) for i in range(count)])  2.78 us
    ppermute x2, waiting for transfers between devices, swapped(): lax.ppermute(far, 'tile', [(i, (i + 1 if i % 2 else i - 1) % count) for i...  2.73 us
  transfers between devices with their start and end apart: 27, of which 6 were waited for; matrix products, arithmetic and copies ran while one was open for 0% of the time, Pallas kernels for 6%

profile of v2, /device:TPU:6, one launch (start us, length us, event | category | flops | bytes accessed | tf_op | source)
XLA Modules:
  0.0 99.3 jit_solution(9754013635962274055)
XLA Ops:
  0.0 1.0 shard_map.75
  1.0 13.9 %collective-permute-start = (f32[256,128]{1,0:T(8,128)S(1)}, f32[256,128]{1,0:T(8,128)S(1)}, u32[]{:S(2)}, u32[]{:S(2)}) collective-permute-start(f32[256,128]{1,0:T(8,128)S(1)} %get-tuple-element.61), channel_id=1, source_target_pairs={{0,63},{1,2},{2,1},{3,4},{4,3},{5,6},{6,5},{7,8},{8,7},{9,10},{10,... | collective-permute-start | bytes 393224 | tf_op jit(solution)/shard_map/ppermute | solution.py:277
  14.9 1.9 %collective-permute-start.1 = (f32[256,128]{1,0:T(8,128)S(1)}, f32[256,128]{1,0:T(8,128)S(1)}, u32[]{:S(2)}, u32[]{:S(2)}) collective-permute-start(f32[256,128]{1,0:T(8,128)S(1)} %get-tuple-element.62), channel_id=1, source_target_pairs={{0,1},{1,0},{2,3},{3,2},{4,5},{5,4},{6,7},{7,6},{8,9},{9,8},{10,11... | collective-permute-start | bytes 393224 | tf_op jit(solution)/shard_map/ppermute | solution.py:278
  16.8 2.4 %shard_map.74 = (f32[12,4,128,128]{3,2,1,0:T(8,128)S(1)}, bf16[1536,256]{1,0:T(8,128)(2,1)S(1)}, f32[1536,128]{1,0:T(8,128)S(1)}) custom-call(f32[12,4,128,128]{3,2,1,0:T(8,128)} %bitcast.8, f32[1536,128]{1,0:T(8,128)} %bitcast.11, f32[1536,128]{1,0:T(8,128)} %refs_2_.3, ...), custom_call_target="tpu_custom_call", output_to_operand_aliasing={{0}: (3, {}), {1}: (4, {}), {2}: (5, {})} | custom-call | bytes 9000000 | tf_op jit(solution)/shard_map/pallas_call | solution.py:96
  19.2 0.0 collective-permute-done.far_ref
  19.2 2.5 %collective-permute-done.1.near_ref = f32[256,128]{1,0:T(8,128)S(1)} collective-permute-done((f32[256,128]{1,0:T(8,128)S(1)}, f32[256,128]{1,0:T(8,128)S(1)}, u32[]{:S(2)}, u32[]{:S(2)}) %collective-permute-start.1) | collective-permute-done | bytes 131104 | tf_op jit(solution)/shard_map/ppermute | solution.py:278
  21.7 1.8 %shard_map.76 = (bf16[1536,256]{1,0:T(8,128)(2,1)S(1)}, f32[256,128]{1,0:T(8,128)S(1)}, f32[256,128]{1,0:T(8,128)S(1)}, f32[8,128]{1,0:T(8,128)S(1)}) custom-call(s32[4,12]{1,0:T(4,128)} %bitcast.12, s32[1,12]{1,0:T(1,128)} %refs_1_.5, f32[12,4,128,128]{3,2,1,0:T(8,128)S(1)} %get-tuple-element.59.ops_ref.refs_2_, ...), custom_call_target="tpu_custom_call" | custom-call | flops 603979776 | bytes 6000000 | tf_op jit(solution)/shard_map/pallas_call | solution.py:310
  23.6 1.5 %shard_map.79 = (bf16[384,1536]{1,0:T(8,128)(2,1)S(1)}, f32[384,128]{1,0:T(8,128)S(1)}, f32[384,128]{1,0:T(8,128)S(1)}) custom-call(s32[12,128]{1,0:T(8,128)} %bitcast.17, bf16[1536,256]{1,0:T(8,128)(2,1)S(1)} %get-tuple-element.60.own_ref.refs_1_, ...), custom_call_target="tpu_custom_call", output_to_operand_aliasing={{0}: (3, {}), {1}: (4, {}), {2}: (5, {})} | custom-call | flops 301989888 | bytes 3000000 | tf_op jit(solution)/shard_map/pallas_call | solution.py:96
  25.1 0.7 collective-permute-start.4
  25.8 3.6 %collective-permute-start.2 = (f32[256,128]{1,0:T(8,128)S(1)}, f32[256,128]{1,0:T(8,128)S(1)}, u32[]{:S(2)}, u32[]{:S(2)}) collective-permute-start(f32[256,128]{1,0:T(8,128)S(1)} %get-tuple-element.66), channel_id=1, source_target_pairs={{0,63},{1,2},{2,1},{3,4},{4,3},{5,6},{6,5},{7,8},{8,7},{9,10},{10,... | collective-permute-start | bytes 393224 | tf_op jit(solution)/shard_map/ppermute | solution.py:277
  29.4 1.9 %collective-permute-start.3 = (f32[256,128]{1,0:T(8,128)S(1)}, f32[256,128]{1,0:T(8,128)S(1)}, u32[]{:S(2)}, u32[]{:S(2)}) collective-permute-start(f32[256,128]{1,0:T(8,128)S(1)} %get-tuple-element.67), channel_id=1, source_target_pairs={{0,1},{1,0},{2,3},{3,2},{4,5},{5,4},{6,7},{7,6},{8,9},{9,8},{10,11... | collective-permute-start | bytes 393224 | tf_op jit(solution)/shard_map/ppermute | solution.py:278
  31.3 1.9 %collective-permute-start.8 = (f32[384,128]{1,0:T(8,128)S(1)}, f32[384,128]{1,0:T(8,128)S(1)}, u32[]{:S(2)}, u32[]{:S(2)}) collective-permute-start(f32[384,128]{1,0:T(8,128)S(1)} %get-tuple-element.73), channel_id=1, source_target_pairs={{128,64},{192,128},{256,192},{320,256},{384,320},{448,384},{129,65... | collective-permute-start | bytes 589832 | tf_op jit(solution)/shard_map/ppermute | solution.py:320
  33.2 2.7 %collective-permute-done.2.refs_4_ = f32[256,128]{1,0:T(8,128)S(1)} collective-permute-done((f32[256,128]{1,0:T(8,128)S(1)}, f32[256,128]{1,0:T(8,128)S(1)}, u32[]{:S(2)}, u32[]{:S(2)}) %collective-permute-start.2) | collective-permute-done | bytes 131104 | tf_op jit(solution)/shard_map/ppermute | solution.py:277
  36.0 0.3 collective-permute-done.3.refs_5_
  36.3 0.7 collective-permute-start.6
  36.9 0.7 collective-permute-start.5
  37.6 0.7 collective-permute-start.7
  38.3 1.4 %shard_map.77.coarse2_ref = bf16[768,768]{1,0:T(8,128)(2,1)S(1)} custom-call(f32[384,768]{1,0:T(8,128)} %coarse_hbm.1, f32[8,128]{1,0:T(8,128)S(1)} %get-tuple-element.64.token_ref.refs_2_), custom_call_target="tpu_custom_call" | custom-call | bytes 4000000 | tf_op jit(solution)/shard_map/pallas_call | solution.py:346
  39.7 0.1 shard_map.81
  39.8 0.6 shard_map.82
  40.4 0.7 collective-permute-start.10
  41.1 0.7 collective-permute-start.11
  41.7 0.7 collective-permute-start.9
  42.4 2.5 %shard_map.83 = (f32[1536,128]{1,0:T(8,128)S(1)}, f32[384,128]{1,0:T(8,128)S(1)}, bf16[1536,384]{1,0:T(8,128)(2,1)S(1)}) custom-call(s32[4,12]{1,0:T(4,128)} %bitcast.15, s32[1,12]{1,0:T(1,128)} %refs_1_.5, f32[12,4,128,128]{3,2,1,0:T(8,128)S(1)} %get-tuple-element.59.ops_ref.refs_2_, ...), custom_call_target="tpu_custom_call", output_to_operand_aliasing={{0}: (9, {})} | custom-call | flops 905969664 | bytes 8000000 | tf_op jit(solution)/shard_map/pallas_call | solution.py:351
  44.9 0.6 shard_map.84
  45.5 0.7 collective-permute-start.13
  46.2 0.7 collective-permute-start.12
  46.8 0.7 collective-permute-start.14
  47.5 0.6 shard_map.85
  48.1 0.7 collective-permute-start.16
  48.8 0.7 collective-permute-start.15
  49.4 0.7 collective-permute-start.17
  50.1 0.6 shard_map.86
  50.7 0.7 collective-permute-start.19
  51.4 0.7 collective-permute-start.18
  52.1 0.7 collective-permute-start.20
  52.8 0.6 shard_map.87
  53.3 1.3 %collective-permute-start.22 = (f32[384,128]{1,0:T(8,128)S(1)}, f32[384,128]{1,0:T(8,128)S(1)}, u32[]{:S(2)}, u32[]{:S(2)}) collective-permute-start(f32[384,128]{1,0:T(8,128)S(1)} %get-tuple-element.98), channel_id=1, source_target_pairs={{320,384},{321,385},{322,386},{323,387},{324,388},{325,389},{326,3... | collective-permute-start | bytes 589832 | tf_op jit(solution)/shard_map/ppermute | solution.py:332
  54.6 1.3 %collective-permute-start.21 = (f32[192,128]{1,0:T(8,128)S(1)}, f32[192,128]{1,0:T(8,128)S(1)}, u32[]{:S(2)}, u32[]{:S(2)}) collective-permute-start(f32[192,128]{1,0:T(8,128)S(1)} %get-tuple-element.97), channel_id=1, source_target_pairs={{320,447},{321,386},{322,385},{323,388},{324,387},{325,390},{326,3... | collective-permute-start | bytes 294920 | tf_op jit(solution)/shard_map/ppermute | solution.py:332
  55.9 1.3 %collective-permute-start.23 = (f32[192,128]{1,0:T(8,128)S(1)}, f32[192,128]{1,0:T(8,128)S(1)}, u32[]{:S(2)}, u32[]{:S(2)}) collective-permute-start(f32[192,128]{1,0:T(8,128)S(1)} %get-tuple-element.99), channel_id=1, source_target_pairs={{320,385},{321,384},{322,387},{323,386},{324,389},{325,388},{326,3... | collective-permute-start | bytes 294920 | tf_op jit(solution)/shard_map/ppermute | solution.py:332
  57.2 33.6 %collective-permute-done.21.far_ref = f32[192,128]{1,0:T(8,128)S(1)} collective-permute-done((f32[192,128]{1,0:T(8,128)S(1)}, f32[192,128]{1,0:T(8,128)S(1)}, u32[]{:S(2)}, u32[]{:S(2)}) %collective-permute-start.21) | collective-permute-done | bytes 98336 | tf_op jit(solution)/shard_map/ppermute | solution.py:332
  90.9 0.5 shard_map.88
  91.4 1.3 %collective-permute-start.25 = (f32[384,128]{1,0:T(8,128)S(1)}, f32[384,128]{1,0:T(8,128)S(1)}, u32[]{:S(2)}, u32[]{:S(2)}) collective-permute-start(f32[384,128]{1,0:T(8,128)S(1)} %get-tuple-element.102), channel_id=1, source_target_pairs={{384,448},{385,449},{386,450},{387,451},{388,452},{389,453},{390,4... | collective-permute-start | bytes 589832 | tf_op jit(solution)/shard_map/ppermute | solution.py:332
  92.7 1.3 %collective-permute-start.24 = (f32[192,128]{1,0:T(8,128)S(1)}, f32[192,128]{1,0:T(8,128)S(1)}, u32[]{:S(2)}, u32[]{:S(2)}) collective-permute-start(f32[192,128]{1,0:T(8,128)S(1)} %get-tuple-element.101), channel_id=1, source_target_pairs={{384,511},{385,450},{386,449},{387,452},{388,451},{389,454},{390,4... | collective-permute-start | bytes 294920 | tf_op jit(solution)/shard_map/ppermute | solution.py:332
  94.0 1.3 %collective-permute-start.26 = (f32[192,128]{1,0:T(8,128)S(1)}, f32[192,128]{1,0:T(8,128)S(1)}, u32[]{:S(2)}, u32[]{:S(2)}) collective-permute-start(f32[192,128]{1,0:T(8,128)S(1)} %get-tuple-element.103), channel_id=1, source_target_pairs={{384,449},{385,448},{386,451},{387,450},{388,453},{389,452},{390,4... | collective-permute-start | bytes 294920 | tf_op jit(solution)/shard_map/ppermute | solution.py:332
  95.3 0.9 collective-permute-done.24.far_ref
  96.2 1.3 %collective-permute-done.26.near_ref = f32[192,128]{1,0:T(8,128)S(1)} collective-permute-done((f32[192,128]{1,0:T(8,128)S(1)}, f32[192,128]{1,0:T(8,128)S(1)}, u32[]{:S(2)}, u32[]{:S(2)}) %collective-permute-start.26) | collective-permute-done | bytes 98336 | tf_op jit(solution)/shard_map/ppermute | solution.py:332
  97.5 1.8 %shard_map.89 = f32[1536,128]{1,0:T(8,128)} custom-call(bf16[768,768]{1,0:T(8,128)(2,1)S(1)} %shard_map.77.coarse2_ref, f32[192,128]{1,0:T(8,128)S(1)} %collective-permute-done.24.far_ref, f32[384,128]{1,0:T(8,128)S(1)} %collective-permute-done.25.own_ref, f32[192,128]{1,0:T(8,128)S(1)} %collective-permute-done.26.near_ref, ...), custom_call_target="tpu_custom_call" | custom-call | flops 528482304 | bytes 4000000 | tf_op jit(solution)/shard_map/pallas_call | solution.py:361
  (23 shorter events, 0.1 us)
Async XLA Ops:
  1.0 18.2 %collective-permute-start = (f32[256,128]{1,0:T(8,128)S(1)}, f32[256,128]{1,0:T(8,128)S(1)}, u32[]{:S(2)}, u32[]{:S(2)}) collective-permute-start(f32[256,128]{1,0:T(8,128)S(1)} %get-tuple-element.61), channel_id=1, source_target_pairs={{0,63},{1,2},{2,1},{3,4},{4,3},{5,6},{6,5},{7,8},{8,7},{9,10},{10,... | collective-permute-start | bytes 393224 | tf_op jit(solution)/shard_map/ppermute | solution.py:277
  14.9 6.9 %collective-permute-start.1 = (f32[256,128]{1,0:T(8,128)S(1)}, f32[256,128]{1,0:T(8,128)S(1)}, u32[]{:S(2)}, u32[]{:S(2)}) collective-permute-start(f32[256,128]{1,0:T(8,128)S(1)} %get-tuple-element.62), channel_id=1, source_target_pairs={{0,1},{1,0},{2,3},{3,2},{4,5},{5,4},{6,7},{7,6},{8,9},{9,8},{10,11... | collective-permute-start | bytes 393224 | tf_op jit(solution)/shard_map/ppermute | solution.py:278
  25.1 11.1 %collective-permute-start.4 = (f32[384,128]{1,0:T(8,128)S(1)}, f32[384,128]{1,0:T(8,128)S(1)}, u32[]{:S(2)}, u32[]{:S(2)}) collective-permute-start(f32[384,128]{1,0:T(8,128)S(1)} %get-tuple-element.73), channel_id=1, source_target_pairs={{64,0},{65,1},{66,2},{67,3},{68,4},{69,5},{70,6},{71,7},{72,8},{73... | collective-permute-start | bytes 589832 | tf_op jit(solution)/shard_map/ppermute | solution.py:321
  25.8 10.2 %collective-permute-start.2 = (f32[256,128]{1,0:T(8,128)S(1)}, f32[256,128]{1,0:T(8,128)S(1)}, u32[]{:S(2)}, u32[]{:S(2)}) collective-permute-start(f32[256,128]{1,0:T(8,128)S(1)} %get-tuple-element.66), channel_id=1, source_target_pairs={{0,63},{1,2},{2,1},{3,4},{4,3},{5,6},{6,5},{7,8},{8,7},{9,10},{10,... | collective-permute-start | bytes 393224 | tf_op jit(solution)/shard_map/ppermute | solution.py:277
  29.4 6.9 %collective-permute-start.3 = (f32[256,128]{1,0:T(8,128)S(1)}, f32[256,128]{1,0:T(8,128)S(1)}, u32[]{:S(2)}, u32[]{:S(2)}) collective-permute-start(f32[256,128]{1,0:T(8,128)S(1)} %get-tuple-element.67), channel_id=1, source_target_pairs={{0,1},{1,0},{2,3},{3,2},{4,5},{5,4},{6,7},{7,6},{8,9},{9,8},{10,11... | collective-permute-start | bytes 393224 | tf_op jit(solution)/shard_map/ppermute | solution.py:278
  31.3 8.5 %collective-permute-start.8 = (f32[384,128]{1,0:T(8,128)S(1)}, f32[384,128]{1,0:T(8,128)S(1)}, u32[]{:S(2)}, u32[]{:S(2)}) collective-permute-start(f32[384,128]{1,0:T(8,128)S(1)} %get-tuple-element.73), channel_id=1, source_target_pairs={{128,64},{192,128},{256,192},{320,256},{384,320},{448,384},{129,65... | collective-permute-start | bytes 589832 | tf_op jit(solution)/shard_map/ppermute | solution.py:320
  36.3 3.6 %collective-permute-start.6 = (f32[384,128]{1,0:T(8,128)S(1)}, f32[384,128]{1,0:T(8,128)S(1)}, u32[]{:S(2)}, u32[]{:S(2)}) collective-permute-start(f32[384,128]{1,0:T(8,128)S(1)} %get-tuple-element.75), channel_id=1, source_target_pairs={{0,64},{1,65},{2,66},{3,67},{4,68},{5,69},{6,70},{7,71},{8,72},{9,... | collective-permute-start | bytes 589832 | tf_op jit(solution)/shard_map/ppermute | solution.py:332
  36.9 2.9 %collective-permute-start.5 = (f32[192,128]{1,0:T(8,128)S(1)}, f32[192,128]{1,0:T(8,128)S(1)}, u32[]{:S(2)}, u32[]{:S(2)}) collective-permute-start(f32[192,128]{1,0:T(8,128)S(1)} %get-tuple-element.74), channel_id=1, source_target_pairs={{0,127},{1,66},{2,65},{3,68},{4,67},{5,70},{6,69},{7,72},{8,71},{9... | collective-permute-start | bytes 294920 | tf_op jit(solution)/shard_map/ppermute | solution.py:332
  37.6 2.2 %collective-permute-start.7 = (f32[192,128]{1,0:T(8,128)S(1)}, f32[192,128]{1,0:T(8,128)S(1)}, u32[]{:S(2)}, u32[]{:S(2)}) collective-permute-start(f32[192,128]{1,0:T(8,128)S(1)} %get-tuple-element.76), channel_id=1, source_target_pairs={{0,65},{1,64},{2,67},{3,66},{4,69},{5,68},{6,71},{7,70},{8,73},{9,... | collective-permute-start | bytes 294920 | tf_op jit(solution)/shard_map/ppermute | solution.py:332
  40.4 4.5 %collective-permute-start.10 = (f32[384,128]{1,0:T(8,128)S(1)}, f32[384,128]{1,0:T(8,128)S(1)}, u32[]{:S(2)}, u32[]{:S(2)}) collective-permute-start(f32[384,128]{1,0:T(8,128)S(1)} %get-tuple-element.80), channel_id=1, source_target_pairs={{64,128},{65,129},{66,130},{67,131},{68,132},{69,133},{70,134},{71... | collective-permute-start | bytes 589832 | tf_op jit(solution)/shard_map/ppermute | solution.py:332
  41.1 3.8 %collective-permute-start.11 = (f32[192,128]{1,0:T(8,128)S(1)}, f32[192,128]{1,0:T(8,128)S(1)}, u32[]{:S(2)}, u32[]{:S(2)}) collective-permute-start(f32[192,128]{1,0:T(8,128)S(1)} %get-tuple-element.81), channel_id=1, source_target_pairs={{64,129},{65,128},{66,131},{67,130},{68,133},{69,132},{70,135},{71... | collective-permute-start | bytes 294920 | tf_op jit(solution)/shard_map/ppermute | solution.py:332
  41.7 3.2 %collective-permute-start.9 = (f32[192,128]{1,0:T(8,128)S(1)}, f32[192,128]{1,0:T(8,128)S(1)}, u32[]{:S(2)}, u32[]{:S(2)}) collective-permute-start(f32[192,128]{1,0:T(8,128)S(1)} %get-tuple-element.79), channel_id=1, source_target_pairs={{64,191},{65,130},{66,129},{67,132},{68,131},{69,134},{70,133},{71... | collective-permute-start | bytes 294920 | tf_op jit(solution)/shard_map/ppermute | solution.py:332
  45.5 2.1 %collective-permute-start.13 = (f32[384,128]{1,0:T(8,128)S(1)}, f32[384,128]{1,0:T(8,128)S(1)}, u32[]{:S(2)}, u32[]{:S(2)}) collective-permute-start(f32[384,128]{1,0:T(8,128)S(1)} %get-tuple-element.86), channel_id=1, source_target_pairs={{128,192},{129,193},{130,194},{131,195},{132,196},{133,197},{134,1... | collective-permute-start | bytes 589832 | tf_op jit(solution)/shard_map/ppermute | solution.py:332
  46.2 1.4 %collective-permute-start.12 = (f32[192,128]{1,0:T(8,128)S(1)}, f32[192,128]{1,0:T(8,128)S(1)}, u32[]{:S(2)}, u32[]{:S(2)}) collective-permute-start(f32[192,128]{1,0:T(8,128)S(1)} %get-tuple-element.85), channel_id=1, source_target_pairs={{128,255},{129,194},{130,193},{131,196},{132,195},{133,198},{134,1... | collective-permute-start | bytes 294920 | tf_op jit(solution)/shard_map/ppermute | solution.py:332
  46.8 0.7 collective-permute-start.14
  48.1 2.1 %collective-permute-start.16 = (f32[384,128]{1,0:T(8,128)S(1)}, f32[384,128]{1,0:T(8,128)S(1)}, u32[]{:S(2)}, u32[]{:S(2)}) collective-permute-start(f32[384,128]{1,0:T(8,128)S(1)} %get-tuple-element.90), channel_id=1, source_target_pairs={{192,256},{193,257},{194,258},{195,259},{196,260},{197,261},{198,2... | collective-permute-start | bytes 589832 | tf_op jit(solution)/shard_map/ppermute | solution.py:332
  48.8 1.4 %collective-permute-start.15 = (f32[192,128]{1,0:T(8,128)S(1)}, f32[192,128]{1,0:T(8,128)S(1)}, u32[]{:S(2)}, u32[]{:S(2)}) collective-permute-start(f32[192,128]{1,0:T(8,128)S(1)} %get-tuple-element.89), channel_id=1, source_target_pairs={{192,319},{193,258},{194,257},{195,260},{196,259},{197,262},{198,2... | collective-permute-start | bytes 294920 | tf_op jit(solution)/shard_map/ppermute | solution.py:332
  49.4 0.7 collective-permute-start.17
  50.7 2.1 %collective-permute-start.19 = (f32[384,128]{1,0:T(8,128)S(1)}, f32[384,128]{1,0:T(8,128)S(1)}, u32[]{:S(2)}, u32[]{:S(2)}) collective-permute-start(f32[384,128]{1,0:T(8,128)S(1)} %get-tuple-element.94), channel_id=1, source_target_pairs={{256,320},{257,321},{258,322},{259,323},{260,324},{261,325},{262,3... | collective-permute-start | bytes 589832 | tf_op jit(solution)/shard_map/ppermute | solution.py:332
  51.4 1.4 %collective-permute-start.18 = (f32[192,128]{1,0:T(8,128)S(1)}, f32[192,128]{1,0:T(8,128)S(1)}, u32[]{:S(2)}, u32[]{:S(2)}) collective-permute-start(f32[192,128]{1,0:T(8,128)S(1)} %get-tuple-element.93), channel_id=1, source_target_pairs={{256,383},{257,322},{258,321},{259,324},{260,323},{261,326},{262,3... | collective-permute-start | bytes 294920 | tf_op jit(solution)/shard_map/ppermute | solution.py:332
  52.1 0.7 collective-permute-start.20
  53.3 37.5 %collective-permute-start.22 = (f32[384,128]{1,0:T(8,128)S(1)}, f32[384,128]{1,0:T(8,128)S(1)}, u32[]{:S(2)}, u32[]{:S(2)}) collective-permute-start(f32[384,128]{1,0:T(8,128)S(1)} %get-tuple-element.98), channel_id=1, source_target_pairs={{320,384},{321,385},{322,386},{323,387},{324,388},{325,389},{326,3... | collective-permute-start | bytes 589832 | tf_op jit(solution)/shard_map/ppermute | solution.py:332
  54.6 36.2 %collective-permute-start.21 = (f32[192,128]{1,0:T(8,128)S(1)}, f32[192,128]{1,0:T(8,128)S(1)}, u32[]{:S(2)}, u32[]{:S(2)}) collective-permute-start(f32[192,128]{1,0:T(8,128)S(1)} %get-tuple-element.97), channel_id=1, source_target_pairs={{320,447},{321,386},{322,385},{323,388},{324,387},{325,390},{326,3... | collective-permute-start | bytes 294920 | tf_op jit(solution)/shard_map/ppermute | solution.py:332
  55.9 34.9 %collective-permute-start.23 = (f32[192,128]{1,0:T(8,128)S(1)}, f32[192,128]{1,0:T(8,128)S(1)}, u32[]{:S(2)}, u32[]{:S(2)}) collective-permute-start(f32[192,128]{1,0:T(8,128)S(1)} %get-tuple-element.99), channel_id=1, source_target_pairs={{320,385},{321,384},{322,387},{323,386},{324,389},{325,388},{326,3... | collective-permute-start | bytes 294920 | tf_op jit(solution)/shard_map/ppermute | solution.py:332
  91.4 6.1 %collective-permute-start.25 = (f32[384,128]{1,0:T(8,128)S(1)}, f32[384,128]{1,0:T(8,128)S(1)}, u32[]{:S(2)}, u32[]{:S(2)}) collective-permute-start(f32[384,128]{1,0:T(8,128)S(1)} %get-tuple-element.102), channel_id=1, source_target_pairs={{384,448},{385,449},{386,450},{387,451},{388,452},{389,453},{390,4... | collective-permute-start | bytes 589832 | tf_op jit(solution)/shard_map/ppermute | solution.py:332
  92.7 3.5 %collective-permute-start.24 = (f32[192,128]{1,0:T(8,128)S(1)}, f32[192,128]{1,0:T(8,128)S(1)}, u32[]{:S(2)}, u32[]{:S(2)}) collective-permute-start(f32[192,128]{1,0:T(8,128)S(1)} %get-tuple-element.101), channel_id=1, source_target_pairs={{384,511},{385,450},{386,449},{387,452},{388,451},{389,454},{390,4... | collective-permute-start | bytes 294920 | tf_op jit(solution)/shard_map/ppermute | solution.py:332
  94.0 3.5 %collective-permute-start.26 = (f32[192,128]{1,0:T(8,128)S(1)}, f32[192,128]{1,0:T(8,128)S(1)}, u32[]{:S(2)}, u32[]{:S(2)}) collective-permute-start(f32[192,128]{1,0:T(8,128)S(1)} %get-tuple-element.103), channel_id=1, source_target_pairs={{384,449},{385,448},{386,451},{387,450},{388,453},{389,452},{390,4... | collective-permute-start | bytes 294920 | tf_op jit(solution)/shard_map/ppermute | solution.py:332

commit v3 on v1

--- a/solution.py
+++ b/solution.py
@@ -7,6 +7,7 @@
 
 
 HALO = 256
+PLANE = 16
 BS = 128
 F32 = jnp.float32
 BF16 = jnp.bfloat16
@@ -155,8 +156,8 @@
     near_ref[...] = block[pl.ds(pl.multiple_of((1 - odd) * last, 64), width), :]
 
 
-def first_step(cols_hbm, live_hbm, ops_ref, own_ref, far_ref, near_ref, sources_ref,
-               next_ref, nfar_ref, nnear_ref, token_ref, cols_ref, live_ref, window, sems, rims):
+def first_step(cols_hbm, live_hbm, ops_ref, own_ref, far_ref, near_ref, sources_ref, last_ref,
+               next_ref, nfar_ref, nnear_ref, token_ref, cols_ref, live_ref, window, sems, rims, whole):
     blocks = ops_ref.shape[0]
     side = HALO // BS
 
@@ -168,7 +169,8 @@
             at = b - blocks + 2 * side
             rims[at * BS:(at + 1) * BS, :] = value
 
-    transport(cols_hbm, live_hbm, ops_ref, own_ref, far_ref, near_ref, sources_ref,
+    whole[...] = near_ref[...] + last_ref[...]
+    transport(cols_hbm, live_hbm, ops_ref, own_ref, far_ref, whole, sources_ref,
               cols_ref, live_ref, window, sems, emit)
     sides(rims, nfar_ref, nnear_ref, HALO)
     token_ref[...] = jnp.zeros_like(token_ref)
@@ -215,12 +217,16 @@
         spread_ref[b * BS:(b + 1) * BS, :] = gather_ref[:, b * BS:(b + 1) * BS].astype(F32).T.astype(BF16)
 
 
-def coarse_product(coarse2_ref, far_ref, own_ref, near_ref, window):
+def fill(far_ref, own_ref, near_ref, window):
     rim, rows = far_ref.shape[0], own_ref.shape[0]
     odd = odd_tile()
     window[pl.ds(pl.multiple_of(odd * (rim + rows), 64), rim), :] = pair(far_ref[...])
     window[pl.ds(pl.multiple_of((1 - odd) * (rim + rows), 64), rim), :] = pair(near_ref[...])
     window[rim:rim + rows, :] = pair(own_ref[...])
+
+
+def coarse_product(coarse2_ref, far_ref, own_ref, near_ref, window):
+    fill(far_ref, own_ref, near_ref, window)
     return folded_twice(dot(coarse2_ref[...], window[...]))
 
 
@@ -233,7 +239,10 @@
 
 
 def finish(coarse2_ref, far_ref, own_ref, near_ref, image_ref, spread_ref, end_ref, out_hbm, window, held, sems):
-    image = image_ref[...] + coarse_product(coarse2_ref, far_ref, own_ref, near_ref, window)
+    fill(far_ref, own_ref, near_ref, window)
+    rows, tracers = own_ref.shape
+    image = folded(dot(coarse2_ref[:rows, :], window[...]))
+    image = image_ref[...] + image + dot(coarse2_ref[rows:, :], window[:, :tracers])
     split = pair(image)
     copies = []
     for b in range(sems.shape[0]):
@@ -251,6 +260,15 @@
     far = lax.ppermute(far, "tile", [(i, (i + 1 if i % 2 else i - 1) % count) for i in range(count)])
     near = lax.ppermute(near, "tile", [(i, i ^ 1) for i in range(count)])
     return far, near
+
+
+def swapped_early(far, near):
+    count = lax.axis_size("tile")
+    last = [i for i in range(count) if i % PLANE >= PLANE - 2]
+    first = lax.ppermute(near, "tile", [(i, i ^ 1) for i in range(count) if i not in last])
+    far = lax.ppermute(far, "tile", [(i, (i + 1 if i % 2 else i - 1) % count) for i in range(count)])
+    second = lax.ppermute(near, "tile", [(i, i ^ 1) for i in last])
+    return far, first, second
 
 
 def on_device(starts, sources, fine_ops, col_index, live_count, coarse_op, cell_map):
@@ -272,7 +290,7 @@
     coarse_all = ((coarse, tracers), F32)
 
     far, near = call(ends, [side, side], [HBM], 0, 500_000, [pltpu.SemaphoreType.DMA((2,))])(kept(first_state))
-    far, near = swapped(far, near)
+    far, near, last = swapped_early(far, near)
     ops, own, sources = call(
         fetch, [(ops.shape, F32), ((rows, 2 * tracers), BF16), (sources.shape, F32)],
         [HBM] * 3, 0, 9_000_000, [pltpu.VMEM((rows, tracers), F32), pltpu.SemaphoreType.DMA((3,))],
@@ -283,8 +301,9 @@
                     pltpu.SemaphoreType.DMA((2,))]
     state, far, near, token = call(
         first_step, [((rows, 2 * tracers), BF16), side, side, ((8, tracers), F32)],
-        step_in, step_flops, 6_000_000, step_scratch + [pltpu.VMEM((2 * HALO, tracers), F32)],
-    )(kept(columns), kept(live), ops, own, far, near, sources)
+        step_in + [VMEM], step_flops, 6_000_000,
+        step_scratch + [pltpu.VMEM((2 * HALO, tracers), F32), pltpu.VMEM((HALO, tracers), F32)],
+    )(kept(columns), kept(live), ops, own, far, near, sources, last)
     far, near = swapped(far, near)
     gather, inverse, rstart = call(
         prepare, [((coarse, rows), BF16), coarse_all, coarse_all],

time: 100 us -> 100 us (level)
    ppermute x0 -> x3, starting transfers between devices: none -> 16.4 us  [the longest x1 13.9 us: swapped_early(): lax.ppermute(far, 'tile', [(i, (i + 1 if i % 2 else i - 1) % count) for i...]
    ppermute x2 -> x1, starting transfers between devices: 17.4 us -> 2.91 us  [swapped(): lax.ppermute(far, 'tile', [(i, (i + 1 if i % 2 else i - 1) % count) for i...]
    ppermute x2 -> x1, waiting for transfers between devices: 2.85 us -> 0.01 us  [swapped(): near = lax.ppermute(near, 'tile', [(i, i ^ 1) for i in range(count)])]
    ppermute x0 -> x3, waiting for transfers between devices: none -> 2.56 us  [the longest x1 2.56 us: swapped_early(): lax.ppermute(near, 'tile', [(i, i ^ 1) for i in range(count) if i not in...]
    ppermute x2 -> x1, starting transfers between devices: 3.84 us -> 1.92 us  [swapped(): near = lax.ppermute(near, 'tile', [(i, i ^ 1) for i in range(count)])]
    ppermute x2 -> x1, waiting for transfers between devices: 2.73 us -> 3.41 us  [swapped(): lax.ppermute(far, 'tile', [(i, (i + 1 if i % 2 else i - 1) % count) for i...]
  transfers between devices with their start and end apart: 27 -> 28, of which waited for: 6 -> 5; matrix products, arithmetic and copies ran while one was open for 0% -> 0% of each run, Pallas kernels for 6% -> 6%
where the time goes in v3:
time: 100 us; the launch traced here: 98.7 us
  starting transfers between devices  41.7 us (42%)
  waiting for transfers between devices  40.8 us (41%)
  Pallas kernels  15.8 us (16%)
    ppermute x21, waiting for transfers between devices, to_slice(): return lax.ppermute(block, ('tm', 'tile'), route)  34.8 us
    ppermute x21, starting transfers between devices, to_slice(): return lax.ppermute(block, ('tm', 'tile'), route)  17.8 us
    ppermute x1, starting transfers between devices, swapped_early(): lax.ppermute(far, 'tile', [(i, (i + 1 if i % 2 else i - 1) % count) for i...  13.9 us
    ppermute x1, waiting for transfers between devices, swapped(): lax.ppermute(far, 'tile', [(i, (i + 1 if i % 2 else i - 1) % count) for i...  3.41 us
    pallas_call x6, Pallas kernels, on_device(): call(advance, [coarse_all, coarse_rim, coarse_rim, coarse_all], [VMEM] *...  3.34 us
    ppermute x1, starting transfers between devices, swapped(): lax.ppermute(far, 'tile', [(i, (i + 1 if i % 2 else i - 1) % count) for i...  2.91 us
    ppermute x1, waiting for transfers between devices, swapped_early(): lax.ppermute(near, 'tile', [(i, i ^ 1) for i in range(count) if i not in...  2.56 us
    pallas_call x1, Pallas kernels, on_device(): call(second_step_others, [((rows, tracers), F32), coarse_all, ((rows, coa...  2.47 us
  transfers between devices with their start and end apart: 28, of which 5 were waited for; matrix products, arithmetic and copies ran while one was open for 0% of the time, Pallas kernels for 6%

profile of v3, /device:TPU:6, one launch (start us, length us, event | category | flops | bytes accessed | tf_op | source)
XLA Modules:
  0.0 98.7 jit_solution(12197868912198310290)
XLA Ops:
  0.0 1.0 shard_map.74
  1.0 13.9 %collective-permute-start = (f32[256,128]{1,0:T(8,128)S(1)}, f32[256,128]{1,0:T(8,128)S(1)}, u32[]{:S(2)}, u32[]{:S(2)}) collective-permute-start(f32[256,128]{1,0:T(8,128)S(1)} %get-tuple-element.52), channel_id=1, source_target_pairs={{0,63},{1,2},{2,1},{3,4},{4,3},{5,6},{6,5},{7,8},{8,7},{9,10},{10,... | collective-permute-start | bytes 393224 | tf_op jit(solution)/shard_map/ppermute | solution.py:269
  14.9 0.7 collective-permute-start.2
  15.5 1.9 %collective-permute-start.1 = (f32[256,128]{1,0:T(8,128)S(1)}, f32[256,128]{1,0:T(8,128)S(1)}, u32[]{:S(2)}, u32[]{:S(2)}) collective-permute-start(f32[256,128]{1,0:T(8,128)S(1)} %get-tuple-element.53), channel_id=1, source_target_pairs={{0,1},{1,0},{2,3},{3,2},{4,5},{5,4},{6,7},{7,6},{8,9},{9,8},{10,11... | collective-permute-start | bytes 393224 | tf_op jit(solution)/shard_map/ppermute | solution.py:268
  17.5 2.3 %shard_map.73 = (f32[12,4,128,128]{3,2,1,0:T(8,128)S(1)}, bf16[1536,256]{1,0:T(8,128)(2,1)S(1)}, f32[1536,128]{1,0:T(8,128)S(1)}) custom-call(f32[12,4,128,128]{3,2,1,0:T(8,128)} %bitcast.9, f32[1536,128]{1,0:T(8,128)} %bitcast.8, f32[1536,128]{1,0:T(8,128)} %sources_ref.1), custom_call_target="tpu_custom_call" | custom-call | bytes 9000000 | tf_op jit(solution)/shard_map/pallas_call | solution.py:294
  19.8 0.0 collective-permute-done.far_ref
  19.8 2.6 %collective-permute-done.1.near_ref = f32[256,128]{1,0:T(8,128)S(1)} collective-permute-done((f32[256,128]{1,0:T(8,128)S(1)}, f32[256,128]{1,0:T(8,128)S(1)}, u32[]{:S(2)}, u32[]{:S(2)}) %collective-permute-start.1) | collective-permute-done | bytes 131104 | tf_op jit(solution)/shard_map/ppermute | solution.py:268
  22.4 1.8 %shard_map.75 = (bf16[1536,256]{1,0:T(8,128)(2,1)S(1)}, f32[256,128]{1,0:T(8,128)S(1)}, f32[256,128]{1,0:T(8,128)S(1)}, f32[8,128]{1,0:T(8,128)S(1)}) custom-call(s32[4,12]{1,0:T(4,128)} %bitcast.10, s32[1,12]{1,0:T(1,128)} %refs_1_.5, f32[12,4,128,128]{3,2,1,0:T(8,128)S(1)} %get-tuple-element.50.ops_ref.refs_2_, ...), custom_call_target="tpu_custom_call" | custom-call | flops 603979776 | bytes 6000000 | tf_op jit(solution)/shard_map/pallas_call | solution.py:302
  24.2 1.5 %shard_map.77 = (bf16[384,1536]{1,0:T(8,128)(2,1)S(1)}, f32[384,128]{1,0:T(8,128)S(1)}, f32[384,128]{1,0:T(8,128)S(1)}) custom-call(s32[12,128]{1,0:T(8,128)} %bitcast.14, bf16[1536,256]{1,0:T(8,128)(2,1)S(1)} %get-tuple-element.51.own_ref, f32[8,128]{1,0:T(8,128)S(1)} %get-tuple-element.55.token_ref), custom_call_target="tpu_custom_call" | custom-call | flops 301989888 | bytes 3000000 | tf_op jit(solution)/shard_map/pallas_call | solution.py:308
  25.7 0.7 collective-permute-start.5
  26.4 2.9 %collective-permute-start.3 = (f32[256,128]{1,0:T(8,128)S(1)}, f32[256,128]{1,0:T(8,128)S(1)}, u32[]{:S(2)}, u32[]{:S(2)}) collective-permute-start(f32[256,128]{1,0:T(8,128)S(1)} %get-tuple-element.57), channel_id=1, source_target_pairs={{0,63},{1,2},{2,1},{3,4},{4,3},{5,6},{6,5},{7,8},{8,7},{9,10},{10,... | collective-permute-start | bytes 393224 | tf_op jit(solution)/shard_map/ppermute | solution.py:260
  29.3 1.9 %collective-permute-start.4 = (f32[256,128]{1,0:T(8,128)S(1)}, f32[256,128]{1,0:T(8,128)S(1)}, u32[]{:S(2)}, u32[]{:S(2)}) collective-permute-start(f32[256,128]{1,0:T(8,128)S(1)} %get-tuple-element.58), channel_id=1, source_target_pairs={{0,1},{1,0},{2,3},{3,2},{4,5},{5,4},{6,7},{7,6},{8,9},{9,8},{10,11... | collective-permute-start | bytes 393224 | tf_op jit(solution)/shard_map/ppermute | solution.py:261
  31.3 1.9 %collective-permute-start.9 = (f32[384,128]{1,0:T(8,128)S(1)}, f32[384,128]{1,0:T(8,128)S(1)}, u32[]{:S(2)}, u32[]{:S(2)}) collective-permute-start(f32[384,128]{1,0:T(8,128)S(1)} %get-tuple-element.61), channel_id=1, source_target_pairs={{128,64},{192,128},{256,192},{320,256},{384,320},{448,384},{129,65... | collective-permute-start | bytes 589832 | tf_op jit(solution)/shard_map/ppermute | solution.py:313
  33.2 3.4 %collective-permute-done.3.refs_4_ = f32[256,128]{1,0:T(8,128)S(1)} collective-permute-done((f32[256,128]{1,0:T(8,128)S(1)}, f32[256,128]{1,0:T(8,128)S(1)}, u32[]{:S(2)}, u32[]{:S(2)}) %collective-permute-start.3) | collective-permute-done | bytes 131104 | tf_op jit(solution)/shard_map/ppermute | solution.py:260
  36.6 0.7 collective-permute-start.7
  37.3 0.7 collective-permute-start.6
  38.0 0.7 collective-permute-start.8
  38.7 1.4 %shard_map.76.coarse2_ref = bf16[768,768]{1,0:T(8,128)(2,1)S(1)} custom-call(f32[384,768]{1,0:T(8,128)} %coarse_hbm.1, f32[8,128]{1,0:T(8,128)S(1)} %get-tuple-element.55.token_ref), custom_call_target="tpu_custom_call" | custom-call | bytes 4000000 | tf_op jit(solution)/shard_map/pallas_call | solution.py:339
  40.1 0.1 shard_map.79
  40.2 0.6 shard_map.80
  40.8 0.7 collective-permute-start.11
  41.4 0.7 collective-permute-start.10
  42.1 0.7 collective-permute-start.12
  42.8 2.5 %shard_map.81 = (f32[1536,128]{1,0:T(8,128)S(1)}, f32[384,128]{1,0:T(8,128)S(1)}, bf16[1536,384]{1,0:T(8,128)(2,1)S(1)}) custom-call(s32[4,12]{1,0:T(4,128)} %bitcast.13, s32[1,12]{1,0:T(1,128)} %refs_1_.5, f32[12,4,128,128]{3,2,1,0:T(8,128)S(1)} %get-tuple-element.50.ops_ref.refs_2_, ...), custom_call_target="tpu_custom_call", output_to_operand_aliasing={{0}: (9, {})} | custom-call | flops 905969664 | bytes 8000000 | tf_op jit(solution)/shard_map/pallas_call | solution.py:344
  45.3 0.6 shard_map.82
  45.9 0.7 collective-permute-start.14
  46.5 0.7 collective-permute-start.13
  47.2 0.7 collective-permute-start.15
  47.9 0.6 shard_map.83
  48.5 0.7 collective-permute-start.17
  49.2 0.7 collective-permute-start.16
  49.8 0.7 collective-permute-start.18
  50.5 0.6 shard_map.84
  51.1 0.7 collective-permute-start.20
  51.8 0.7 collective-permute-start.19
  52.5 0.7 collective-permute-start.21
  53.2 0.6 shard_map.85
  53.7 1.3 %collective-permute-start.23 = (f32[384,128]{1,0:T(8,128)S(1)}, f32[384,128]{1,0:T(8,128)S(1)}, u32[]{:S(2)}, u32[]{:S(2)}) collective-permute-start(f32[384,128]{1,0:T(8,128)S(1)} %get-tuple-element.86), channel_id=1, source_target_pairs={{320,384},{321,385},{322,386},{323,387},{324,388},{325,389},{326,3... | collective-permute-start | bytes 589832 | tf_op jit(solution)/shard_map/ppermute | solution.py:325
  55.0 1.3 %collective-permute-start.22 = (f32[192,128]{1,0:T(8,128)S(1)}, f32[192,128]{1,0:T(8,128)S(1)}, u32[]{:S(2)}, u32[]{:S(2)}) collective-permute-start(f32[192,128]{1,0:T(8,128)S(1)} %get-tuple-element.85), channel_id=1, source_target_pairs={{320,447},{321,386},{322,385},{323,388},{324,387},{325,390},{326,3... | collective-permute-start | bytes 294920 | tf_op jit(solution)/shard_map/ppermute | solution.py:325
  56.3 1.3 %collective-permute-start.24 = (f32[192,128]{1,0:T(8,128)S(1)}, f32[192,128]{1,0:T(8,128)S(1)}, u32[]{:S(2)}, u32[]{:S(2)}) collective-permute-start(f32[192,128]{1,0:T(8,128)S(1)} %get-tuple-element.87), channel_id=1, source_target_pairs={{320,385},{321,384},{322,387},{323,386},{324,389},{325,388},{326,3... | collective-permute-start | bytes 294920 | tf_op jit(solution)/shard_map/ppermute | solution.py:325
  57.6 32.6 %collective-permute-done.22.far_ref = f32[192,128]{1,0:T(8,128)S(1)} collective-permute-done((f32[192,128]{1,0:T(8,128)S(1)}, f32[192,128]{1,0:T(8,128)S(1)}, u32[]{:S(2)}, u32[]{:S(2)}) %collective-permute-start.22) | collective-permute-done | bytes 98336 | tf_op jit(solution)/shard_map/ppermute | solution.py:325
  90.2 0.6 shard_map.86
  90.8 1.3 %collective-permute-start.26 = (f32[384,128]{1,0:T(8,128)S(1)}, f32[384,128]{1,0:T(8,128)S(1)}, u32[]{:S(2)}, u32[]{:S(2)}) collective-permute-start(f32[384,128]{1,0:T(8,128)S(1)} %get-tuple-element.90), channel_id=1, source_target_pairs={{384,448},{385,449},{386,450},{387,451},{388,452},{389,453},{390,4... | collective-permute-start | bytes 589832 | tf_op jit(solution)/shard_map/ppermute | solution.py:325
  92.1 1.3 %collective-permute-start.25 = (f32[192,128]{1,0:T(8,128)S(1)}, f32[192,128]{1,0:T(8,128)S(1)}, u32[]{:S(2)}, u32[]{:S(2)}) collective-permute-start(f32[192,128]{1,0:T(8,128)S(1)} %get-tuple-element.89), channel_id=1, source_target_pairs={{384,511},{385,450},{386,449},{387,452},{388,451},{389,454},{390,4... | collective-permute-start | bytes 294920 | tf_op jit(solution)/shard_map/ppermute | solution.py:325
  93.4 1.3 %collective-permute-start.27 = (f32[192,128]{1,0:T(8,128)S(1)}, f32[192,128]{1,0:T(8,128)S(1)}, u32[]{:S(2)}, u32[]{:S(2)}) collective-permute-start(f32[192,128]{1,0:T(8,128)S(1)} %get-tuple-element.91), channel_id=1, source_target_pairs={{384,449},{385,448},{386,451},{387,450},{388,453},{389,452},{390,4... | collective-permute-start | bytes 294920 | tf_op jit(solution)/shard_map/ppermute | solution.py:325
  94.7 0.9 collective-permute-done.25.far_ref
  95.6 1.3 %collective-permute-done.27.near_ref = f32[192,128]{1,0:T(8,128)S(1)} collective-permute-done((f32[192,128]{1,0:T(8,128)S(1)}, f32[192,128]{1,0:T(8,128)S(1)}, u32[]{:S(2)}, u32[]{:S(2)}) %collective-permute-start.27) | collective-permute-done | bytes 98336 | tf_op jit(solution)/shard_map/ppermute | solution.py:325
  96.9 1.8 %shard_map.87 = f32[1536,128]{1,0:T(8,128)} custom-call(bf16[768,768]{1,0:T(8,128)(2,1)S(1)} %shard_map.76.coarse2_ref, f32[192,128]{1,0:T(8,128)S(1)} %collective-permute-done.25.far_ref, f32[384,128]{1,0:T(8,128)S(1)} %collective-permute-done.26.own_ref, f32[192,128]{1,0:T(8,128)S(1)} %collective-permute-done.27.near_ref, ...), custom_call_target="tpu_custom_call" | custom-call | flops 528482304 | bytes 4000000 | tf_op jit(solution)/shard_map/pallas_call | solution.py:354
  (23 shorter events, 0.1 us)
Async XLA Ops:
  1.0 18.8 %collective-permute-start = (f32[256,128]{1,0:T(8,128)S(1)}, f32[256,128]{1,0:T(8,128)S(1)}, u32[]{:S(2)}, u32[]{:S(2)}) collective-permute-start(f32[256,128]{1,0:T(8,128)S(1)} %get-tuple-element.52), channel_id=1, source_target_pairs={{0,63},{1,2},{2,1},{3,4},{4,3},{5,6},{6,5},{7,8},{8,7},{9,10},{10,... | collective-permute-start | bytes 393224 | tf_op jit(solution)/shard_map/ppermute | solution.py:269
  14.9 5.0 %collective-permute-start.2 = (f32[256,128]{1,0:T(8,128)S(1)}, f32[256,128]{1,0:T(8,128)S(1)}, u32[]{:S(2)}, u32[]{:S(2)}) collective-permute-start(f32[256,128]{1,0:T(8,128)S(1)} %get-tuple-element.53), channel_id=1, source_target_pairs={{14,15},{15,14},{30,31},{31,30},{46,47},{47,46},{62,63},{63,62},{7... | collective-permute-start | bytes 393224 | tf_op jit(solution)/shard_map/ppermute | solution.py:270
  15.5 6.9 %collective-permute-start.1 = (f32[256,128]{1,0:T(8,128)S(1)}, f32[256,128]{1,0:T(8,128)S(1)}, u32[]{:S(2)}, u32[]{:S(2)}) collective-permute-start(f32[256,128]{1,0:T(8,128)S(1)} %get-tuple-element.53), channel_id=1, source_target_pairs={{0,1},{1,0},{2,3},{3,2},{4,5},{5,4},{6,7},{7,6},{8,9},{9,8},{10,11... | collective-permute-start | bytes 393224 | tf_op jit(solution)/shard_map/ppermute | solution.py:268
  25.7 10.9 %collective-permute-start.5 = (f32[384,128]{1,0:T(8,128)S(1)}, f32[384,128]{1,0:T(8,128)S(1)}, u32[]{:S(2)}, u32[]{:S(2)}) collective-permute-start(f32[384,128]{1,0:T(8,128)S(1)} %get-tuple-element.61), channel_id=1, source_target_pairs={{64,0},{65,1},{66,2},{67,3},{68,4},{69,5},{70,6},{71,7},{72,8},{73... | collective-permute-start | bytes 589832 | tf_op jit(solution)/shard_map/ppermute | solution.py:314
  26.4 10.2 %collective-permute-start.3 = (f32[256,128]{1,0:T(8,128)S(1)}, f32[256,128]{1,0:T(8,128)S(1)}, u32[]{:S(2)}, u32[]{:S(2)}) collective-permute-start(f32[256,128]{1,0:T(8,128)S(1)} %get-tuple-element.57), channel_id=1, source_target_pairs={{0,63},{1,2},{2,1},{3,4},{4,3},{5,6},{6,5},{7,8},{8,7},{9,10},{10,... | collective-permute-start | bytes 393224 | tf_op jit(solution)/shard_map/ppermute | solution.py:260
  29.3 7.3 %collective-permute-start.4 = (f32[256,128]{1,0:T(8,128)S(1)}, f32[256,128]{1,0:T(8,128)S(1)}, u32[]{:S(2)}, u32[]{:S(2)}) collective-permute-start(f32[256,128]{1,0:T(8,128)S(1)} %get-tuple-element.58), channel_id=1, source_target_pairs={{0,1},{1,0},{2,3},{3,2},{4,5},{5,4},{6,7},{7,6},{8,9},{9,8},{10,11... | collective-permute-start | bytes 393224 | tf_op jit(solution)/shard_map/ppermute | solution.py:261
  31.3 8.9 %collective-permute-start.9 = (f32[384,128]{1,0:T(8,128)S(1)}, f32[384,128]{1,0:T(8,128)S(1)}, u32[]{:S(2)}, u32[]{:S(2)}) collective-permute-start(f32[384,128]{1,0:T(8,128)S(1)} %get-tuple-element.61), channel_id=1, source_target_pairs={{128,64},{192,128},{256,192},{320,256},{384,320},{448,384},{129,65... | collective-permute-start | bytes 589832 | tf_op jit(solution)/shard_map/ppermute | solution.py:313
  36.6 3.6 %collective-permute-start.7 = (f32[384,128]{1,0:T(8,128)S(1)}, f32[384,128]{1,0:T(8,128)S(1)}, u32[]{:S(2)}, u32[]{:S(2)}) collective-permute-start(f32[384,128]{1,0:T(8,128)S(1)} %get-tuple-element.63), channel_id=1, source_target_pairs={{0,64},{1,65},{2,66},{3,67},{4,68},{5,69},{6,70},{7,71},{8,72},{9,... | collective-permute-start | bytes 589832 | tf_op jit(solution)/shard_map/ppermute | solution.py:325
  37.3 2.9 %collective-permute-start.6 = (f32[192,128]{1,0:T(8,128)S(1)}, f32[192,128]{1,0:T(8,128)S(1)}, u32[]{:S(2)}, u32[]{:S(2)}) collective-permute-start(f32[192,128]{1,0:T(8,128)S(1)} %get-tuple-element.62), channel_id=1, source_target_pairs={{0,127},{1,66},{2,65},{3,68},{4,67},{5,70},{6,69},{7,72},{8,71},{9... | collective-permute-start | bytes 294920 | tf_op jit(solution)/shard_map/ppermute | solution.py:325
  38.0 2.2 %collective-permute-start.8 = (f32[192,128]{1,0:T(8,128)S(1)}, f32[192,128]{1,0:T(8,128)S(1)}, u32[]{:S(2)}, u32[]{:S(2)}) collective-permute-start(f32[192,128]{1,0:T(8,128)S(1)} %get-tuple-element.64), channel_id=1, source_target_pairs={{0,65},{1,64},{2,67},{3,66},{4,69},{5,68},{6,71},{7,70},{8,73},{9,... | collective-permute-start | bytes 294920 | tf_op jit(solution)/shard_map/ppermute | solution.py:325
  40.8 4.5 %collective-permute-start.11 = (f32[384,128]{1,0:T(8,128)S(1)}, f32[384,128]{1,0:T(8,128)S(1)}, u32[]{:S(2)}, u32[]{:S(2)}) collective-permute-start(f32[384,128]{1,0:T(8,128)S(1)} %get-tuple-element.68), channel_id=1, source_target_pairs={{64,128},{65,129},{66,130},{67,131},{68,132},{69,133},{70,134},{71... | collective-permute-start | bytes 589832 | tf_op jit(solution)/shard_map/ppermute | solution.py:325
  41.4 3.8 %collective-permute-start.10 = (f32[192,128]{1,0:T(8,128)S(1)}, f32[192,128]{1,0:T(8,128)S(1)}, u32[]{:S(2)}, u32[]{:S(2)}) collective-permute-start(f32[192,128]{1,0:T(8,128)S(1)} %get-tuple-element.67), channel_id=1, source_target_pairs={{64,191},{65,130},{66,129},{67,132},{68,131},{69,134},{70,133},{71... | collective-permute-start | bytes 294920 | tf_op jit(solution)/shard_map/ppermute | solution.py:325
  42.1 3.2 %collective-permute-start.12 = (f32[192,128]{1,0:T(8,128)S(1)}, f32[192,128]{1,0:T(8,128)S(1)}, u32[]{:S(2)}, u32[]{:S(2)}) collective-permute-start(f32[192,128]{1,0:T(8,128)S(1)} %get-tuple-element.69), channel_id=1, source_target_pairs={{64,129},{65,128},{66,131},{67,130},{68,133},{69,132},{70,135},{71... | collective-permute-start | bytes 294920 | tf_op jit(solution)/shard_map/ppermute | solution.py:325
  45.9 2.1 %collective-permute-start.14 = (f32[384,128]{1,0:T(8,128)S(1)}, f32[384,128]{1,0:T(8,128)S(1)}, u32[]{:S(2)}, u32[]{:S(2)}) collective-permute-start(f32[384,128]{1,0:T(8,128)S(1)} %get-tuple-element.74), channel_id=1, source_target_pairs={{128,192},{129,193},{130,194},{131,195},{132,196},{133,197},{134,1... | collective-permute-start | bytes 589832 | tf_op jit(solution)/shard_map/ppermute | solution.py:325
  46.5 1.4 %collective-permute-start.13 = (f32[192,128]{1,0:T(8,128)S(1)}, f32[192,128]{1,0:T(8,128)S(1)}, u32[]{:S(2)}, u32[]{:S(2)}) collective-permute-start(f32[192,128]{1,0:T(8,128)S(1)} %get-tuple-element.73), channel_id=1, source_target_pairs={{128,255},{129,194},{130,193},{131,196},{132,195},{133,198},{134,1... | collective-permute-start | bytes 294920 | tf_op jit(solution)/shard_map/ppermute | solution.py:325
  47.2 0.7 collective-permute-start.15
  48.5 2.1 %collective-permute-start.17 = (f32[384,128]{1,0:T(8,128)S(1)}, f32[384,128]{1,0:T(8,128)S(1)}, u32[]{:S(2)}, u32[]{:S(2)}) collective-permute-start(f32[384,128]{1,0:T(8,128)S(1)} %get-tuple-element.78), channel_id=1, source_target_pairs={{192,256},{193,257},{194,258},{195,259},{196,260},{197,261},{198,2... | collective-permute-start | bytes 589832 | tf_op jit(solution)/shard_map/ppermute | solution.py:325
  49.2 1.4 %collective-permute-start.16 = (f32[192,128]{1,0:T(8,128)S(1)}, f32[192,128]{1,0:T(8,128)S(1)}, u32[]{:S(2)}, u32[]{:S(2)}) collective-permute-start(f32[192,128]{1,0:T(8,128)S(1)} %get-tuple-element.77), channel_id=1, source_target_pairs={{192,319},{193,258},{194,257},{195,260},{196,259},{197,262},{198,2... | collective-permute-start | bytes 294920 | tf_op jit(solution)/shard_map/ppermute | solution.py:325
  49.8 0.7 collective-permute-start.18
  51.1 2.1 %collective-permute-start.20 = (f32[384,128]{1,0:T(8,128)S(1)}, f32[384,128]{1,0:T(8,128)S(1)}, u32[]{:S(2)}, u32[]{:S(2)}) collective-permute-start(f32[384,128]{1,0:T(8,128)S(1)} %get-tuple-element.82), channel_id=1, source_target_pairs={{256,320},{257,321},{258,322},{259,323},{260,324},{261,325},{262,3... | collective-permute-start | bytes 589832 | tf_op jit(solution)/shard_map/ppermute | solution.py:325
  51.8 1.4 %collective-permute-start.19 = (f32[192,128]{1,0:T(8,128)S(1)}, f32[192,128]{1,0:T(8,128)S(1)}, u32[]{:S(2)}, u32[]{:S(2)}) collective-permute-start(f32[192,128]{1,0:T(8,128)S(1)} %get-tuple-element.81), channel_id=1, source_target_pairs={{256,383},{257,322},{258,321},{259,324},{260,323},{261,326},{262,3... | collective-permute-start | bytes 294920 | tf_op jit(solution)/shard_map/ppermute | solution.py:325
  52.5 0.7 collective-permute-start.21
  53.7 36.5 %collective-permute-start.23 = (f32[384,128]{1,0:T(8,128)S(1)}, f32[384,128]{1,0:T(8,128)S(1)}, u32[]{:S(2)}, u32[]{:S(2)}) collective-permute-start(f32[384,128]{1,0:T(8,128)S(1)} %get-tuple-element.86), channel_id=1, source_target_pairs={{320,384},{321,385},{322,386},{323,387},{324,388},{325,389},{326,3... | collective-permute-start | bytes 589832 | tf_op jit(solution)/shard_map/ppermute | solution.py:325
  55.0 35.2 %collective-permute-start.22 = (f32[192,128]{1,0:T(8,128)S(1)}, f32[192,128]{1,0:T(8,128)S(1)}, u32[]{:S(2)}, u32[]{:S(2)}) collective-permute-start(f32[192,128]{1,0:T(8,128)S(1)} %get-tuple-element.85), channel_id=1, source_target_pairs={{320,447},{321,386},{322,385},{323,388},{324,387},{325,390},{326,3... | collective-permute-start | bytes 294920 | tf_op jit(solution)/shard_map/ppermute | solution.py:325
  56.3 33.9 %collective-permute-start.24 = (f32[192,128]{1,0:T(8,128)S(1)}, f32[192,128]{1,0:T(8,128)S(1)}, u32[]{:S(2)}, u32[]{:S(2)}) collective-permute-start(f32[192,128]{1,0:T(8,128)S(1)} %get-tuple-element.87), channel_id=1, source_target_pairs={{320,385},{321,384},{322,387},{323,386},{324,389},{325,388},{326,3... | collective-permute-start | bytes 294920 | tf_op jit(solution)/shard_map/ppermute | solution.py:325
  90.8 6.1 %collective-permute-start.26 = (f32[384,128]{1,0:T(8,128)S(1)}, f32[384,128]{1,0:T(8,128)S(1)}, u32[]{:S(2)}, u32[]{:S(2)}) collective-permute-start(f32[384,128]{1,0:T(8,128)S(1)} %get-tuple-element.90), channel_id=1, source_target_pairs={{384,448},{385,449},{386,450},{387,451},{388,452},{389,453},{390,4... | collective-permute-start | bytes 589832 | tf_op jit(solution)/shard_map/ppermute | solution.py:325
  92.1 3.5 %collective-permute-start.25 = (f32[192,128]{1,0:T(8,128)S(1)}, f32[192,128]{1,0:T(8,128)S(1)}, u32[]{:S(2)}, u32[]{:S(2)}) collective-permute-start(f32[192,128]{1,0:T(8,128)S(1)} %get-tuple-element.89), channel_id=1, source_target_pairs={{384,511},{385,450},{386,449},{387,452},{388,451},{389,454},{390,4... | collective-permute-start | bytes 294920 | tf_op jit(solution)/shard_map/ppermute | solution.py:325
  93.4 3.5 %collective-permute-start.27 = (f32[192,128]{1,0:T(8,128)S(1)}, f32[192,128]{1,0:T(8,128)S(1)}, u32[]{:S(2)}, u32[]{:S(2)}) collective-permute-start(f32[192,128]{1,0:T(8,128)S(1)} %get-tuple-element.91), channel_id=1, source_target_pairs={{384,449},{385,448},{386,451},{387,450},{388,453},{389,452},{390,4... | collective-permute-start | bytes 294920 | tf_op jit(solution)/shard_map/ppermute | solution.py:325

commit v4 on v3

--- a/solution.py
+++ b/solution.py
@@ -157,7 +157,7 @@
 
 
 def first_step(cols_hbm, live_hbm, ops_ref, own_ref, far_ref, near_ref, sources_ref, last_ref,
-               next_ref, nfar_ref, nnear_ref, token_ref, cols_ref, live_ref, window, sems, rims, whole):
+               next_ref, nfar_ref, nnear_ref, cols_ref, live_ref, window, sems, rims, whole):
     blocks = ops_ref.shape[0]
     side = HALO // BS
 
@@ -173,25 +173,51 @@
     transport(cols_hbm, live_hbm, ops_ref, own_ref, far_ref, whole, sources_ref,
               cols_ref, live_ref, window, sems, emit)
     sides(rims, nfar_ref, nnear_ref, HALO)
+
+
+def late_tile():
+    return lax.rem(lax.axis_index("tile"), PLANE) == PLANE - 1
+
+
+def first_step_early(*refs):
+    @pl.when(jnp.logical_not(late_tile()))
+    def _():
+        first_step(*refs)
+
+
+def first_step_late(*refs):
+    far_ref, near_ref = refs[9:11]
+    nfar_ref, nnear_ref, token_ref = refs[12:15]
     token_ref[...] = jnp.zeros_like(token_ref)
-
-
-def restricted_step(refs, gather_ref, inverse_ref, end_ref, jump_ref, cols_ref, live_ref, window, sems, split):
+    late = late_tile()
+
+    @pl.when(jnp.logical_not(late))
+    def _():
+        nfar_ref[...] = far_ref[...]
+        nnear_ref[...] = near_ref[...]
+
+    @pl.when(late)
+    def _():
+        first_step(*refs[:8], *refs[11:14], *refs[15:])
+
+
+def restricted_step(refs, gather_ref, inverse_ref, end_ref, jump_ref, cols_ref, live_ref, window, sems, split, whole):
     def emit(b, value):
         end_ref[b * BS:(b + 1) * BS, :] = value
         split[b * BS:(b + 1) * BS, :] = pair(value)
 
-    transport(*refs, cols_ref, live_ref, window, sems, emit)
+    whole[...] = refs[4][...] + refs[7][...]
+    transport(*refs[:4], whole, *refs[5:7], cols_ref, live_ref, window, sems, emit)
     jump_ref[...] = folded(dot(gather_ref[...], split[...])) * inverse_ref[...]
 
 
 def second_step_first(*refs):
-    operands, (gather_ref, inverse_ref, following_ref) = refs[:7], refs[7:10]
-    end_ref, jump_ref, nfar_ref, nnear_ref = refs[10:14]
+    operands, (gather_ref, inverse_ref, following_ref) = refs[:8], refs[8:11]
+    end_ref, jump_ref, nfar_ref, nnear_ref = refs[11:15]
 
     @pl.when(lax.axis_index("tm") == 0)
     def _():
-        restricted_step(operands, gather_ref, inverse_ref, end_ref, jump_ref, *refs[14:])
+        restricted_step(operands, gather_ref, inverse_ref, end_ref, jump_ref, *refs[15:])
         jump_ref[...] = jump_ref[...] - following_ref[...]
         sides(jump_ref, nfar_ref, nnear_ref, nfar_ref.shape[0])
 
@@ -207,12 +233,12 @@
 
 
 def second_step_one(*refs):
-    second_step_rest(lax.axis_index("tm") == 1, refs[7], refs[8], refs[:7], refs[10], refs[11], refs[12:])
+    second_step_rest(lax.axis_index("tm") == 1, refs[8], refs[9], refs[:8], refs[11], refs[12], refs[13:])
 
 
 def second_step_others(*refs):
-    second_step_rest(lax.axis_index("tm") > 1, refs[7], refs[8], refs[:7], refs[10], refs[11], refs[13:])
-    gather_ref, spread_ref = refs[7], refs[12]
+    second_step_rest(lax.axis_index("tm") > 1, refs[8], refs[9], refs[:8], refs[11], refs[12], refs[14:])
+    gather_ref, spread_ref = refs[8], refs[13]
     for b in range(gather_ref.shape[1] // BS):
         spread_ref[b * BS:(b + 1) * BS, :] = gather_ref[:, b * BS:(b + 1) * BS].astype(F32).T.astype(BF16)
 
@@ -255,19 +281,12 @@
         copy.wait()
 
 
-def swapped(far, near):
+def swapped_first(far, near):
     count = lax.axis_size("tile")
+    early = [i for i in range(count) if i % PLANE < 2]
+    first = lax.ppermute(near, "tile", [(i, i ^ 1) for i in early])
     far = lax.ppermute(far, "tile", [(i, (i + 1 if i % 2 else i - 1) % count) for i in range(count)])
-    near = lax.ppermute(near, "tile", [(i, i ^ 1) for i in range(count)])
-    return far, near
-
-
-def swapped_early(far, near):
-    count = lax.axis_size("tile")
-    last = [i for i in range(count) if i % PLANE >= PLANE - 2]
-    first = lax.ppermute(near, "tile", [(i, i ^ 1) for i in range(count) if i not in last])
-    far = lax.ppermute(far, "tile", [(i, (i + 1 if i % 2 else i - 1) % count) for i in range(count)])
-    second = lax.ppermute(near, "tile", [(i, i ^ 1) for i in last])
+    second = lax.ppermute(near, "tile", [(i, i ^ 1) for i in range(count) if i not in early])
     return far, first, second
 
 
@@ -290,7 +309,7 @@
     coarse_all = ((coarse, tracers), F32)
 
     far, near = call(ends, [side, side], [HBM], 0, 500_000, [pltpu.SemaphoreType.DMA((2,))])(kept(first_state))
-    far, near, last = swapped_early(far, near)
+    far, near, last = swapped_first(far, near)
     ops, own, sources = call(
         fetch, [(ops.shape, F32), ((rows, 2 * tracers), BF16), (sources.shape, F32)],
         [HBM] * 3, 0, 9_000_000, [pltpu.VMEM((rows, tracers), F32), pltpu.SemaphoreType.DMA((3,))],
@@ -299,12 +318,23 @@
     step_in = [HBM] * 2 + [VMEM] * 5
     step_scratch = [pltpu.SMEM(columns.shape, jnp.int32), pltpu.SMEM(live.shape, jnp.int32), window,
                     pltpu.SemaphoreType.DMA((2,))]
+    first_args = (kept(columns), kept(live), ops, own, far, near, sources, last)
+    first_scratch = step_scratch + [pltpu.VMEM((2 * HALO, tracers), F32), pltpu.VMEM((HALO, tracers), F32)]
+    state, far, near = call(
+        first_step_early, [((rows, 2 * tracers), BF16), side, side],
+        step_in + [VMEM], step_flops, 6_000_000, first_scratch,
+    )(*first_args)
+    planes = range(0, tiles, PLANE)
+    early = lax.ppermute(far, "tile", [(i, (i - 1) % tiles) for i in planes])
     state, far, near, token = call(
-        first_step, [((rows, 2 * tracers), BF16), side, side, ((8, tracers), F32)],
-        step_in + [VMEM], step_flops, 6_000_000,
-        step_scratch + [pltpu.VMEM((2 * HALO, tracers), F32), pltpu.VMEM((HALO, tracers), F32)],
-    )(kept(columns), kept(live), ops, own, far, near, sources, last)
-    far, near = swapped(far, near)
+        first_step_late, [((rows, 2 * tracers), BF16), side, side, ((8, tracers), F32)],
+        step_in + [VMEM] * 4, step_flops, 6_000_000, first_scratch, aliases={8: 0},
+    )(*first_args, state, far, near)
+    far = lax.ppermute(
+        far, "tile",
+        [(i, (i + 1 if i % 2 else i - 1) % tiles) for i in range(tiles) if i not in planes],
+    )
+    near = lax.ppermute(near, "tile", [(i, i ^ 1) for i in range(tiles)])
     gather, inverse, rstart = call(
         prepare, [((coarse, rows), BF16), coarse_all, coarse_all],
         [HBM, VMEM, VMEM], 4 * coarse * rows * tracers, 3_000_000,
@@ -312,12 +342,12 @@
     )(kept(cell_map.reshape(-1, BS)), own, token)
     later = lax.ppermute(rstart, "tm", [(i + 1, i) for i in range(1, slices - 1)])
     following = lax.ppermute(rstart, "tm", [(1, 0)])
-    step_scratch = step_scratch + [pltpu.VMEM((rows, 2 * tracers), BF16)]
-    step_args = (kept(columns), kept(live), ops, state, far, near, sources, gather, inverse)
+    step_scratch = step_scratch + [pltpu.VMEM((rows, 2 * tracers), BF16), pltpu.VMEM((HALO, tracers), F32)]
+    step_args = (kept(columns), kept(live), ops, state, far, near, sources, early, gather, inverse)
     step_flops = step_flops + 4 * coarse * rows * tracers
     fine_end, jump, far, near = call(
         second_step_first, [((rows, tracers), F32), coarse_all, coarse_rim, coarse_rim],
-        step_in + [VMEM] * 3, step_flops, 8_000_000, step_scratch,
+        step_in + [VMEM] * 4, step_flops, 8_000_000, step_scratch,
     )(*step_args, following)
 
     def to_slice(block, n, target):
@@ -334,7 +364,7 @@
         if n == 1:
             fine_end, jump = call(
                 second_step_one, [((rows, tracers), F32), coarse_all],
-                step_in + [VMEM] * 3, step_flops, 8_000_000, step_scratch, aliases={9: 0},
+                step_in + [VMEM] * 4, step_flops, 8_000_000, step_scratch, aliases={10: 0},
             )(*step_args, fine_end)
             (coarse2,) = call(
                 split_coarse, [((2 * coarse, reach), BF16)], [HBM, VMEM], 0, 4_000_000,
@@ -343,7 +373,7 @@
         if n == 2:
             fine_end, jump, spread = call(
                 second_step_others, [((rows, tracers), F32), coarse_all, ((rows, coarse), BF16)],
-                step_in + [VMEM] * 3, step_flops, 8_000_000, step_scratch, aliases={9: 0},
+                step_in + [VMEM] * 4, step_flops, 8_000_000, step_scratch, aliases={10: 0},
             )(*step_args, fine_end)
         if n < slices - 1:
             state, far, near, *image = call(

time: 100 us -> 106 us (1.060)
  starting transfers between devices: 41.7 us -> 47.9 us
    ppermute x5 -> x6, starting transfers between devices: 21.3 us -> 27.5 us  [the longest x1 13.9 us: swapped_first(): lax.ppermute(far, 'tile', [(i, (i + 1 if i % 2 else i - 1) % count) for i...]
    ppermute x5 -> x6, waiting for transfers between devices: 5.97 us -> 3.12 us  [the longest x1 2.56 us: swapped_first(): first = lax.ppermute(near, 'tile', [(i, i ^ 1) for i in early])]
    ppermute x21, waiting for transfers between devices: 34.8 us -> 36.7 us  [to_slice(): return lax.ppermute(block, ('tm', 'tile'), route)]
  transfers between devices with their start and end apart: 28 -> 29, of which waited for: 5 -> 5; matrix products, arithmetic and copies ran while one was open for 0% -> 0% of each run, Pallas kernels for 6% -> 6%
where the time goes in v4:
time: 106 us; the launch traced here: 104 us
  starting transfers between devices  47.9 us (45%)
  waiting for transfers between devices  39.8 us (38%)
  Pallas kernels  15.8 us (15%)
    ppermute x21, waiting for transfers between devices, to_slice(): return lax.ppermute(block, ('tm', 'tile'), route)  36.7 us
    ppermute x21, starting transfers between devices, to_slice(): return lax.ppermute(block, ('tm', 'tile'), route)  17.8 us
    ppermute x1, starting transfers between devices, swapped_first(): lax.ppermute(far, 'tile', [(i, (i + 1 if i % 2 else i - 1) % count) for i...  13.9 us
    ppermute x1, starting transfers between devices, on_device(): early = lax.ppermute(far, 'tile', [(i, (i - 1) % tiles) for i in planes])  6.98 us
    pallas_call x6, Pallas kernels, on_device(): call(advance, [coarse_all, coarse_rim, coarse_rim, coarse_all], [VMEM] *...  3.32 us
    ppermute x1, starting transfers between devices, on_device(): near = lax.ppermute(near, 'tile', [(i, i ^ 1) for i in range(tiles)])  2.82 us
    ppermute x1, waiting for transfers between devices, swapped_first(): first = lax.ppermute(near, 'tile', [(i, i ^ 1) for i in early])  2.56 us
    pallas_call x1, Pallas kernels, on_device(): call(second_step_others, [((rows, tracers), F32), coarse_all, ((rows, coa...  2.47 us
  transfers between devices with their start and end apart: 29, of which 5 were waited for; matrix products, arithmetic and copies ran while one was open for 0% of the time, Pallas kernels for 6%

profile of v4, /device:TPU:6, one launch (start us, length us, event | category | flops | bytes accessed | tf_op | source)
XLA Modules:
  0.0 104.0 jit_solution(2473390620089833152)
XLA Ops:
  0.0 1.0 shard_map.74
  1.0 13.9 %collective-permute-start = (f32[256,128]{1,0:T(8,128)S(1)}, f32[256,128]{1,0:T(8,128)S(1)}, u32[]{:S(2)}, u32[]{:S(2)}) collective-permute-start(f32[256,128]{1,0:T(8,128)S(1)} %get-tuple-element.55), channel_id=1, source_target_pairs={{0,63},{1,2},{2,1},{3,4},{4,3},{5,6},{6,5},{7,8},{8,7},{9,10},{10,... | collective-permute-start | bytes 393224 | tf_op jit(solution)/shard_map/ppermute | solution.py:288
  14.9 0.7 collective-permute-start.2
  15.5 1.9 %collective-permute-start.1 = (f32[256,128]{1,0:T(8,128)S(1)}, f32[256,128]{1,0:T(8,128)S(1)}, u32[]{:S(2)}, u32[]{:S(2)}) collective-permute-start(f32[256,128]{1,0:T(8,128)S(1)} %get-tuple-element.56), channel_id=1, source_target_pairs={{0,1},{1,0},{16,17},{17,16},{32,33},{33,32},{48,49},{49,48},{64,65... | collective-permute-start | bytes 393224 | tf_op jit(solution)/shard_map/ppermute | solution.py:287
  17.5 2.3 %shard_map.73 = (f32[12,4,128,128]{3,2,1,0:T(8,128)S(1)}, bf16[1536,256]{1,0:T(8,128)(2,1)S(1)}, f32[1536,128]{1,0:T(8,128)S(1)}) custom-call(f32[12,4,128,128]{3,2,1,0:T(8,128)} %bitcast.9, f32[1536,128]{1,0:T(8,128)} %bitcast.8, f32[1536,128]{1,0:T(8,128)} %sources_ref.1), custom_call_target="tpu_custom_call" | custom-call | bytes 9000000 | tf_op jit(solution)/shard_map/pallas_call | solution.py:313
  19.8 2.6 %collective-permute-done.1.refs_5_ = f32[256,128]{1,0:T(8,128)S(1)} collective-permute-done((f32[256,128]{1,0:T(8,128)S(1)}, f32[256,128]{1,0:T(8,128)S(1)}, u32[]{:S(2)}, u32[]{:S(2)}) %collective-permute-start.1) | collective-permute-done | bytes 131104 | tf_op jit(solution)/shard_map/ppermute | solution.py:287
  22.4 1.8 %shard_map.75 = (bf16[1536,256]{1,0:T(8,128)(2,1)S(1)}, f32[256,128]{1,0:T(8,128)S(1)}, f32[256,128]{1,0:T(8,128)S(1)}) custom-call(s32[4,12]{1,0:T(4,128)} %bitcast.10, s32[1,12]{1,0:T(1,128)} %refs_1_.9, f32[12,4,128,128]{3,2,1,0:T(8,128)S(1)} %get-tuple-element.53.refs_2_, bf16[1536,256]{1,0:T(8,128)(2,1)S(1)} %get-tuple-element.54.refs_3_.own_ref, ...), custom_call_target="tpu_custom_call" | custom-call | flops 603979776 | bytes 6000000 | tf_op jit(solution)/shard_map/pallas_call | solution.py:323
  24.2 0.1 shard_map.76
  24.3 1.5 %shard_map.78 = (bf16[384,1536]{1,0:T(8,128)(2,1)S(1)}, f32[384,128]{1,0:T(8,128)S(1)}, f32[384,128]{1,0:T(8,128)S(1)}) custom-call(s32[12,128]{1,0:T(8,128)} %bitcast.15, bf16[1536,256]{1,0:T(8,128)(2,1)S(1)} %get-tuple-element.54.refs_3_.own_ref, f32[8,128]{1,0:T(8,128)S(1)} %get-tuple-element.61.token_ref), custom_call_target="tpu_custom_call" | custom-call | flops 301989888 | bytes 3000000 | tf_op jit(solution)/shard_map/pallas_call | solution.py:338
  25.8 0.7 collective-permute-start.6
  26.5 1.3 %collective-permute-start.3 = (f32[256,128]{1,0:T(8,128)S(1)}, f32[256,128]{1,0:T(8,128)S(1)}, u32[]{:S(2)}, u32[]{:S(2)}) collective-permute-start(f32[256,128]{1,0:T(8,128)S(1)} %get-tuple-element.63), channel_id=1, source_target_pairs={{1,2},{2,1},{3,4},{4,3},{5,6},{6,5},{7,8},{8,7},{9,10},{10,9},{11,... | collective-permute-start | bytes 393224 | tf_op jit(solution)/shard_map/ppermute | solution.py:333
  27.8 2.8 %collective-permute-start.4 = (f32[256,128]{1,0:T(8,128)S(1)}, f32[256,128]{1,0:T(8,128)S(1)}, u32[]{:S(2)}, u32[]{:S(2)}) collective-permute-start(f32[256,128]{1,0:T(8,128)S(1)} %get-tuple-element.64), channel_id=1, source_target_pairs={{0,1},{1,0},{2,3},{3,2},{4,5},{5,4},{6,7},{7,6},{8,9},{9,8},{10,11... | collective-permute-start | bytes 393224 | tf_op jit(solution)/shard_map/ppermute | solution.py:337
  30.6 7.0 %collective-permute-start.5 = (f32[256,128]{1,0:T(8,128)S(1)}, f32[256,128]{1,0:T(8,128)S(1)}, u32[]{:S(2)}, u32[]{:S(2)}) collective-permute-start(f32[256,128]{1,0:T(8,128)S(1)} %get-tuple-element.59.refs_9_), channel_id=1, source_target_pairs={{0,63},{16,15},{32,31},{48,47},{64,127},{80,79},{96,95},{112,111},... | collective-permute-start | bytes 393224 | tf_op jit(solution)/shard_map/ppermute | solution.py:328
  37.6 1.9 %collective-permute-start.10 = (f32[384,128]{1,0:T(8,128)S(1)}, f32[384,128]{1,0:T(8,128)S(1)}, u32[]{:S(2)}, u32[]{:S(2)}) collective-permute-start(f32[384,128]{1,0:T(8,128)S(1)} %get-tuple-element.67), channel_id=1, source_target_pairs={{128,64},{192,128},{256,192},{320,256},{384,320},{448,384},{129,65... | collective-permute-start | bytes 589832 | tf_op jit(solution)/shard_map/ppermute | solution.py:343
  39.5 0.5 collective-permute-done.5.refs_7_
  40.1 0.7 collective-permute-start.8
  40.8 0.7 collective-permute-start.7
  41.5 0.7 collective-permute-start.9
  42.1 1.4 %shard_map.77.coarse2_ref = bf16[768,768]{1,0:T(8,128)(2,1)S(1)} custom-call(f32[384,768]{1,0:T(8,128)} %coarse_hbm.1, f32[8,128]{1,0:T(8,128)S(1)} %get-tuple-element.61.token_ref), custom_call_target="tpu_custom_call" | custom-call | bytes 4000000 | tf_op jit(solution)/shard_map/pallas_call | solution.py:369
  43.7 0.6 shard_map.81
  44.2 0.7 collective-permute-start.12
  44.9 0.7 collective-permute-start.11
  45.6 0.7 collective-permute-start.13
  46.3 2.5 %shard_map.82 = (f32[1536,128]{1,0:T(8,128)S(1)}, f32[384,128]{1,0:T(8,128)S(1)}, bf16[1536,384]{1,0:T(8,128)(2,1)S(1)}) custom-call(s32[4,12]{1,0:T(4,128)} %bitcast.14, s32[1,12]{1,0:T(1,128)} %refs_1_.9, f32[12,4,128,128]{3,2,1,0:T(8,128)S(1)} %get-tuple-element.53.refs_2_, ...), custom_call_target="tpu_custom_call", output_to_operand_aliasing={{0}: (10, {})} | custom-call | flops 905969664 | bytes 8000000 | tf_op jit(solution)/shard_map/pallas_call | solution.py:374
  48.8 0.6 shard_map.83
  49.3 0.7 collective-permute-start.15
  50.0 0.7 collective-permute-start.14
  50.7 0.7 collective-permute-start.16
  51.4 0.6 shard_map.84
  51.9 0.7 collective-permute-start.18
  52.6 0.7 collective-permute-start.17
  53.3 0.7 collective-permute-start.19
  54.0 0.6 shard_map.85
  54.6 0.7 collective-permute-start.21
  55.2 0.7 collective-permute-start.20
  55.9 0.7 collective-permute-start.22
  56.6 0.6 shard_map.86
  57.2 1.3 %collective-permute-start.24 = (f32[384,128]{1,0:T(8,128)S(1)}, f32[384,128]{1,0:T(8,128)S(1)}, u32[]{:S(2)}, u32[]{:S(2)}) collective-permute-start(f32[384,128]{1,0:T(8,128)S(1)} %get-tuple-element.92), channel_id=1, source_target_pairs={{320,384},{321,385},{322,386},{323,387},{324,388},{325,389},{326,3... | collective-permute-start | bytes 589832 | tf_op jit(solution)/shard_map/ppermute | solution.py:355
  58.5 1.3 %collective-permute-start.23 = (f32[192,128]{1,0:T(8,128)S(1)}, f32[192,128]{1,0:T(8,128)S(1)}, u32[]{:S(2)}, u32[]{:S(2)}) collective-permute-start(f32[192,128]{1,0:T(8,128)S(1)} %get-tuple-element.91), channel_id=1, source_target_pairs={{320,447},{321,386},{322,385},{323,388},{324,387},{325,390},{326,3... | collective-permute-start | bytes 294920 | tf_op jit(solution)/shard_map/ppermute | solution.py:355
  59.8 1.3 %collective-permute-start.25 = (f32[192,128]{1,0:T(8,128)S(1)}, f32[192,128]{1,0:T(8,128)S(1)}, u32[]{:S(2)}, u32[]{:S(2)}) collective-permute-start(f32[192,128]{1,0:T(8,128)S(1)} %get-tuple-element.93), channel_id=1, source_target_pairs={{320,385},{321,384},{322,387},{323,386},{324,389},{325,388},{326,3... | collective-permute-start | bytes 294920 | tf_op jit(solution)/shard_map/ppermute | solution.py:355
  61.1 34.4 %collective-permute-done.23.far_ref = f32[192,128]{1,0:T(8,128)S(1)} collective-permute-done((f32[192,128]{1,0:T(8,128)S(1)}, f32[192,128]{1,0:T(8,128)S(1)}, u32[]{:S(2)}, u32[]{:S(2)}) %collective-permute-start.23) | collective-permute-done | bytes 98336 | tf_op jit(solution)/shard_map/ppermute | solution.py:355
  95.5 0.6 shard_map.87
  96.1 1.3 %collective-permute-start.27 = (f32[384,128]{1,0:T(8,128)S(1)}, f32[384,128]{1,0:T(8,128)S(1)}, u32[]{:S(2)}, u32[]{:S(2)}) collective-permute-start(f32[384,128]{1,0:T(8,128)S(1)} %get-tuple-element.96), channel_id=1, source_target_pairs={{384,448},{385,449},{386,450},{387,451},{388,452},{389,453},{390,4... | collective-permute-start | bytes 589832 | tf_op jit(solution)/shard_map/ppermute | solution.py:355
  97.4 1.3 %collective-permute-start.26 = (f32[192,128]{1,0:T(8,128)S(1)}, f32[192,128]{1,0:T(8,128)S(1)}, u32[]{:S(2)}, u32[]{:S(2)}) collective-permute-start(f32[192,128]{1,0:T(8,128)S(1)} %get-tuple-element.95), channel_id=1, source_target_pairs={{384,511},{385,450},{386,449},{387,452},{388,451},{389,454},{390,4... | collective-permute-start | bytes 294920 | tf_op jit(solution)/shard_map/ppermute | solution.py:355
  98.7 1.3 %collective-permute-start.28 = (f32[192,128]{1,0:T(8,128)S(1)}, f32[192,128]{1,0:T(8,128)S(1)}, u32[]{:S(2)}, u32[]{:S(2)}) collective-permute-start(f32[192,128]{1,0:T(8,128)S(1)} %get-tuple-element.97), channel_id=1, source_target_pairs={{384,449},{385,448},{386,451},{387,450},{388,453},{389,452},{390,4... | collective-permute-start | bytes 294920 | tf_op jit(solution)/shard_map/ppermute | solution.py:355
  100.0 0.9 collective-permute-done.26.far_ref
  100.9 1.3 %collective-permute-done.28.near_ref = f32[192,128]{1,0:T(8,128)S(1)} collective-permute-done((f32[192,128]{1,0:T(8,128)S(1)}, f32[192,128]{1,0:T(8,128)S(1)}, u32[]{:S(2)}, u32[]{:S(2)}) %collective-permute-start.28) | collective-permute-done | bytes 98336 | tf_op jit(solution)/shard_map/ppermute | solution.py:355
  102.2 1.8 %shard_map.88 = f32[1536,128]{1,0:T(8,128)} custom-call(bf16[768,768]{1,0:T(8,128)(2,1)S(1)} %shard_map.77.coarse2_ref, f32[192,128]{1,0:T(8,128)S(1)} %collective-permute-done.26.far_ref, f32[384,128]{1,0:T(8,128)S(1)} %collective-permute-done.27.own_ref, f32[192,128]{1,0:T(8,128)S(1)} %collective-permute-done.28.near_ref, ...), custom_call_target="tpu_custom_call" | custom-call | flops 528482304 | bytes 4000000 | tf_op jit(solution)/shard_map/pallas_call | solution.py:384
  (26 shorter events, 0.1 us)
Async XLA Ops:
  1.0 18.8 %collective-permute-start = (f32[256,128]{1,0:T(8,128)S(1)}, f32[256,128]{1,0:T(8,128)S(1)}, u32[]{:S(2)}, u32[]{:S(2)}) collective-permute-start(f32[256,128]{1,0:T(8,128)S(1)} %get-tuple-element.55), channel_id=1, source_target_pairs={{0,63},{1,2},{2,1},{3,4},{4,3},{5,6},{6,5},{7,8},{8,7},{9,10},{10,... | collective-permute-start | bytes 393224 | tf_op jit(solution)/shard_map/ppermute | solution.py:288
  14.9 5.0 %collective-permute-start.2 = (f32[256,128]{1,0:T(8,128)S(1)}, f32[256,128]{1,0:T(8,128)S(1)}, u32[]{:S(2)}, u32[]{:S(2)}) collective-permute-start(f32[256,128]{1,0:T(8,128)S(1)} %get-tuple-element.56), channel_id=1, source_target_pairs={{2,3},{3,2},{4,5},{5,4},{6,7},{7,6},{8,9},{9,8},{10,11},{11,10},{1... | collective-permute-start | bytes 393224 | tf_op jit(solution)/shard_map/ppermute | solution.py:289
  15.5 6.9 %collective-permute-start.1 = (f32[256,128]{1,0:T(8,128)S(1)}, f32[256,128]{1,0:T(8,128)S(1)}, u32[]{:S(2)}, u32[]{:S(2)}) collective-permute-start(f32[256,128]{1,0:T(8,128)S(1)} %get-tuple-element.56), channel_id=1, source_target_pairs={{0,1},{1,0},{16,17},{17,16},{32,33},{33,32},{48,49},{49,48},{64,65... | collective-permute-start | bytes 393224 | tf_op jit(solution)/shard_map/ppermute | solution.py:287
  25.8 14.3 %collective-permute-start.6 = (f32[384,128]{1,0:T(8,128)S(1)}, f32[384,128]{1,0:T(8,128)S(1)}, u32[]{:S(2)}, u32[]{:S(2)}) collective-permute-start(f32[384,128]{1,0:T(8,128)S(1)} %get-tuple-element.67), channel_id=1, source_target_pairs={{64,0},{65,1},{66,2},{67,3},{68,4},{69,5},{70,6},{71,7},{72,8},{73... | collective-permute-start | bytes 589832 | tf_op jit(solution)/shard_map/ppermute | solution.py:344
  26.5 13.0 %collective-permute-start.3 = (f32[256,128]{1,0:T(8,128)S(1)}, f32[256,128]{1,0:T(8,128)S(1)}, u32[]{:S(2)}, u32[]{:S(2)}) collective-permute-start(f32[256,128]{1,0:T(8,128)S(1)} %get-tuple-element.63), channel_id=1, source_target_pairs={{1,2},{2,1},{3,4},{4,3},{5,6},{6,5},{7,8},{8,7},{9,10},{10,9},{11,... | collective-permute-start | bytes 393224 | tf_op jit(solution)/shard_map/ppermute | solution.py:333
  27.8 11.8 %collective-permute-start.4 = (f32[256,128]{1,0:T(8,128)S(1)}, f32[256,128]{1,0:T(8,128)S(1)}, u32[]{:S(2)}, u32[]{:S(2)}) collective-permute-start(f32[256,128]{1,0:T(8,128)S(1)} %get-tuple-element.64), channel_id=1, source_target_pairs={{0,1},{1,0},{2,3},{3,2},{4,5},{5,4},{6,7},{7,6},{8,9},{9,8},{10,11... | collective-permute-start | bytes 393224 | tf_op jit(solution)/shard_map/ppermute | solution.py:337
  30.6 9.5 %collective-permute-start.5 = (f32[256,128]{1,0:T(8,128)S(1)}, f32[256,128]{1,0:T(8,128)S(1)}, u32[]{:S(2)}, u32[]{:S(2)}) collective-permute-start(f32[256,128]{1,0:T(8,128)S(1)} %get-tuple-element.59.refs_9_), channel_id=1, source_target_pairs={{0,63},{16,15},{32,31},{48,47},{64,127},{80,79},{96,95},{112,111},... | collective-permute-start | bytes 393224 | tf_op jit(solution)/shard_map/ppermute | solution.py:328
  37.6 6.1 %collective-permute-start.10 = (f32[384,128]{1,0:T(8,128)S(1)}, f32[384,128]{1,0:T(8,128)S(1)}, u32[]{:S(2)}, u32[]{:S(2)}) collective-permute-start(f32[384,128]{1,0:T(8,128)S(1)} %get-tuple-element.67), channel_id=1, source_target_pairs={{128,64},{192,128},{256,192},{320,256},{384,320},{448,384},{129,65... | collective-permute-start | bytes 589832 | tf_op jit(solution)/shard_map/ppermute | solution.py:343
  40.1 3.6 %collective-permute-start.8 = (f32[384,128]{1,0:T(8,128)S(1)}, f32[384,128]{1,0:T(8,128)S(1)}, u32[]{:S(2)}, u32[]{:S(2)}) collective-permute-start(f32[384,128]{1,0:T(8,128)S(1)} %get-tuple-element.69), channel_id=1, source_target_pairs={{0,64},{1,65},{2,66},{3,67},{4,68},{5,69},{6,70},{7,71},{8,72},{9,... | collective-permute-start | bytes 589832 | tf_op jit(solution)/shard_map/ppermute | solution.py:355
  40.8 2.9 %collective-permute-start.7 = (f32[192,128]{1,0:T(8,128)S(1)}, f32[192,128]{1,0:T(8,128)S(1)}, u32[]{:S(2)}, u32[]{:S(2)}) collective-permute-start(f32[192,128]{1,0:T(8,128)S(1)} %get-tuple-element.68), channel_id=1, source_target_pairs={{0,127},{1,66},{2,65},{3,68},{4,67},{5,70},{6,69},{7,72},{8,71},{9... | collective-permute-start | bytes 294920 | tf_op jit(solution)/shard_map/ppermute | solution.py:355
  41.5 2.2 %collective-permute-start.9 = (f32[192,128]{1,0:T(8,128)S(1)}, f32[192,128]{1,0:T(8,128)S(1)}, u32[]{:S(2)}, u32[]{:S(2)}) collective-permute-start(f32[192,128]{1,0:T(8,128)S(1)} %get-tuple-element.70), channel_id=1, source_target_pairs={{0,65},{1,64},{2,67},{3,66},{4,69},{5,68},{6,71},{7,70},{8,73},{9,... | collective-permute-start | bytes 294920 | tf_op jit(solution)/shard_map/ppermute | solution.py:355
  44.2 4.5 %collective-permute-start.12 = (f32[384,128]{1,0:T(8,128)S(1)}, f32[384,128]{1,0:T(8,128)S(1)}, u32[]{:S(2)}, u32[]{:S(2)}) collective-permute-start(f32[384,128]{1,0:T(8,128)S(1)} %get-tuple-element.74), channel_id=1, source_target_pairs={{64,128},{65,129},{66,130},{67,131},{68,132},{69,133},{70,134},{71... | collective-permute-start | bytes 589832 | tf_op jit(solution)/shard_map/ppermute | solution.py:355
  44.9 3.8 %collective-permute-start.11 = (f32[192,128]{1,0:T(8,128)S(1)}, f32[192,128]{1,0:T(8,128)S(1)}, u32[]{:S(2)}, u32[]{:S(2)}) collective-permute-start(f32[192,128]{1,0:T(8,128)S(1)} %get-tuple-element.73), channel_id=1, source_target_pairs={{64,191},{65,130},{66,129},{67,132},{68,131},{69,134},{70,133},{71... | collective-permute-start | bytes 294920 | tf_op jit(solution)/shard_map/ppermute | solution.py:355
  45.6 3.2 %collective-permute-start.13 = (f32[192,128]{1,0:T(8,128)S(1)}, f32[192,128]{1,0:T(8,128)S(1)}, u32[]{:S(2)}, u32[]{:S(2)}) collective-permute-start(f32[192,128]{1,0:T(8,128)S(1)} %get-tuple-element.75), channel_id=1, source_target_pairs={{64,129},{65,128},{66,131},{67,130},{68,133},{69,132},{70,135},{71... | collective-permute-start | bytes 294920 | tf_op jit(solution)/shard_map/ppermute | solution.py:355
  49.3 2.1 %collective-permute-start.15 = (f32[384,128]{1,0:T(8,128)S(1)}, f32[384,128]{1,0:T(8,128)S(1)}, u32[]{:S(2)}, u32[]{:S(2)}) collective-permute-start(f32[384,128]{1,0:T(8,128)S(1)} %get-tuple-element.80), channel_id=1, source_target_pairs={{128,192},{129,193},{130,194},{131,195},{132,196},{133,197},{134,1... | collective-permute-start | bytes 589832 | tf_op jit(solution)/shard_map/ppermute | solution.py:355
  50.0 1.4 %collective-permute-start.14 = (f32[192,128]{1,0:T(8,128)S(1)}, f32[192,128]{1,0:T(8,128)S(1)}, u32[]{:S(2)}, u32[]{:S(2)}) collective-permute-start(f32[192,128]{1,0:T(8,128)S(1)} %get-tuple-element.79), channel_id=1, source_target_pairs={{128,255},{129,194},{130,193},{131,196},{132,195},{133,198},{134,1... | collective-permute-start | bytes 294920 | tf_op jit(solution)/shard_map/ppermute | solution.py:355
  50.7 0.7 collective-permute-start.16
  51.9 2.1 %collective-permute-start.18 = (f32[384,128]{1,0:T(8,128)S(1)}, f32[384,128]{1,0:T(8,128)S(1)}, u32[]{:S(2)}, u32[]{:S(2)}) collective-permute-start(f32[384,128]{1,0:T(8,128)S(1)} %get-tuple-element.84), channel_id=1, source_target_pairs={{192,256},{193,257},{194,258},{195,259},{196,260},{197,261},{198,2... | collective-permute-start | bytes 589832 | tf_op jit(solution)/shard_map/ppermute | solution.py:355
  52.6 1.4 %collective-permute-start.17 = (f32[192,128]{1,0:T(8,128)S(1)}, f32[192,128]{1,0:T(8,128)S(1)}, u32[]{:S(2)}, u32[]{:S(2)}) collective-permute-start(f32[192,128]{1,0:T(8,128)S(1)} %get-tuple-element.83), channel_id=1, source_target_pairs={{192,319},{193,258},{194,257},{195,260},{196,259},{197,262},{198,2... | collective-permute-start | bytes 294920 | tf_op jit(solution)/shard_map/ppermute | solution.py:355
  53.3 0.7 collective-permute-start.19
  54.6 2.1 %collective-permute-start.21 = (f32[384,128]{1,0:T(8,128)S(1)}, f32[384,128]{1,0:T(8,128)S(1)}, u32[]{:S(2)}, u32[]{:S(2)}) collective-permute-start(f32[384,128]{1,0:T(8,128)S(1)} %get-tuple-element.88), channel_id=1, source_target_pairs={{256,320},{257,321},{258,322},{259,323},{260,324},{261,325},{262,3... | collective-permute-start | bytes 589832 | tf_op jit(solution)/shard_map/ppermute | solution.py:355
  55.2 1.4 %collective-permute-start.20 = (f32[192,128]{1,0:T(8,128)S(1)}, f32[192,128]{1,0:T(8,128)S(1)}, u32[]{:S(2)}, u32[]{:S(2)}) collective-permute-start(f32[192,128]{1,0:T(8,128)S(1)} %get-tuple-element.87), channel_id=1, source_target_pairs={{256,383},{257,322},{258,321},{259,324},{260,323},{261,326},{262,3... | collective-permute-start | bytes 294920 | tf_op jit(solution)/shard_map/ppermute | solution.py:355
  55.9 0.7 collective-permute-start.22
  57.2 38.3 %collective-permute-start.24 = (f32[384,128]{1,0:T(8,128)S(1)}, f32[384,128]{1,0:T(8,128)S(1)}, u32[]{:S(2)}, u32[]{:S(2)}) collective-permute-start(f32[384,128]{1,0:T(8,128)S(1)} %get-tuple-element.92), channel_id=1, source_target_pairs={{320,384},{321,385},{322,386},{323,387},{324,388},{325,389},{326,3... | collective-permute-start | bytes 589832 | tf_op jit(solution)/shard_map/ppermute | solution.py:355
  58.5 37.0 %collective-permute-start.23 = (f32[192,128]{1,0:T(8,128)S(1)}, f32[192,128]{1,0:T(8,128)S(1)}, u32[]{:S(2)}, u32[]{:S(2)}) collective-permute-start(f32[192,128]{1,0:T(8,128)S(1)} %get-tuple-element.91), channel_id=1, source_target_pairs={{320,447},{321,386},{322,385},{323,388},{324,387},{325,390},{326,3... | collective-permute-start | bytes 294920 | tf_op jit(solution)/shard_map/ppermute | solution.py:355
  59.8 35.7 %collective-permute-start.25 = (f32[192,128]{1,0:T(8,128)S(1)}, f32[192,128]{1,0:T(8,128)S(1)}, u32[]{:S(2)}, u32[]{:S(2)}) collective-permute-start(f32[192,128]{1,0:T(8,128)S(1)} %get-tuple-element.93), channel_id=1, source_target_pairs={{320,385},{321,384},{322,387},{323,386},{324,389},{325,388},{326,3... | collective-permute-start | bytes 294920 | tf_op jit(solution)/shard_map/ppermute | solution.py:355
  96.1 6.1 %collective-permute-start.27 = (f32[384,128]{1,0:T(8,128)S(1)}, f32[384,128]{1,0:T(8,128)S(1)}, u32[]{:S(2)}, u32[]{:S(2)}) collective-permute-start(f32[384,128]{1,0:T(8,128)S(1)} %get-tuple-element.96), channel_id=1, source_target_pairs={{384,448},{385,449},{386,450},{387,451},{388,452},{389,453},{390,4... | collective-permute-start | bytes 589832 | tf_op jit(solution)/shard_map/ppermute | solution.py:355
  97.4 3.5 %collective-permute-start.26 = (f32[192,128]{1,0:T(8,128)S(1)}, f32[192,128]{1,0:T(8,128)S(1)}, u32[]{:S(2)}, u32[]{:S(2)}) collective-permute-start(f32[192,128]{1,0:T(8,128)S(1)} %get-tuple-element.95), channel_id=1, source_target_pairs={{384,511},{385,450},{386,449},{387,452},{388,451},{389,454},{390,4... | collective-permute-start | bytes 294920 | tf_op jit(solution)/shard_map/ppermute | solution.py:355
  98.7 3.5 %collective-permute-start.28 = (f32[192,128]{1,0:T(8,128)S(1)}, f32[192,128]{1,0:T(8,128)S(1)}, u32[]{:S(2)}, u32[]{:S(2)}) collective-permute-start(f32[192,128]{1,0:T(8,128)S(1)} %get-tuple-element.97), channel_id=1, source_target_pairs={{384,449},{385,448},{386,451},{387,450},{388,453},{389,452},{390,4... | collective-permute-start | bytes 294920 | tf_op jit(solution)/shard_map/ppermute | solution.py:355

commit v5 on v3

--- a/solution.py
+++ b/solution.py
@@ -101,12 +101,10 @@
     copy.wait()
     coarse = gather_ref.shape[0]
     cells = lax.broadcasted_iota(jnp.int32, (coarse, BS), 0)
-    children = jnp.zeros((coarse, 1), F32)
     for b in range(map_ref.shape[0]):
         chosen = jnp.where(map_ref[b:b + 1, :] == cells, 1.0, 0.0)
-        children = children + jnp.sum(chosen, axis=1, keepdims=True)
         gather_ref[:, b * BS:(b + 1) * BS] = chosen.astype(BF16)
-    inverse = jnp.broadcast_to(1.0 / children, inverse_ref.shape)
+    inverse = 1.0 / dot(gather_ref[...], jnp.ones((gather_ref.shape[1], inverse_ref.shape[1]), BF16))
     inverse_ref[...] = inverse
     rstart_ref[...] = folded(dot(gather_ref[...], own_ref[...])) * inverse
 
@@ -176,22 +174,23 @@
     token_ref[...] = jnp.zeros_like(token_ref)
 
 
-def restricted_step(refs, gather_ref, inverse_ref, end_ref, jump_ref, cols_ref, live_ref, window, sems, split):
+def restricted_step(refs, gather_ref, inverse_ref, end_ref, jump_ref, cols_ref, live_ref, window, sems, split, whole):
     def emit(b, value):
         end_ref[b * BS:(b + 1) * BS, :] = value
         split[b * BS:(b + 1) * BS, :] = pair(value)
 
-    transport(*refs, cols_ref, live_ref, window, sems, emit)
+    whole[...] = refs[5][...] + refs[7][...]
+    transport(*refs[:5], whole, refs[6], cols_ref, live_ref, window, sems, emit)
     jump_ref[...] = folded(dot(gather_ref[...], split[...])) * inverse_ref[...]
 
 
 def second_step_first(*refs):
-    operands, (gather_ref, inverse_ref, following_ref) = refs[:7], refs[7:10]
-    end_ref, jump_ref, nfar_ref, nnear_ref = refs[10:14]
+    operands, (gather_ref, inverse_ref, following_ref) = refs[:8], refs[8:11]
+    end_ref, jump_ref, nfar_ref, nnear_ref = refs[11:15]
 
     @pl.when(lax.axis_index("tm") == 0)
     def _():
-        restricted_step(operands, gather_ref, inverse_ref, end_ref, jump_ref, *refs[14:])
+        restricted_step(operands, gather_ref, inverse_ref, end_ref, jump_ref, *refs[15:])
         jump_ref[...] = jump_ref[...] - following_ref[...]
         sides(jump_ref, nfar_ref, nnear_ref, nfar_ref.shape[0])
 
@@ -207,12 +206,12 @@
 
 
 def second_step_one(*refs):
-    second_step_rest(lax.axis_index("tm") == 1, refs[7], refs[8], refs[:7], refs[10], refs[11], refs[12:])
+    second_step_rest(lax.axis_index("tm") == 1, refs[8], refs[9], refs[:8], refs[11], refs[12], refs[13:])
 
 
 def second_step_others(*refs):
-    second_step_rest(lax.axis_index("tm") > 1, refs[7], refs[8], refs[:7], refs[10], refs[11], refs[13:])
-    gather_ref, spread_ref = refs[7], refs[12]
+    second_step_rest(lax.axis_index("tm") > 1, refs[8], refs[9], refs[:8], refs[11], refs[12], refs[14:])
+    gather_ref, spread_ref = refs[8], refs[13]
     for b in range(gather_ref.shape[1] // BS):
         spread_ref[b * BS:(b + 1) * BS, :] = gather_ref[:, b * BS:(b + 1) * BS].astype(F32).T.astype(BF16)
 
@@ -257,18 +256,11 @@
 
 def swapped(far, near):
     count = lax.axis_size("tile")
+    early = [i for i in range(count) if i % PLANE < 2]
+    first = lax.ppermute(near, "tile", [(i, i ^ 1) for i in early])
     far = lax.ppermute(far, "tile", [(i, (i + 1 if i % 2 else i - 1) % count) for i in range(count)])
-    near = lax.ppermute(near, "tile", [(i, i ^ 1) for i in range(count)])
-    return far, near
-
-
-def swapped_early(far, near):
-    count = lax.axis_size("tile")
-    last = [i for i in range(count) if i % PLANE >= PLANE - 2]
-    first = lax.ppermute(near, "tile", [(i, i ^ 1) for i in range(count) if i not in last])
-    far = lax.ppermute(far, "tile", [(i, (i + 1 if i % 2 else i - 1) % count) for i in range(count)])
-    second = lax.ppermute(near, "tile", [(i, i ^ 1) for i in last])
-    return far, first, second
+    last = lax.ppermute(near, "tile", [(i, i ^ 1) for i in range(count) if i not in early])
+    return far, first, last
 
 
 def on_device(starts, sources, fine_ops, col_index, live_count, coarse_op, cell_map):
@@ -290,7 +282,7 @@
     coarse_all = ((coarse, tracers), F32)
 
     far, near = call(ends, [side, side], [HBM], 0, 500_000, [pltpu.SemaphoreType.DMA((2,))])(kept(first_state))
-    far, near, last = swapped_early(far, near)
+    far, near, last = swapped(far, near)
     ops, own, sources = call(
         fetch, [(ops.shape, F32), ((rows, 2 * tracers), BF16), (sources.shape, F32)],
         [HBM] * 3, 0, 9_000_000, [pltpu.VMEM((rows, tracers), F32), pltpu.SemaphoreType.DMA((3,))],
@@ -304,7 +296,7 @@
         step_in + [VMEM], step_flops, 6_000_000,
         step_scratch + [pltpu.VMEM((2 * HALO, tracers), F32), pltpu.VMEM((HALO, tracers), F32)],
     )(kept(columns), kept(live), ops, own, far, near, sources, last)
-    far, near = swapped(far, near)
+    far, near, last = swapped(far, near)
     gather, inverse, rstart = call(
         prepare, [((coarse, rows), BF16), coarse_all, coarse_all],
         [HBM, VMEM, VMEM], 4 * coarse * rows * tracers, 3_000_000,
@@ -312,12 +304,12 @@
     )(kept(cell_map.reshape(-1, BS)), own, token)
     later = lax.ppermute(rstart, "tm", [(i + 1, i) for i in range(1, slices - 1)])
     following = lax.ppermute(rstart, "tm", [(1, 0)])
-    step_scratch = step_scratch + [pltpu.VMEM((rows, 2 * tracers), BF16)]
-    step_args = (kept(columns), kept(live), ops, state, far, near, sources, gather, inverse)
+    step_scratch = step_scratch + [pltpu.VMEM((rows, 2 * tracers), BF16), pltpu.VMEM((HALO, tracers), F32)]
+    step_args = (kept(columns), kept(live), ops, state, far, near, sources, last, gather, inverse)
     step_flops = step_flops + 4 * coarse * rows * tracers
     fine_end, jump, far, near = call(
         second_step_first, [((rows, tracers), F32), coarse_all, coarse_rim, coarse_rim],
-        step_in + [VMEM] * 3, step_flops, 8_000_000, step_scratch,
+        step_in + [VMEM] * 4, step_flops, 8_000_000, step_scratch,
     )(*step_args, following)
 
     def to_slice(block, n, target):
@@ -334,7 +326,7 @@
         if n == 1:
             fine_end, jump = call(
                 second_step_one, [((rows, tracers), F32), coarse_all],
-                step_in + [VMEM] * 3, step_flops, 8_000_000, step_scratch, aliases={9: 0},
+                step_in + [VMEM] * 4, step_flops, 8_000_000, step_scratch, aliases={10: 0},
             )(*step_args, fine_end)
             (coarse2,) = call(
                 split_coarse, [((2 * coarse, reach), BF16)], [HBM, VMEM], 0, 4_000_000,
@@ -343,7 +335,7 @@
         if n == 2:
             fine_end, jump, spread = call(
                 second_step_others, [((rows, tracers), F32), coarse_all, ((rows, coarse), BF16)],
-                step_in + [VMEM] * 3, step_flops, 8_000_000, step_scratch, aliases={9: 0},
+                step_in + [VMEM] * 4, step_flops, 8_000_000, step_scratch, aliases={10: 0},
             )(*step_args, fine_end)
         if n < slices - 1:
             state, far, near, *image = call(

time: 100 us -> 100 us (level)
    ppermute x1 -> x2, starting transfers between devices: 2.91 us -> 16.8 us  [swapped(): lax.ppermute(far, 'tile', [(i, (i + 1 if i % 2 else i - 1) % count) for i...]
    ppermute x4, starting transfers between devices: 18.4 us -> 5.18 us  [the longest x2 3.84 us: swapped(): first = lax.ppermute(near, 'tile', [(i, i ^ 1) for i in early])]
    ppermute x1 -> x2, waiting for transfers between devices: 3.41 us -> 2.73 us  [swapped(): lax.ppermute(far, 'tile', [(i, (i + 1 if i % 2 else i - 1) % count) for i...]
  transfers between devices with their start and end apart: 28 -> 29, of which waited for: 5 -> 6; matrix products, arithmetic and copies ran while one was open for 0% -> 0% of each run, Pallas kernels for 6% -> 6%
where the time goes in v5:
time: 100 us; the launch traced here: 98.7 us
  starting transfers between devices  42.3 us (42%)
  waiting for transfers between devices  40.1 us (40%)
  Pallas kernels  15.8 us (16%)
    ppermute x21, waiting for transfers between devices, to_slice(): return lax.ppermute(block, ('tm', 'tile'), route)  34.6 us
    ppermute x21, starting transfers between devices, to_slice(): return lax.ppermute(block, ('tm', 'tile'), route)  17.8 us
    ppermute x2, starting transfers between devices, swapped(): lax.ppermute(far, 'tile', [(i, (i + 1 if i % 2 else i - 1) % count) for i...  16.8 us
    ppermute x2, starting transfers between devices, swapped(): first = lax.ppermute(near, 'tile', [(i, i ^ 1) for i in early])  3.84 us
    pallas_call x6, Pallas kernels, on_device(): call(advance, [coarse_all, coarse_rim, coarse_rim, coarse_all], [VMEM] *...  3.34 us
    ppermute x2, waiting for transfers between devices, swapped(): first = lax.ppermute(near, 'tile', [(i, i ^ 1) for i in early])  2.84 us
    ppermute x2, waiting for transfers between devices, swapped(): lax.ppermute(far, 'tile', [(i, (i + 1 if i % 2 else i - 1) % count) for i...  2.73 us
    pallas_call x1, Pallas kernels, on_device(): call(second_step_others, [((rows, tracers), F32), coarse_all, ((rows, coa...  2.47 us
  transfers between devices with their start and end apart: 29, of which 6 were waited for; matrix products, arithmetic and copies ran while one was open for 0% of the time, Pallas kernels for 6%

profile of v5, /device:TPU:6, one launch (start us, length us, event | category | flops | bytes accessed | tf_op | source)
XLA Modules:
  0.0 98.7 jit_solution(17397947479945502457)
XLA Ops:
  0.0 1.0 shard_map.74
  1.0 13.9 %collective-permute-start = (f32[256,128]{1,0:T(8,128)S(1)}, f32[256,128]{1,0:T(8,128)S(1)}, u32[]{:S(2)}, u32[]{:S(2)}) collective-permute-start(f32[256,128]{1,0:T(8,128)S(1)} %get-tuple-element.52), channel_id=1, source_target_pairs={{0,63},{1,2},{2,1},{3,4},{4,3},{5,6},{6,5},{7,8},{8,7},{9,10},{10,... | collective-permute-start | bytes 393224 | tf_op jit(solution)/shard_map/ppermute | solution.py:261
  14.9 0.7 collective-permute-start.2
  15.5 1.9 %collective-permute-start.1 = (f32[256,128]{1,0:T(8,128)S(1)}, f32[256,128]{1,0:T(8,128)S(1)}, u32[]{:S(2)}, u32[]{:S(2)}) collective-permute-start(f32[256,128]{1,0:T(8,128)S(1)} %get-tuple-element.53), channel_id=1, source_target_pairs={{0,1},{1,0},{16,17},{17,16},{32,33},{33,32},{48,49},{49,48},{64,65... | collective-permute-start | bytes 393224 | tf_op jit(solution)/shard_map/ppermute | solution.py:260
  17.5 2.3 %shard_map.73 = (f32[12,4,128,128]{3,2,1,0:T(8,128)S(1)}, bf16[1536,256]{1,0:T(8,128)(2,1)S(1)}, f32[1536,128]{1,0:T(8,128)S(1)}) custom-call(f32[12,4,128,128]{3,2,1,0:T(8,128)} %bitcast.9, f32[1536,128]{1,0:T(8,128)} %bitcast.8, f32[1536,128]{1,0:T(8,128)} %sources_ref.1), custom_call_target="tpu_custom_call" | custom-call | bytes 9000000 | tf_op jit(solution)/shard_map/pallas_call | solution.py:286
  19.8 2.6 %collective-permute-done.1.near_ref = f32[256,128]{1,0:T(8,128)S(1)} collective-permute-done((f32[256,128]{1,0:T(8,128)S(1)}, f32[256,128]{1,0:T(8,128)S(1)}, u32[]{:S(2)}, u32[]{:S(2)}) %collective-permute-start.1) | collective-permute-done | bytes 131104 | tf_op jit(solution)/shard_map/ppermute | solution.py:260
  22.4 1.8 %shard_map.75 = (bf16[1536,256]{1,0:T(8,128)(2,1)S(1)}, f32[256,128]{1,0:T(8,128)S(1)}, f32[256,128]{1,0:T(8,128)S(1)}, f32[8,128]{1,0:T(8,128)S(1)}) custom-call(s32[4,12]{1,0:T(4,128)} %bitcast.10, s32[1,12]{1,0:T(1,128)} %refs_1_.5, f32[12,4,128,128]{3,2,1,0:T(8,128)S(1)} %get-tuple-element.50.ops_ref.refs_2_, ...), custom_call_target="tpu_custom_call" | custom-call | flops 603979776 | bytes 6000000 | tf_op jit(solution)/shard_map/pallas_call | solution.py:294
  24.2 1.5 %shard_map.77 = (bf16[384,1536]{1,0:T(8,128)(2,1)S(1)}, f32[384,128]{1,0:T(8,128)S(1)}, f32[384,128]{1,0:T(8,128)S(1)}) custom-call(s32[12,128]{1,0:T(8,128)} %bitcast.14, bf16[1536,256]{1,0:T(8,128)(2,1)S(1)} %get-tuple-element.51.own_ref, f32[8,128]{1,0:T(8,128)S(1)} %get-tuple-element.55.token_ref), custom_call_target="tpu_custom_call" | custom-call | flops 301989888 | bytes 3000000 | tf_op jit(solution)/shard_map/pallas_call | solution.py:300
  25.7 0.7 collective-permute-start.6
  26.4 2.9 %collective-permute-start.3 = (f32[256,128]{1,0:T(8,128)S(1)}, f32[256,128]{1,0:T(8,128)S(1)}, u32[]{:S(2)}, u32[]{:S(2)}) collective-permute-start(f32[256,128]{1,0:T(8,128)S(1)} %get-tuple-element.57), channel_id=1, source_target_pairs={{0,63},{1,2},{2,1},{3,4},{4,3},{5,6},{6,5},{7,8},{8,7},{9,10},{10,... | collective-permute-start | bytes 393224 | tf_op jit(solution)/shard_map/ppermute | solution.py:261
  29.3 0.7 collective-permute-start.5
  30.0 1.9 %collective-permute-start.4 = (f32[256,128]{1,0:T(8,128)S(1)}, f32[256,128]{1,0:T(8,128)S(1)}, u32[]{:S(2)}, u32[]{:S(2)}) collective-permute-start(f32[256,128]{1,0:T(8,128)S(1)} %get-tuple-element.58), channel_id=1, source_target_pairs={{0,1},{1,0},{16,17},{17,16},{32,33},{33,32},{48,49},{49,48},{64,65... | collective-permute-start | bytes 393224 | tf_op jit(solution)/shard_map/ppermute | solution.py:260
  31.9 1.9 %collective-permute-start.10 = (f32[384,128]{1,0:T(8,128)S(1)}, f32[384,128]{1,0:T(8,128)S(1)}, u32[]{:S(2)}, u32[]{:S(2)}) collective-permute-start(f32[384,128]{1,0:T(8,128)S(1)} %get-tuple-element.61), channel_id=1, source_target_pairs={{128,64},{192,128},{256,192},{320,256},{384,320},{448,384},{129,65... | collective-permute-start | bytes 589832 | tf_op jit(solution)/shard_map/ppermute | solution.py:305
  33.9 2.7 %collective-permute-done.3.refs_4_ = f32[256,128]{1,0:T(8,128)S(1)} collective-permute-done((f32[256,128]{1,0:T(8,128)S(1)}, f32[256,128]{1,0:T(8,128)S(1)}, u32[]{:S(2)}, u32[]{:S(2)}) %collective-permute-start.3) | collective-permute-done | bytes 131104 | tf_op jit(solution)/shard_map/ppermute | solution.py:261
  36.6 0.3 collective-permute-done.4.refs_5_
  36.9 0.7 collective-permute-start.8
  37.6 0.7 collective-permute-start.7
  38.2 0.7 collective-permute-start.9
  38.9 1.4 %shard_map.76.coarse2_ref = bf16[768,768]{1,0:T(8,128)(2,1)S(1)} custom-call(f32[384,768]{1,0:T(8,128)} %coarse_hbm.1, f32[8,128]{1,0:T(8,128)S(1)} %get-tuple-element.55.token_ref), custom_call_target="tpu_custom_call" | custom-call | bytes 4000000 | tf_op jit(solution)/shard_map/pallas_call | solution.py:331
  40.5 0.6 shard_map.80
  41.0 0.7 collective-permute-start.12
  41.7 0.7 collective-permute-start.11
  42.4 0.7 collective-permute-start.13
  43.1 2.5 %shard_map.81 = (f32[1536,128]{1,0:T(8,128)S(1)}, f32[384,128]{1,0:T(8,128)S(1)}, bf16[1536,384]{1,0:T(8,128)(2,1)S(1)}) custom-call(s32[4,12]{1,0:T(4,128)} %bitcast.13, s32[1,12]{1,0:T(1,128)} %refs_1_.5, f32[12,4,128,128]{3,2,1,0:T(8,128)S(1)} %get-tuple-element.50.ops_ref.refs_2_, ...), custom_call_target="tpu_custom_call", output_to_operand_aliasing={{0}: (10, {})} | custom-call | flops 905969664 | bytes 8000000 | tf_op jit(solution)/shard_map/pallas_call | solution.py:336
  45.6 0.6 shard_map.82
  46.1 0.7 collective-permute-start.15
  46.8 0.7 collective-permute-start.14
  47.5 0.7 collective-permute-start.16
  48.2 0.6 shard_map.83
  48.7 0.7 collective-permute-start.18
  49.4 0.7 collective-permute-start.17
  50.1 0.7 collective-permute-start.19
  50.8 0.6 shard_map.84
  51.4 0.7 collective-permute-start.21
  52.0 0.7 collective-permute-start.20
  52.7 0.7 collective-permute-start.22
  53.4 0.6 shard_map.85
  54.0 1.3 %collective-permute-start.24 = (f32[384,128]{1,0:T(8,128)S(1)}, f32[384,128]{1,0:T(8,128)S(1)}, u32[]{:S(2)}, u32[]{:S(2)}) collective-permute-start(f32[384,128]{1,0:T(8,128)S(1)} %get-tuple-element.86), channel_id=1, source_target_pairs={{320,384},{321,385},{322,386},{323,387},{324,388},{325,389},{326,3... | collective-permute-start | bytes 589832 | tf_op jit(solution)/shard_map/ppermute | solution.py:317
  55.3 1.3 %collective-permute-start.23 = (f32[192,128]{1,0:T(8,128)S(1)}, f32[192,128]{1,0:T(8,128)S(1)}, u32[]{:S(2)}, u32[]{:S(2)}) collective-permute-start(f32[192,128]{1,0:T(8,128)S(1)} %get-tuple-element.85), channel_id=1, source_target_pairs={{320,447},{321,386},{322,385},{323,388},{324,387},{325,390},{326,3... | collective-permute-start | bytes 294920 | tf_op jit(solution)/shard_map/ppermute | solution.py:317
  56.6 1.3 %collective-permute-start.25 = (f32[192,128]{1,0:T(8,128)S(1)}, f32[192,128]{1,0:T(8,128)S(1)}, u32[]{:S(2)}, u32[]{:S(2)}) collective-permute-start(f32[192,128]{1,0:T(8,128)S(1)} %get-tuple-element.87), channel_id=1, source_target_pairs={{320,385},{321,384},{322,387},{323,386},{324,389},{325,388},{326,3... | collective-permute-start | bytes 294920 | tf_op jit(solution)/shard_map/ppermute | solution.py:317
  57.9 32.3 %collective-permute-done.23.far_ref = f32[192,128]{1,0:T(8,128)S(1)} collective-permute-done((f32[192,128]{1,0:T(8,128)S(1)}, f32[192,128]{1,0:T(8,128)S(1)}, u32[]{:S(2)}, u32[]{:S(2)}) %collective-permute-start.23) | collective-permute-done | bytes 98336 | tf_op jit(solution)/shard_map/ppermute | solution.py:317
  90.2 0.6 shard_map.86
  90.8 1.3 %collective-permute-start.27 = (f32[384,128]{1,0:T(8,128)S(1)}, f32[384,128]{1,0:T(8,128)S(1)}, u32[]{:S(2)}, u32[]{:S(2)}) collective-permute-start(f32[384,128]{1,0:T(8,128)S(1)} %get-tuple-element.90), channel_id=1, source_target_pairs={{384,448},{385,449},{386,450},{387,451},{388,452},{389,453},{390,4... | collective-permute-start | bytes 589832 | tf_op jit(solution)/shard_map/ppermute | solution.py:317
  92.1 1.3 %collective-permute-start.26 = (f32[192,128]{1,0:T(8,128)S(1)}, f32[192,128]{1,0:T(8,128)S(1)}, u32[]{:S(2)}, u32[]{:S(2)}) collective-permute-start(f32[192,128]{1,0:T(8,128)S(1)} %get-tuple-element.89), channel_id=1, source_target_pairs={{384,511},{385,450},{386,449},{387,452},{388,451},{389,454},{390,4... | collective-permute-start | bytes 294920 | tf_op jit(solution)/shard_map/ppermute | solution.py:317
  93.4 1.3 %collective-permute-start.28 = (f32[192,128]{1,0:T(8,128)S(1)}, f32[192,128]{1,0:T(8,128)S(1)}, u32[]{:S(2)}, u32[]{:S(2)}) collective-permute-start(f32[192,128]{1,0:T(8,128)S(1)} %get-tuple-element.91), channel_id=1, source_target_pairs={{384,449},{385,448},{386,451},{387,450},{388,453},{389,452},{390,4... | collective-permute-start | bytes 294920 | tf_op jit(solution)/shard_map/ppermute | solution.py:317
  94.7 0.9 collective-permute-done.26.far_ref
  95.6 1.3 %collective-permute-done.28.near_ref = f32[192,128]{1,0:T(8,128)S(1)} collective-permute-done((f32[192,128]{1,0:T(8,128)S(1)}, f32[192,128]{1,0:T(8,128)S(1)}, u32[]{:S(2)}, u32[]{:S(2)}) %collective-permute-start.28) | collective-permute-done | bytes 98336 | tf_op jit(solution)/shard_map/ppermute | solution.py:317
  96.9 1.8 %shard_map.87 = f32[1536,128]{1,0:T(8,128)} custom-call(bf16[768,768]{1,0:T(8,128)(2,1)S(1)} %shard_map.76.coarse2_ref, f32[192,128]{1,0:T(8,128)S(1)} %collective-permute-done.26.far_ref, f32[384,128]{1,0:T(8,128)S(1)} %collective-permute-done.27.own_ref, f32[192,128]{1,0:T(8,128)S(1)} %collective-permute-done.28.near_ref, ...), custom_call_target="tpu_custom_call" | custom-call | flops 528482304 | bytes 4000000 | tf_op jit(solution)/shard_map/pallas_call | solution.py:346
  (25 shorter events, 0.1 us)
Async XLA Ops:
  1.0 18.8 %collective-permute-start = (f32[256,128]{1,0:T(8,128)S(1)}, f32[256,128]{1,0:T(8,128)S(1)}, u32[]{:S(2)}, u32[]{:S(2)}) collective-permute-start(f32[256,128]{1,0:T(8,128)S(1)} %get-tuple-element.52), channel_id=1, source_target_pairs={{0,63},{1,2},{2,1},{3,4},{4,3},{5,6},{6,5},{7,8},{8,7},{9,10},{10,... | collective-permute-start | bytes 393224 | tf_op jit(solution)/shard_map/ppermute | solution.py:261
  14.9 5.0 %collective-permute-start.2 = (f32[256,128]{1,0:T(8,128)S(1)}, f32[256,128]{1,0:T(8,128)S(1)}, u32[]{:S(2)}, u32[]{:S(2)}) collective-permute-start(f32[256,128]{1,0:T(8,128)S(1)} %get-tuple-element.53), channel_id=1, source_target_pairs={{2,3},{3,2},{4,5},{5,4},{6,7},{7,6},{8,9},{9,8},{10,11},{11,10},{1... | collective-permute-start | bytes 393224 | tf_op jit(solution)/shard_map/ppermute | solution.py:262
  15.5 6.9 %collective-permute-start.1 = (f32[256,128]{1,0:T(8,128)S(1)}, f32[256,128]{1,0:T(8,128)S(1)}, u32[]{:S(2)}, u32[]{:S(2)}) collective-permute-start(f32[256,128]{1,0:T(8,128)S(1)} %get-tuple-element.53), channel_id=1, source_target_pairs={{0,1},{1,0},{16,17},{17,16},{32,33},{33,32},{48,49},{49,48},{64,65... | collective-permute-start | bytes 393224 | tf_op jit(solution)/shard_map/ppermute | solution.py:260
  25.7 11.1 %collective-permute-start.6 = (f32[384,128]{1,0:T(8,128)S(1)}, f32[384,128]{1,0:T(8,128)S(1)}, u32[]{:S(2)}, u32[]{:S(2)}) collective-permute-start(f32[384,128]{1,0:T(8,128)S(1)} %get-tuple-element.61), channel_id=1, source_target_pairs={{64,0},{65,1},{66,2},{67,3},{68,4},{69,5},{70,6},{71,7},{72,8},{73... | collective-permute-start | bytes 589832 | tf_op jit(solution)/shard_map/ppermute | solution.py:306
  26.4 10.2 %collective-permute-start.3 = (f32[256,128]{1,0:T(8,128)S(1)}, f32[256,128]{1,0:T(8,128)S(1)}, u32[]{:S(2)}, u32[]{:S(2)}) collective-permute-start(f32[256,128]{1,0:T(8,128)S(1)} %get-tuple-element.57), channel_id=1, source_target_pairs={{0,63},{1,2},{2,1},{3,4},{4,3},{5,6},{6,5},{7,8},{8,7},{9,10},{10,... | collective-permute-start | bytes 393224 | tf_op jit(solution)/shard_map/ppermute | solution.py:261
  29.3 7.3 %collective-permute-start.5 = (f32[256,128]{1,0:T(8,128)S(1)}, f32[256,128]{1,0:T(8,128)S(1)}, u32[]{:S(2)}, u32[]{:S(2)}) collective-permute-start(f32[256,128]{1,0:T(8,128)S(1)} %get-tuple-element.58), channel_id=1, source_target_pairs={{2,3},{3,2},{4,5},{5,4},{6,7},{7,6},{8,9},{9,8},{10,11},{11,10},{1... | collective-permute-start | bytes 393224 | tf_op jit(solution)/shard_map/ppermute | solution.py:262
  30.0 6.9 %collective-permute-start.4 = (f32[256,128]{1,0:T(8,128)S(1)}, f32[256,128]{1,0:T(8,128)S(1)}, u32[]{:S(2)}, u32[]{:S(2)}) collective-permute-start(f32[256,128]{1,0:T(8,128)S(1)} %get-tuple-element.58), channel_id=1, source_target_pairs={{0,1},{1,0},{16,17},{17,16},{32,33},{33,32},{48,49},{49,48},{64,65... | collective-permute-start | bytes 393224 | tf_op jit(solution)/shard_map/ppermute | solution.py:260
  31.9 8.5 %collective-permute-start.10 = (f32[384,128]{1,0:T(8,128)S(1)}, f32[384,128]{1,0:T(8,128)S(1)}, u32[]{:S(2)}, u32[]{:S(2)}) collective-permute-start(f32[384,128]{1,0:T(8,128)S(1)} %get-tuple-element.61), channel_id=1, source_target_pairs={{128,64},{192,128},{256,192},{320,256},{384,320},{448,384},{129,65... | collective-permute-start | bytes 589832 | tf_op jit(solution)/shard_map/ppermute | solution.py:305
  36.9 3.6 %collective-permute-start.8 = (f32[384,128]{1,0:T(8,128)S(1)}, f32[384,128]{1,0:T(8,128)S(1)}, u32[]{:S(2)}, u32[]{:S(2)}) collective-permute-start(f32[384,128]{1,0:T(8,128)S(1)} %get-tuple-element.63), channel_id=1, source_target_pairs={{0,64},{1,65},{2,66},{3,67},{4,68},{5,69},{6,70},{7,71},{8,72},{9,... | collective-permute-start | bytes 589832 | tf_op jit(solution)/shard_map/ppermute | solution.py:317
  37.6 2.9 %collective-permute-start.7 = (f32[192,128]{1,0:T(8,128)S(1)}, f32[192,128]{1,0:T(8,128)S(1)}, u32[]{:S(2)}, u32[]{:S(2)}) collective-permute-start(f32[192,128]{1,0:T(8,128)S(1)} %get-tuple-element.62), channel_id=1, source_target_pairs={{0,127},{1,66},{2,65},{3,68},{4,67},{5,70},{6,69},{7,72},{8,71},{9... | collective-permute-start | bytes 294920 | tf_op jit(solution)/shard_map/ppermute | solution.py:317
  38.2 2.2 %collective-permute-start.9 = (f32[192,128]{1,0:T(8,128)S(1)}, f32[192,128]{1,0:T(8,128)S(1)}, u32[]{:S(2)}, u32[]{:S(2)}) collective-permute-start(f32[192,128]{1,0:T(8,128)S(1)} %get-tuple-element.64), channel_id=1, source_target_pairs={{0,65},{1,64},{2,67},{3,66},{4,69},{5,68},{6,71},{7,70},{8,73},{9,... | collective-permute-start | bytes 294920 | tf_op jit(solution)/shard_map/ppermute | solution.py:317
  41.0 4.5 %collective-permute-start.12 = (f32[384,128]{1,0:T(8,128)S(1)}, f32[384,128]{1,0:T(8,128)S(1)}, u32[]{:S(2)}, u32[]{:S(2)}) collective-permute-start(f32[384,128]{1,0:T(8,128)S(1)} %get-tuple-element.68), channel_id=1, source_target_pairs={{64,128},{65,129},{66,130},{67,131},{68,132},{69,133},{70,134},{71... | collective-permute-start | bytes 589832 | tf_op jit(solution)/shard_map/ppermute | solution.py:317
  41.7 3.8 %collective-permute-start.11 = (f32[192,128]{1,0:T(8,128)S(1)}, f32[192,128]{1,0:T(8,128)S(1)}, u32[]{:S(2)}, u32[]{:S(2)}) collective-permute-start(f32[192,128]{1,0:T(8,128)S(1)} %get-tuple-element.67), channel_id=1, source_target_pairs={{64,191},{65,130},{66,129},{67,132},{68,131},{69,134},{70,133},{71... | collective-permute-start | bytes 294920 | tf_op jit(solution)/shard_map/ppermute | solution.py:317
  42.4 3.2 %collective-permute-start.13 = (f32[192,128]{1,0:T(8,128)S(1)}, f32[192,128]{1,0:T(8,128)S(1)}, u32[]{:S(2)}, u32[]{:S(2)}) collective-permute-start(f32[192,128]{1,0:T(8,128)S(1)} %get-tuple-element.69), channel_id=1, source_target_pairs={{64,129},{65,128},{66,131},{67,130},{68,133},{69,132},{70,135},{71... | collective-permute-start | bytes 294920 | tf_op jit(solution)/shard_map/ppermute | solution.py:317
  46.1 2.1 %collective-permute-start.15 = (f32[384,128]{1,0:T(8,128)S(1)}, f32[384,128]{1,0:T(8,128)S(1)}, u32[]{:S(2)}, u32[]{:S(2)}) collective-permute-start(f32[384,128]{1,0:T(8,128)S(1)} %get-tuple-element.74), channel_id=1, source_target_pairs={{128,192},{129,193},{130,194},{131,195},{132,196},{133,197},{134,1... | collective-permute-start | bytes 589832 | tf_op jit(solution)/shard_map/ppermute | solution.py:317
  46.8 1.4 %collective-permute-start.14 = (f32[192,128]{1,0:T(8,128)S(1)}, f32[192,128]{1,0:T(8,128)S(1)}, u32[]{:S(2)}, u32[]{:S(2)}) collective-permute-start(f32[192,128]{1,0:T(8,128)S(1)} %get-tuple-element.73), channel_id=1, source_target_pairs={{128,255},{129,194},{130,193},{131,196},{132,195},{133,198},{134,1... | collective-permute-start | bytes 294920 | tf_op jit(solution)/shard_map/ppermute | solution.py:317
  47.5 0.7 collective-permute-start.16
  48.7 2.1 %collective-permute-start.18 = (f32[384,128]{1,0:T(8,128)S(1)}, f32[384,128]{1,0:T(8,128)S(1)}, u32[]{:S(2)}, u32[]{:S(2)}) collective-permute-start(f32[384,128]{1,0:T(8,128)S(1)} %get-tuple-element.78), channel_id=1, source_target_pairs={{192,256},{193,257},{194,258},{195,259},{196,260},{197,261},{198,2... | collective-permute-start | bytes 589832 | tf_op jit(solution)/shard_map/ppermute | solution.py:317
  49.4 1.4 %collective-permute-start.17 = (f32[192,128]{1,0:T(8,128)S(1)}, f32[192,128]{1,0:T(8,128)S(1)}, u32[]{:S(2)}, u32[]{:S(2)}) collective-permute-start(f32[192,128]{1,0:T(8,128)S(1)} %get-tuple-element.77), channel_id=1, source_target_pairs={{192,319},{193,258},{194,257},{195,260},{196,259},{197,262},{198,2... | collective-permute-start | bytes 294920 | tf_op jit(solution)/shard_map/ppermute | solution.py:317
  50.1 0.7 collective-permute-start.19
  51.4 2.1 %collective-permute-start.21 = (f32[384,128]{1,0:T(8,128)S(1)}, f32[384,128]{1,0:T(8,128)S(1)}, u32[]{:S(2)}, u32[]{:S(2)}) collective-permute-start(f32[384,128]{1,0:T(8,128)S(1)} %get-tuple-element.82), channel_id=1, source_target_pairs={{256,320},{257,321},{258,322},{259,323},{260,324},{261,325},{262,3... | collective-permute-start | bytes 589832 | tf_op jit(solution)/shard_map/ppermute | solution.py:317
  52.0 1.4 %collective-permute-start.20 = (f32[192,128]{1,0:T(8,128)S(1)}, f32[192,128]{1,0:T(8,128)S(1)}, u32[]{:S(2)}, u32[]{:S(2)}) collective-permute-start(f32[192,128]{1,0:T(8,128)S(1)} %get-tuple-element.81), channel_id=1, source_target_pairs={{256,383},{257,322},{258,321},{259,324},{260,323},{261,326},{262,3... | collective-permute-start | bytes 294920 | tf_op jit(solution)/shard_map/ppermute | solution.py:317
  52.7 0.7 collective-permute-start.22
  54.0 36.2 %collective-permute-start.24 = (f32[384,128]{1,0:T(8,128)S(1)}, f32[384,128]{1,0:T(8,128)S(1)}, u32[]{:S(2)}, u32[]{:S(2)}) collective-permute-start(f32[384,128]{1,0:T(8,128)S(1)} %get-tuple-element.86), channel_id=1, source_target_pairs={{320,384},{321,385},{322,386},{323,387},{324,388},{325,389},{326,3... | collective-permute-start | bytes 589832 | tf_op jit(solution)/shard_map/ppermute | solution.py:317
  55.3 34.9 %collective-permute-start.23 = (f32[192,128]{1,0:T(8,128)S(1)}, f32[192,128]{1,0:T(8,128)S(1)}, u32[]{:S(2)}, u32[]{:S(2)}) collective-permute-start(f32[192,128]{1,0:T(8,128)S(1)} %get-tuple-element.85), channel_id=1, source_target_pairs={{320,447},{321,386},{322,385},{323,388},{324,387},{325,390},{326,3... | collective-permute-start | bytes 294920 | tf_op jit(solution)/shard_map/ppermute | solution.py:317
  56.6 33.6 %collective-permute-start.25 = (f32[192,128]{1,0:T(8,128)S(1)}, f32[192,128]{1,0:T(8,128)S(1)}, u32[]{:S(2)}, u32[]{:S(2)}) collective-permute-start(f32[192,128]{1,0:T(8,128)S(1)} %get-tuple-element.87), channel_id=1, source_target_pairs={{320,385},{321,384},{322,387},{323,386},{324,389},{325,388},{326,3... | collective-permute-start | bytes 294920 | tf_op jit(solution)/shard_map/ppermute | solution.py:317
  90.8 6.1 %collective-permute-start.27 = (f32[384,128]{1,0:T(8,128)S(1)}, f32[384,128]{1,0:T(8,128)S(1)}, u32[]{:S(2)}, u32[]{:S(2)}) collective-permute-start(f32[384,128]{1,0:T(8,128)S(1)} %get-tuple-element.90), channel_id=1, source_target_pairs={{384,448},{385,449},{386,450},{387,451},{388,452},{389,453},{390,4... | collective-permute-start | bytes 589832 | tf_op jit(solution)/shard_map/ppermute | solution.py:317
  92.1 3.5 %collective-permute-start.26 = (f32[192,128]{1,0:T(8,128)S(1)}, f32[192,128]{1,0:T(8,128)S(1)}, u32[]{:S(2)}, u32[]{:S(2)}) collective-permute-start(f32[192,128]{1,0:T(8,128)S(1)} %get-tuple-element.89), channel_id=1, source_target_pairs={{384,511},{385,450},{386,449},{387,452},{388,451},{389,454},{390,4... | collective-permute-start | bytes 294920 | tf_op jit(solution)/shard_map/ppermute | solution.py:317
  93.4 3.5 %collective-permute-start.28 = (f32[192,128]{1,0:T(8,128)S(1)}, f32[192,128]{1,0:T(8,128)S(1)}, u32[]{:S(2)}, u32[]{:S(2)}) collective-permute-start(f32[192,128]{1,0:T(8,128)S(1)} %get-tuple-element.91), channel_id=1, source_target_pairs={{384,449},{385,448},{386,451},{387,450},{388,453},{389,452},{390,4... | collective-permute-start | bytes 294920 | tf_op jit(solution)/shard_map/ppermute | solution.py:317
